TPU v7x, 32 devices: a whole 2x2x4 slice. The times are simulated.
32 devices in a mesh: grp: 4 (over y, x), tp: 8 (over z, core).
Axes of the slice: x: 2, y: 2, z: 4, core: 2. Of those that a mesh axis runs over, the one named last changes fastest.
Arguments:
- layer_input: bfloat16 [8192, 2048], P('grp'), may hold values from -6 to 6
- out_cotangent: bfloat16 [8192, 2048], P('grp'), may hold values from -6 to 6
- seq_group: int32 [6], replicated, may hold values from 0 to 3, as said below
- seq_len: int32 [6], replicated, may hold values from 512 to 2048, as said below
- w_qkv: float32 [2048, 6144], P('grp', 'tp'), may hold values from -0.1875 to 0.1875
- b_qv: float32 [4096], replicated, may hold values from -3 to 3
- w_out: float32 [2048, 2048], P('grp', 'tp'), may hold values from -0.75 to 0.75
- b_out: float32 [2048], replicated, may hold values from -2 to 2
- w_up: float32 [2048, 8192], P('grp', 'tp'), may hold values from -0.125 to 0.125
- b_up: float32 [8192], replicated, may hold values from -3 to 3
- w_down: float32 [2048, 8192], P('grp', 'tp'), may hold values from -0.0625 to 0.0625
- b_down: float32 [2048], replicated, may hold values from -2 to 2
- first_norm_gain: float32 [2048], replicated, may hold values from 0.1 to 1.9
- first_norm_bias: float32 [2048], replicated, may hold values from -2 to 2
- second_norm_gain: float32 [2048], replicated, may hold values from 0.1 to 1.9
- second_norm_bias: float32 [2048], replicated, may hold values from -2 to 2
Outputs:
- layer_output: bfloat16 [8192, 2048], P(('grp', 'tp'))
- grad_x: float32 [8192, 2048], P(('grp', 'tp'))
- grad_w_qkv: float32 [2048, 6144], P('grp', 'tp')
- grad_b_qv: float32 [4096], replicated
- grad_w_out: float32 [2048, 2048], P('grp', 'tp')
- grad_b_out: float32 [2048], replicated
- grad_w_up: float32 [2048, 8192], P('grp', 'tp')
- grad_b_up: float32 [8192], replicated
- grad_w_down: float32 [2048, 8192], P('grp', 'tp')
- grad_b_down: float32 [2048], replicated
- grad_ln1_gain: float32 [2048], replicated
- grad_ln1_bias: float32 [2048], replicated
- grad_ln2_gain: float32 [2048], replicated
- grad_ln2_bias: float32 [2048], replicated
Inputs may be any that keep to these rules, and one draw needn't show every extreme that they name: `seq_group`: each group's sequences total at most 2048 tokens, and in every draw some group holds exactly 2048; every group holds at least one sequence. `seq_len`: each sequence has 2048 or 512 tokens.
All inputs are finite; a program needn't handle non-finite values.
Results may differ from a plain program's by a relative error of at most 0.023.
Values may be sent and summed in bfloat16 or wider, within the bound.
A program may use at most 320 MiB of HBM per device.

v0:
```python
import jax
import jax.numpy as jnp
from jax import lax
from jax.sharding import PartitionSpec as P

HD = 128


def layer_normalize(rows, gain, bias):
    mean_row = jnp.mean(rows, -1, keepdims=True)
    centred = rows - mean_row
    inverse = lax.rsqrt(jnp.mean(centred * centred, -1, keepdims=True) + 1e-05)
    normed = centred * inverse
    return (normed * gain + bias, normed, inverse)


def norm_backward_pass(grad_norm, normed, inverse, gain):
    scaled = grad_norm * gain
    inner = jnp.mean(scaled, -1, keepdims=True) + normed * jnp.mean(
        scaled * normed, -1, keepdims=True
    )
    return inverse * (scaled - inner)


def contract(left, right, left_dim, right_dim):
    return lax.dot_general(
        left, right, (((left_dim,), (right_dim,)), ((), ())), preferred_element_type=jnp.float32
    )


def activate(values_in):
    return jax.nn.gelu(values_in, approximate=True)


def on_device(
    layer_input,
    out_cotangent,
    seq_group,
    seq_len,
    w_qkv,
    b_qv,
    w_out,
    b_out,
    w_up,
    b_up,
    w_down,
    b_down,
    first_norm_gain,
    first_norm_bias,
    second_norm_gain,
    second_norm_bias,
):
    w_attn, w_proj, w_expand, w_reduce = (
        lax.all_gather(w_qkv.astype(jnp.bfloat16), "grp", axis=0, tiled=True),
        lax.all_gather(w_out.astype(jnp.bfloat16), "grp", axis=0, tiled=True),
        lax.all_gather(w_up.astype(jnp.bfloat16), "grp", axis=0, tiled=True),
        lax.all_gather(w_down.astype(jnp.bfloat16), "grp", axis=0, tiled=True),
    )
    tp_rank = lax.axis_index("tp")
    tp_count = lax.axis_size("tp")
    group_rank = lax.axis_index("grp")
    length = layer_input.shape[0]
    shared_row_block = length // tp_count
    local_row_start = tp_rank * shared_row_block
    heads_here = w_proj.shape[1] // HD
    hidden_here = w_expand.shape[1]
    seq_count = seq_group.shape[0]
    in_group = seq_group == group_rank
    lengths = jnp.where(in_group, seq_len, 0)
    seq_order = jnp.arange(seq_count, dtype=jnp.int32)
    earlier = seq_order[:, None] > seq_order[None, :]
    offsets = jnp.sum(jnp.where(earlier, lengths[None, :], 0), 1)
    places = jnp.arange(length, dtype=jnp.int32)
    inside = (
        in_group[None, :]
        & (places[:, None] >= offsets[None, :])
        & (places[:, None] < (offsets + lengths)[None, :])
    )
    segment = jnp.sum(jnp.where(inside, seq_order[None, :] + 1, 0), 1) - 1
    live_rows = (segment >= 0).astype(jnp.float32)[:, None]
    input_row_block = layer_input.astype(jnp.float32)
    first_normalized, first_standardized, first_inverse_deviation = layer_normalize(
        input_row_block, first_norm_gain, first_norm_bias
    )
    normed_oneb = first_normalized.astype(jnp.bfloat16)
    head_bias = lax.dynamic_slice_in_dim(
        b_qv.reshape(-1, 2, HD), tp_rank * heads_here, heads_here, 0
    )
    bias_three = jnp.stack(
        [head_bias[:, 0], jnp.zeros_like(head_bias[:, 0]), head_bias[:, 1]], 1
    ).reshape(-1)
    projected = (
        jnp.dot(normed_oneb, w_attn, preferred_element_type=jnp.float32) + bias_three
    ).astype(jnp.bfloat16)
    projected = projected.reshape(length, heads_here, 3, HD)
    query = projected[:, :, 0]
    keys = projected[:, :, 1]
    values = projected[:, :, 2]
    block_rows = min(512, length)
    blocks = length // block_rows
    score_scale = HD ** (-0.5)
    columns = jnp.arange(length, dtype=jnp.int32)

    def scores_for(block_index):
        first_row = block_index * block_rows
        query_block = lax.dynamic_slice_in_dim(query, first_row, block_rows, 0)
        dotted = (
            jnp.einsum("qhe,khe->hqk", query_block, keys, preferred_element_type=jnp.float32)
            * score_scale
        )
        segment_block = lax.dynamic_slice_in_dim(segment, first_row, block_rows, 0)
        row_places = first_row + jnp.arange(block_rows, dtype=jnp.int32)
        allowed = (segment_block[:, None] == segment[None, :]) & (
            columns[None, :] <= row_places[:, None]
        )
        return (jnp.where(allowed[None], dotted, -1e30), query_block)

    def attend(block_index):
        masked, unused = scores_for(block_index)
        highest_score = jnp.max(masked, -1, keepdims=True)
        powers = jnp.exp(masked - highest_score)
        summed = jnp.sum(powers, -1, keepdims=True)
        chances = (powers / summed).astype(jnp.bfloat16)
        context = jnp.einsum(
            "hqk,khe->qhe", chances, values, preferred_element_type=jnp.float32
        ).astype(jnp.bfloat16)
        return (context, highest_score[..., 0] + jnp.log(summed[..., 0]))

    contexts, log_totals = lax.map(attend, jnp.arange(blocks))
    context_all = contexts.reshape(length, heads_here * HD)
    attn_total = lax.psum(contract(context_all, w_proj, 1, 1).astype(jnp.bfloat16), "tp").astype(
        jnp.float32
    )
    hidden_input = input_row_block + attn_total + b_out
    second_normalized, second_standardized, second_inverse_deviation = layer_normalize(
        hidden_input, second_norm_gain, second_norm_bias
    )
    normed_twob = second_normalized.astype(jnp.bfloat16)
    up_bias = lax.dynamic_slice_in_dim(b_up, tp_rank * hidden_here, hidden_here, 0)
    before = jnp.dot(normed_twob, w_expand, preferred_element_type=jnp.float32) + up_bias
    active = activate(before).astype(jnp.bfloat16)
    live_share = lax.dynamic_slice_in_dim(live_rows, local_row_start, shared_row_block, 0)
    mlp_total = lax.psum(contract(active, w_reduce, 1, 1).astype(jnp.bfloat16), "tp").astype(
        jnp.float32
    )
    out_share = (
        lax.dynamic_slice_in_dim(hidden_input, local_row_start, shared_row_block, 0)
        + lax.dynamic_slice_in_dim(mlp_total, local_row_start, shared_row_block, 0)
        + b_down
    )
    result = (live_share * out_share).astype(jnp.bfloat16)
    output_gradient = out_cotangent.astype(jnp.float32) * live_rows
    grad_outb = output_gradient.astype(jnp.bfloat16)
    grad_share = lax.dynamic_slice_in_dim(output_gradient, local_row_start, shared_row_block, 0)
    grad_reduce = contract(grad_outb, active, 0, 0)
    grad_active = jnp.dot(grad_outb, w_reduce, preferred_element_type=jnp.float32)
    unused, gelu_back = jax.vjp(activate, before)
    grad_beforeb = gelu_back(grad_active)[0].astype(jnp.bfloat16)
    grad_expand = contract(normed_twob, grad_beforeb, 0, 0)
    up_bias_part = jnp.sum(grad_beforeb.astype(jnp.float32), 0)
    second_norm_gradient = lax.psum(
        contract(grad_beforeb, w_expand, 1, 1).astype(jnp.bfloat16), "tp"
    ).astype(jnp.float32)
    hidden_gradient = output_gradient + norm_backward_pass(
        second_norm_gradient, second_standardized, second_inverse_deviation, second_norm_gain
    )
    grad_resb = hidden_gradient.astype(jnp.bfloat16)
    residual_share_gradient = lax.dynamic_slice_in_dim(
        hidden_gradient, local_row_start, shared_row_block, 0
    )
    second_norm_shared = lax.dynamic_slice_in_dim(
        second_norm_gradient, local_row_start, shared_row_block, 0
    )
    gain_two_grad = jnp.sum(
        second_norm_shared
        * lax.dynamic_slice_in_dim(second_standardized, local_row_start, shared_row_block, 0),
        0,
    )
    bias_two_grad = jnp.sum(second_norm_shared, 0)
    bias_out_grad = jnp.sum(residual_share_gradient, 0)
    down_bias_grad = jnp.sum(grad_share, 0)
    grad_proj = contract(grad_resb, context_all, 0, 0)
    grad_context = (
        jnp.dot(grad_resb, w_proj, preferred_element_type=jnp.float32)
        .astype(jnp.bfloat16)
        .reshape(length, heads_here, HD)
    )

    def attend_back(running, block_index):
        grad_keys, grad_values = running
        masked, query_block = scores_for(block_index)
        chances = jnp.exp(masked - log_totals[block_index][..., None])
        grad_block = lax.dynamic_slice_in_dim(grad_context, block_index * block_rows, block_rows, 0)
        grad_values = grad_values + jnp.einsum(
            "hqk,qhe->khe",
            chances.astype(jnp.bfloat16),
            grad_block,
            preferred_element_type=jnp.float32,
        )
        grad_chances = jnp.einsum(
            "qhe,khe->hqk", grad_block, values, preferred_element_type=jnp.float32
        )
        grad_scores = (
            chances * (grad_chances - jnp.sum(chances * grad_chances, -1, keepdims=True))
        ).astype(jnp.bfloat16)
        grad_query = (
            jnp.einsum("hqk,khe->qhe", grad_scores, keys, preferred_element_type=jnp.float32)
            * score_scale
        )
        grad_keys = (
            grad_keys
            + jnp.einsum(
                "hqk,qhe->khe", grad_scores, query_block, preferred_element_type=jnp.float32
            )
            * score_scale
        )
        return ((grad_keys, grad_values), grad_query)

    zeros_heads = jnp.zeros((length, heads_here, HD), jnp.float32)
    (grad_keys, grad_values), grad_queries = lax.scan(
        attend_back, (zeros_heads, zeros_heads), jnp.arange(blocks)
    )
    grad_queries = grad_queries.reshape(length, heads_here, HD)
    grad_projected = (
        jnp.stack([grad_queries, grad_keys, grad_values], 2)
        .astype(jnp.bfloat16)
        .reshape(length, heads_here * 3 * HD)
    )
    grad_attn = contract(normed_oneb, grad_projected, 0, 0)
    projected_sums = jnp.sum(grad_projected.astype(jnp.float32), 0).reshape(heads_here, 3, HD)
    query_value = jnp.stack([projected_sums[:, 0], projected_sums[:, 2]], 1)
    query_value_full = lax.dynamic_update_slice_in_dim(
        jnp.zeros((b_qv.shape[0] // (2 * HD), 2, HD), jnp.float32),
        query_value,
        tp_rank * heads_here,
        0,
    ).reshape(-1)
    up_bias_full = lax.dynamic_update_slice_in_dim(
        jnp.zeros(b_up.shape, jnp.float32), up_bias_part, tp_rank * hidden_here, 0
    )
    first_norm_gradient = lax.dynamic_slice_in_dim(
        lax.psum(contract(grad_projected, w_attn, 1, 1).astype(jnp.bfloat16), "tp").astype(
            jnp.float32
        ),
        local_row_start,
        shared_row_block,
        0,
    )
    shared_standardized = lax.dynamic_slice_in_dim(
        first_standardized, local_row_start, shared_row_block, 0
    )
    shared_inverse_deviation = lax.dynamic_slice_in_dim(
        first_inverse_deviation, local_row_start, shared_row_block, 0
    )
    input_gradient = residual_share_gradient + norm_backward_pass(
        first_norm_gradient, shared_standardized, shared_inverse_deviation, first_norm_gain
    )
    first_gain_gradient = jnp.sum(first_norm_gradient * shared_standardized, 0)
    bias_one_grad = jnp.sum(first_norm_gradient, 0)
    grads_attn, grads_proj, grads_expand, grads_reduce = (
        lax.psum_scatter(
            grad_attn.astype(jnp.bfloat16), "grp", scatter_dimension=0, tiled=True
        ).astype(jnp.float32),
        lax.psum_scatter(
            grad_proj.astype(jnp.bfloat16), "grp", scatter_dimension=0, tiled=True
        ).astype(jnp.float32),
        lax.psum_scatter(
            grad_expand.astype(jnp.bfloat16), "grp", scatter_dimension=0, tiled=True
        ).astype(jnp.float32),
        lax.psum_scatter(
            grad_reduce.astype(jnp.bfloat16), "grp", scatter_dimension=0, tiled=True
        ).astype(jnp.float32),
    )
    small_grads = lax.psum(
        (
            query_value_full,
            bias_out_grad,
            up_bias_full,
            down_bias_grad,
            first_gain_gradient,
            bias_one_grad,
            gain_two_grad,
            bias_two_grad,
        ),
        ("grp", "tp"),
    )
    return (
        result,
        input_gradient,
        grads_attn,
        small_grads[0],
        grads_proj,
        small_grads[1],
        grads_expand,
        small_grads[2],
        grads_reduce,
        small_grads[3],
        small_grads[4],
        small_grads[5],
        small_grads[6],
        small_grads[7],
    )


def solution(mesh):
    in_specs = (
        P("grp", None),
        P("grp", None),
        P(),
        P(),
        P("grp", "tp"),
        P(),
        P("grp", "tp"),
        P(),
        P("grp", "tp"),
        P(),
        P("grp", "tp"),
        P(),
        P(),
        P(),
        P(),
        P(),
    )
    out_specs = (
        P(("grp", "tp"), None),
        P(("grp", "tp"), None),
        P("grp", "tp"),
        P(),
        P("grp", "tp"),
        P(),
        P("grp", "tp"),
        P(),
        P("grp", "tp"),
        P(),
        P(),
        P(),
        P(),
        P(),
    )
    return jax.shard_map(
        on_device, mesh=mesh, in_specs=in_specs, out_specs=out_specs, check_vma=False
    )
```

profile of v0, /device:TPU:0, one launch (start us, length us, event | category | flops | bytes accessed | tf_op | source)
XLA Modules:
  0.0 1345.2 jit_solution(15598600205464487332)
XLA Ops:
  13.4 4.7 convert_reduce_fusion
  21.4 35.8 %all-gather.5.cloned.1.call-done = bf16[2048,768]{1,0:T(8,128)(2,1)} async-done(((bf16[512,768]{1,0:T(8,128)(2,1)}), bf16[2048,768]{1,0:T(8,128)(2,1)}) %all-gather.5.cloned.1.call-update) | async-done | bytes 3145744 | tf_op jit(solution)/shard_map/all_gather | solution.py:54
  57.1 11.2 add_convert_fusion.2
  72.6 46.2 %while.28 = (s32[]{:T(128)}, bf16[4,512,2,128]{3,2,1,0:T(2,128)(2,1)}, f32[4,2,512]{2,1,0:T(2,128)}, s32[4]{0:T(128)S(1)}, s32[2048]{0:T(1024)S(1)}, /*index=5*/...) while((s32[]{:T(128)}, ...), condition=%wide.region_7.8_spmd.clone, body=%wide.region_4.7_spmd.clone.sunk | while | flops 1102183936 | bytes 32557260 | solution.py:129
  118.9 8.2 convolution_convert_fusion.3
  133.5 169.3 %all-reduce.7.cloned.1.call-done = bf16[2048,2048]{1,0:T(8,128)(2,1)} async-done(((bf16[2048,2048]{1,0:T(8,128)(2,1)}), bf16[2048,2048]{1,0:T(8,128)(2,1)}) %all-reduce.7.cloned.1.call-update) | async-done | bytes 8388624 | tf_op jit(solution)/shard_map/psum | solution.py:131
  302.8 17.6 %fusion.88 = (f32[2048]{0:T(1024)S(1)}, f32[2048,2048]{1,0:T(8,128)}, f32[2048,2048]{1,0:T(8,128)}) fusion(f32[2048]{0:T(1024)S(1)} %copy-done.25, bf16[2048,2048]{1,0:T(8,128)(2,1)} %all-reduce.7.cloned.1.call-done, bf16[2048,2048]{1,0:T(8,128)(2,1)} %param.20, f32[2048]{0:T(1024)S(1)} %add_rsqrt_fusion.1, f32[2048]{0:T(1024)S(1)} %broadcast_multiply_fusion.3), kind=kLoop, calls=%fused_computation.141 | loop fusion | flops 29358080 | bytes 50364416 | tf_op jit(solution)/shard_map/reduce_sum | solution.py:10
  320.4 7.6 multiply_reduce_fusion.2
  328.0 11.8 subtract_multiply_fusion
  339.8 18.2 %all-gather.9.cloned.1.call-done = bf16[2048,1024]{1,0:T(8,128)(2,1)} async-done(((bf16[512,1024]{1,0:T(8,128)(2,1)}), bf16[2048,1024]{1,0:T(8,128)(2,1)}) %all-gather.9.cloned.1.call-update) | async-done | bytes 4194320 | tf_op jit(solution)/shard_map/all_gather | solution.py:56
  358.0 15.5 %fusion.75 = f32[2048,1024]{1,0:T(8,128)} fusion(bf16[2048,1024]{1,0:T(8,128)(2,1)} %all-gather.9.cloned.1.call-done, f32[2048,2048]{1,0:T(8,128)} %subtract_multiply_fusion, f32[2048]{0:T(1024)S(1)} %copy-done.31, f32[2048]{0:T(1024)S(1)} %copy-done.21), kind=kOutput, calls=%fused_computation.102 | convolution fusion | flops 8602517504 | bytes 29376512 | tf_op jit(solution)/shard_map/dot_general | solution.py:140
  373.5 39.5 %all-gather.11.cloned.1.call-done = bf16[2048,1024]{1,0:T(8,128)(2,1)} async-done(((bf16[512,1024]{1,0:T(8,128)(2,1)}), bf16[2048,1024]{1,0:T(8,128)(2,1)}) %all-gather.11.cloned.1.call-update) | async-done | bytes 4194320 | tf_op jit(solution)/shard_map/all_gather | solution.py:57
  413.0 19.9 %convert_reduce_fusion.1 = (f32[1024]{0:T(1024)}, bf16[2048,1024]{1,0:T(8,128)(2,1)S(1)}) fusion(f32[2048,1024]{1,0:T(8,128)} %fusion.75, f32[1024]{0:T(1024)S(1)} %dynamic_slice.59, bf16[2048,1024]{1,0:T(8,128)(2,1)} %all-gather.11.cloned.1.call-done, f32[2048]{0:T(1024)S(1)} %compare_convert_fusion, bf16[2048,2048]{1,0:T(8,128)(2,1)} %param.21), kind=kOutput, calls=%fused_computation.74 | convolution fusion | flops 8650750976 | bytes 25182208 | tf_op jit(solution)/shard_map/dot_general | solution.py:156
  434.8 10.9 convolution_convert_fusion.1
  445.8 175.7 %all-reduce.9.cloned.1.call-done = bf16[2048,2048]{1,0:T(8,128)(2,1)} async-done(((bf16[2048,2048]{1,0:T(8,128)(2,1)}), bf16[2048,2048]{1,0:T(8,128)(2,1)}) %all-reduce.9.cloned.1.call-update) | async-done | bytes 8388624 | tf_op jit(solution)/shard_map/psum | solution.py:161
  621.4 10.3 multiply_reduce_fusion.3
  631.7 19.1 %convert_multiply_fusion = (f32[2048,2048]{1,0:T(8,128)}, f32[2048,2048]{1,0:T(8,128)S(1)}) fusion(bf16[2048,2048]{1,0:T(8,128)(2,1)} %param.21, f32[2048]{0:T(1024)S(1)} %compare_convert_fusion, f32[2048]{0:T(1024)S(1)} %broadcast_multiply_fusion, f32[2048]{0:T(1024)S(1)} %broadcast_multiply_fusion.1, f32[2048]{0:T(1024)S(1)} %copy-done.21, ...), kind=kLoop, calls=%fused_computation.59 | loop fusion | flops 46137344 | bytes 67158016 | tf_op jit(solution)/shard_map/mul | solution.py:152
  650.8 5.7 copy-done
  660.2 16.8 %fusion.61 = bf16[2048,1024]{1,0:T(8,128)(2,1)} fusion(bf16[2048,2048]{1,0:T(8,128)(2,1)} %param.21, f32[2048]{0:T(1024)S(1)} %compare_convert_fusion, f32[2048,1024]{1,0:T(8,128)} %fusion.75, f32[1024]{0:T(1024)S(1)} %dynamic_slice.59), kind=kOutput, calls=%fused_computation.91 | convolution fusion | flops 8625586176 | bytes 20983808 | tf_op jit(solution)/shard_map/dot_general | solution.py:26
  677.1 15.3 %convolution_convert_fusion.4 = bf16[2048,1024]{1,0:T(8,128)(2,1)} fusion(bf16[2048,1024]{1,0:T(8,128)(2,1)} %copy-done.34, f32[2048,2048]{1,0:T(8,128)} %subtract_multiply_fusion, f32[2048]{0:T(1024)S(1)} %copy-done.31, f32[2048]{0:T(1024)S(1)} %copy-done.21), kind=kOutput, calls=%fused_computation.92 | convolution fusion | flops 8604614656 | bytes 25182208 | tf_op jit(solution)/shard_map/dot_general | solution.py:26
  692.6 10.1 fusion.67
  702.7 89.9 %while.29 = (s32[]{:T(128)}, f32[2048,2,128]{0,2,1:T(8,128)S(1)}, f32[2048,2,128]{0,2,1:T(8,128)}, bf16[4,512,2,128]{3,1,0,2:T(8,128)(2,1)}, s32[4]{0:T(128)S(1)...) while((s32[]{:T(128)}, f32[2048,2,128]{0,2,1:T(8,128)S(1)}, ...), condition=%wide.region_17.18_spmd.clone, body=%wide.region_15.17_spmd.clone.sunk | while | flops 2721709568 | bytes 97040784 | solution.py:220
  732.0 5.0 fusion.149
  754.7 5.0 fusion.149
  777.4 5.0 fusion.149
  801.9 13.0 convolution_convert_fusion.5
  815.0 17.8 %convolution_convert_fusion.2 = bf16[2048,2048]{1,0:T(8,128)(2,1)} fusion(bf16[2048,1024]{1,0:T(8,128)(2,1)} %all-gather.11.cloned.1.call-done, f32[2048,1024]{1,0:T(8,128)} %fusion.75, f32[1024]{0:T(1024)S(1)} %copy-done.28), kind=kOutput, calls=%fused_computation.78 | convolution fusion | flops 8615100416 | bytes 20975616 | tf_op jit(solution)/shard_map/dot_general | solution.py:26
  832.8 9.2 convolution_convert_fusion
  843.3 11.3 convert_element_type.149
  870.1 325.1 %all-reduce.13.cloned.1.call-done = (bf16[2048,2048]{1,0:T(8,128)(2,1)}, bf16[2048,2048]{1,0:T(8,128)(2,1)}) async-done(((bf16[2048,2048]{1,0:T(8,128)(2,1)}, bf16[2048,2048]{1,0:T(8,128)(2,1)}), (bf16[2048,2048]{1,0:T(8,128)(2,1)}, bf16[2048,2048]{1,0:T(8,128)(2,1)})) %all-reduce.13.cloned.1.call-update) | async-done | bytes 16777232 | tf_op jit(solution)/shard_map/psum | solution.py:143
  1198.4 5.2 dynamic-slice_reduce_fusion.2
  1206.8 120.9 %all-reduce.11.cloned.1.call-done = (f32[4096]{0:T(1024)}, f32[2048]{0:T(1024)}, f32[8192]{0:T(1024)}, f32[2048]{0:T(1024)}, f32[2048]{0:T(1024)}, /*index=5*/f32[2048]{0:T(1024)}, f32[2048]{0:T(1024)}, f32[2048]{0:T(1024)}) async-done(((f32[4096]{0:T(1024)}, f32[2048]{0:T(1024)}, f32[8192]{0:T(1024)}, f32[2048]{0:T(1024)}, f32[2048]{0:T(1024)}, /*index=5*/f32[2048]{0:T(1024)}, f32[2048]{0:T(1024)}, ...) | async-done | bytes 98320 | tf_op jit(solution)/shard_map/psum | solution.py:274
  (263 shorter events, 175.6 us)
Async XLA Ops:
  7.2 50.0 %all-gather.5.cloned.1.call-start = ((), (), s32[]{:S(2)}) async-start(), calls=%async_computation.4 | async-start | bytes 3932160 | tf_op jit(solution)/shard_map/all_gather | solution.py:54
  9.6 109.2 %all-gather.7.cloned.1.call-start = ((), (), s32[]{:S(2)}) async-start(), calls=%async_computation.5 | async-start | bytes 1310720 | tf_op jit(solution)/shard_map/all_gather | solution.py:55
  11.5 291.4 %all-reduce.7.cloned.1.call-start = ((), (), s32[]{:S(2)}) async-start(), calls=%async_computation.6 | async-start | bytes 16777216 | tf_op jit(solution)/shard_map/psum | solution.py:131
  13.4 43.8 %copy-start.22 = (f32[2048]{0:T(1024)S(1)}, f32[2048]{0:T(1024)}, u32[]{:S(2)}) copy-start(f32[2048]{0:T(1024)} %param.32) | copy-start | bytes 24580
  13.4 43.7 %copy-start.32 = (f32[2048]{0:T(1024)S(1)}, f32[2048]{0:T(1024)}, u32[]{:S(2)}) copy-start(f32[2048]{0:T(1024)} %param.33) | copy-start | bytes 24580
  19.0 283.8 %copy-start.15 = (f32[2048]{0:T(1024)}, f32[2048]{0:T(1024)S(1)}, u32[]{:S(2)}) copy-start(f32[2048]{0:T(1024)S(1)} %broadcast_multiply_fusion.3) | copy-start | bytes 24580
  21.4 281.5 %copy-start.19 = (f32[2048]{0:T(1024)}, f32[2048]{0:T(1024)S(1)}, u32[]{:S(2)}) copy-start(f32[2048]{0:T(1024)S(1)} %add_rsqrt_fusion.1) | copy-start | bytes 24580
  118.8 8.3 copy-start.1
  127.1 175.8 %copy-start.25 = (f32[2048]{0:T(1024)S(1)}, f32[2048]{0:T(1024)}, u32[]{:S(2)}) copy-start(f32[2048]{0:T(1024)} %param.27) | copy-start | bytes 24580
  127.1 230.8 %all-gather.9.cloned.1.call-start = ((), (), s32[]{:S(2)}) async-start(), calls=%async_computation.7 | async-start | bytes 5242880 | tf_op jit(solution)/shard_map/all_gather | solution.py:56
  129.9 283.0 %all-gather.11.cloned.1.call-start = ((), (), s32[]{:S(2)}) async-start(), calls=%async_computation.8 | async-start | bytes 5242880 | tf_op jit(solution)/shard_map/all_gather | solution.py:57
  132.8 488.7 %all-reduce.9.cloned.1.call-start = ((), (), s32[]{:S(2)}) async-start(), calls=%async_computation.9 | async-start | bytes 16777216 | tf_op jit(solution)/shard_map/psum | solution.py:161
  132.8 527.3 %copy-start.18 = (f32[2048]{0:T(1024)}, f32[2048]{0:T(1024)S(1)}, u32[]{:S(2)}) copy-start(f32[2048]{0:T(1024)S(1)} %compare_convert_fusion) | copy-start | bytes 24580
  133.5 526.6 %copy-start.27 = (f32[1024]{0:T(1024)}, f32[1024]{0:T(1024)S(1)}, u32[]{:S(2)}) copy-start(f32[1024]{0:T(1024)S(1)} %dynamic_slice.59) | copy-start | bytes 12292
  328.0 30.0 %copy-start.21 = (f32[2048]{0:T(1024)S(1)}, f32[2048]{0:T(1024)}, u32[]{:S(2)}) copy-start(f32[2048]{0:T(1024)} %param.34) | copy-start | bytes 24580
  328.0 30.0 %copy-start.31 = (f32[2048]{0:T(1024)S(1)}, f32[2048]{0:T(1024)}, u32[]{:S(2)}) copy-start(f32[2048]{0:T(1024)} %param.35) | copy-start | bytes 24580
  413.0 21.8 %copy-start.29 = (bf16[2048,1024]{1,0:T(8,128)(2,1)S(1)}, bf16[2048,1024]{1,0:T(8,128)(2,1)}, u32[]{:S(2)}) copy-start(bf16[2048,1024]{1,0:T(8,128)(2,1)} %all-gather.9.cloned.1.call-done) | copy-start | bytes 12582916
  445.7 414.6 %reduce-scatter.7.cloned.1.call-start = ((), (), s32[]{:S(2)}) async-start(), calls=%async_computation.11 | async-start | bytes 1310720 | tf_op jit(solution)/shard_map/reduce_scatter | solution.py:264
  631.7 24.8 %copy-start.8 = (bf16[4,512,2,128]{3,2,1,0:T(2,128)(2,1)S(1)}, bf16[4,512,2,128]{3,2,1,0:T(2,128)(2,1)}, u32[]{:S(2)}) copy-start(bf16[4,512,2,128]{3,2,1,0:T(2,128)(2,1)} %get-tuple-element.126) | copy-start | bytes 3145732
  660.1 201.9 %reduce-scatter.11.cloned.1.call-start = ((), (), s32[]{:S(2)}) async-start(), calls=%async_computation.13 | async-start | bytes 5242880 | tf_op jit(solution)/shard_map/reduce_scatter | solution.py:270
  677.1 187.8 %reduce-scatter.9.cloned.1.call-start = ((), (), s32[]{:S(2)}) async-start(), calls=%async_computation.12 | async-start | bytes 5242880 | tf_op jit(solution)/shard_map/reduce_scatter | solution.py:267
  692.5 10.2 copy-start.2
  692.5 10.2 copy-start.11
  692.5 175.1 %reduce-scatter.5.cloned.1.call-start = ((), (), s32[]{:S(2)}) async-start(), calls=%async_computation.10 | async-start | bytes 3932160 | tf_op jit(solution)/shard_map/reduce_scatter | solution.py:261
  801.8 13.1 copy-start.28
  814.9 17.9 %copy-start.9 = (bf16[2048,2,3,128]{0,3,2,1:T(8,128)(2,1)S(1)}, bf16[2048,2,3,128]{0,3,2,1:T(8,128)(2,1)}, u32[]{:S(2)}) copy-start(bf16[2048,2,3,128]{0,3,2,1:T(8,128)(2,1)} %copy.80) | copy-start | bytes 9437188
  814.9 380.3 %all-reduce.13.cloned.1.call-start = ((), (), s32[]{:S(2)}) async-start(), calls=%async_computation.15 | async-start | bytes 33554432 | tf_op jit(solution)/shard_map/psum | solution.py:143
  814.9 17.8 %copy-start.30 = (bf16[2048,768]{1,0:T(8,128)(2,1)S(1)}, bf16[2048,768]{1,0:T(8,128)(2,1)}, u32[]{:S(2)}) copy-start(bf16[2048,768]{1,0:T(8,128)(2,1)} %all-gather.5.cloned.1.call-done) | copy-start | bytes 9437188
  841.9 485.7 %all-reduce.11.cloned.1.call-start = ((), (), s32[]{:S(2)}) async-start(), calls=%async_computation.14 | async-start | bytes 196608 | tf_op jit(solution)/shard_map/psum | solution.py:274
  843.3 11.3 copy-start.14
  860.2 343.4 %copy-start.17 = (f32[16,2,128]{2,1,0:T(2,128)}, f32[16,2,128]{2,1,0:T(2,128)S(1)}, u32[]{:S(2)}) copy-start(f32[16,2,128]{2,1,0:T(2,128)S(1)} %constant_dynamic-update-slice_fusion) | copy-start | bytes 49156
  864.8 338.8 %copy-start.24 = (f32[2048]{0:T(1024)S(1)}, f32[2048]{0:T(1024)}, u32[]{:S(2)}) copy-start(f32[2048]{0:T(1024)} %param.31) | copy-start | bytes 24580
  (27 other events, 126.6 us)
Sparse Core Ops, SparseCore 0:
  10.4 46.6 all-gather.4
  59.6 26.6 all-gather.6
  127.2 175.5 all-reduce.6
  305.1 52.8 all-gather.8
  360.2 52.6 all-gather.10
  445.8 175.5 all-reduce.8
  660.2 27.8 reduce-scatter.6
  691.3 52.7 reduce-scatter.10
  747.1 52.6 reduce-scatter.8
  815.0 43.7 reduce-scatter.4
  861.6 333.5 all-reduce.12
  1203.8 123.8 all-reduce.10
where the time goes:
time: 1350 us
  waiting for transfers between devices  885 us (66%)
  matrix products  229 us (17%)
  other arithmetic  157 us (12%)
  local copies, waits for them, and re-layouts  45.5 us (3%)
  between operations  14.9 us (1%)
  loops' own time  14.3 us (1%)
    psum x1, waiting for transfers between devices, on_device(): lax.psum(contract(active, w_reduce, 1, 1).astype(jnp.bfloat16), 'tp')  325 us
    psum x1, waiting for transfers between devices, on_device(): lax.psum(contract(grad_beforeb, w_expand, 1, 1).astype(jnp.bfloat16), 'tp')  176 us
    psum x1, waiting for transfers between devices, on_device(): lax.psum(contract(context_all, w_proj, 1, 1).astype(jnp.bfloat16), 'tp')  169 us
    psum x1, waiting for transfers between devices, on_device(): lax.psum((query_value_full, bias_out_grad, up_bias_full, down_bias_grad,...  121 us
    dot_general x8, matrix products, contract(): lax.dot_general(left, right, (((left_dim,), (right_dim,)), ((), ())), pre...  94.8 us
    all_gather x1, waiting for transfers between devices, on_device(): lax.all_gather(w_down.astype(jnp.bfloat16), 'grp', axis=0, tiled=True)  39.5 us
    all_gather x1, waiting for transfers between devices, on_device(): lax.all_gather(w_qkv.astype(jnp.bfloat16), 'grp', axis=0, tiled=True)  35.8 us
  transfers between devices with their start and end apart: 12, of which 7 were waited for; matrix products, arithmetic and copies ran while one was open for 24% of the time, Pallas kernels for 0%

commit v1 on v0

v1 whole, which is shorter than its diff:
```python
import functools

import jax
import jax.numpy as jnp
from jax import lax
from jax.experimental import pallas as pl
from jax.experimental.pallas import tpu as pltpu
from jax.sharding import PartitionSpec as P

HD = 128
BLK=512
F32=jnp.float32
BF=jnp.bfloat16
LOG2E=1.4426950408889634

def dg(a,b,ca,cb):
    return lax.dot_general(a,b,(((ca,),(cb,)),((),())),preferred_element_type=F32)

def attn_fwd_kernel(info, q_ref, k_ref, v_ref, o_ref, lse_ref, *, nb):
    c = HD ** -0.5 * LOG2E
    for qi in range(nb):
        rows = pl.ds(qi*BLK, BLK)
        @pl.when(info[2, qi] > 0)
        def _():
            q = q_ref[rows, :]
            def step(j, carry, diag=False):
                m, l, acc = carry
                kr = pl.ds(pl.multiple_of(j*BLK, BLK), BLK)
                s = dg(k_ref[kr, :], q, 1, 1)
                if diag:
                    ki = lax.broadcasted_iota(jnp.int32, s.shape, 0)
                    qq = lax.broadcasted_iota(jnp.int32, s.shape, 1)
                    s = jnp.where(ki <= qq, s, -1e30)
                mn = jnp.maximum(m, jnp.max(s, 0, keepdims=True))
                p = jnp.exp2(s*c - mn*c)
                alpha = jnp.exp2((m - mn)*c)
                l = l*alpha + jnp.sum(p, 0, keepdims=True)
                acc = acc*alpha + dg(v_ref[kr, :], p.astype(BF), 0, 0)
                return mn, l, acc
            init = (jnp.full((1, BLK), -1e30, F32), jnp.zeros((1, BLK), F32), jnp.zeros((HD, BLK), F32))
            carry = step(qi, init, True)
            m, l, acc = lax.fori_loop(info[0, qi], qi, step, carry)
            o_ref[rows, :] = jnp.transpose(acc / l).astype(BF)
            lse_ref[0, :, rows] = m*c + jnp.log2(l)
        @pl.when(info[2, qi] <= 0)
        def _():
            o_ref[rows, :] = jnp.zeros((BLK, HD), BF)
            lse_ref[0, :, rows] = jnp.zeros((1, BLK), F32)

def attn_fwd(info, proj):
    length = proj.shape[0]; heads = proj.shape[1]//(3*HD); nb = length//BLK
    spec = lambda o: pl.BlockSpec((length, HD), lambda h, info: (0, 3*h+o))
    return pl.pallas_call(functools.partial(attn_fwd_kernel, nb=nb),
        grid_spec=pltpu.PrefetchScalarGridSpec(num_scalar_prefetch=1, grid=(heads,),
            in_specs=[spec(0), spec(1), spec(2)],
            out_specs=[pl.BlockSpec((length, HD), lambda h, info: (0, h)), pl.BlockSpec((1, 1, length), lambda h, info: (h, 0, 0))]),
        out_shape=[jax.ShapeDtypeStruct((length, heads*HD), BF), jax.ShapeDtypeStruct((heads, 1, length), F32)],
        compiler_params=pltpu.CompilerParams(vmem_limit_bytes=40<<20), name="attn_fwd",
        cost_estimate=pl.CostEstimate(flops=heads*length*length*HD*2, bytes_accessed=length*heads*HD*8, transcendentals=heads*length*length//2),
    )(info, proj, proj, proj)

def attn_bwd_kernel(info, q_ref, k_ref, v_ref, o_ref, do_ref, lse_ref, dp_ref, dq_sc, dl_sc, *, nb):
    sc = HD ** -0.5
    c = sc * LOG2E
    prod = do_ref[...].astype(F32) * o_ref[...].astype(F32)
    dl_sc[...] = jnp.sum(jnp.transpose(prod), 0, keepdims=True)
    dq_sc[...] = jnp.zeros_like(dq_sc)
    for j in range(nb):
        kr = pl.ds(j*BLK, BLK)
        @pl.when(info[2, j] > 0)
        def _():
            k = k_ref[kr, :]; v = v_ref[kr, :]
            def step(i, carry, diag=False):
                dk, dv = carry
                qr = pl.ds(pl.multiple_of(i*BLK, BLK), BLK)
                q = q_ref[qr, :]; do = do_ref[qr, :]
                s = dg(k, q, 1, 1)
                p = jnp.exp2(s*c - lse_ref[0, :, qr])
                if diag:
                    ki = lax.broadcasted_iota(jnp.int32, s.shape, 0)
                    qq = lax.broadcasted_iota(jnp.int32, s.shape, 1)
                    p = jnp.where(ki <= qq, p, 0.0)
                dp = dg(v, do, 1, 1)
                ds = (p * (dp - dl_sc[:, qr])).astype(BF)
                dv = dv + dg(p.astype(BF), do, 1, 0)
                dk = dk + dg(ds, q, 1, 0)
                dq_sc[qr, :] += dg(ds, k, 0, 0)
                return dk, dv
            z = jnp.zeros((BLK, HD), F32)
            carry = step(j, (z, z), True)
            dk, dv = lax.fori_loop(j+1, info[1, j]+1, step, carry)
            dp_ref[kr, HD:2*HD] = (dk*sc).astype(BF)
            dp_ref[kr, 2*HD:] = dv.astype(BF)
        @pl.when(info[2, j] <= 0)
        def _():
            dp_ref[kr, HD:] = jnp.zeros((BLK, 2*HD), BF)
    dp_ref[:, :HD] = (dq_sc[...]*sc).astype(BF)

def attn_bwd(info, proj, ctx, dctx, lse):
    length = proj.shape[0]; heads = proj.shape[1]//(3*HD); nb = length//BLK
    spec = lambda o: pl.BlockSpec((length, HD), lambda h, info: (0, 3*h+o))
    hs = pl.BlockSpec((length, HD), lambda h, info: (0, h))
    return pl.pallas_call(functools.partial(attn_bwd_kernel, nb=nb),
        grid_spec=pltpu.PrefetchScalarGridSpec(num_scalar_prefetch=1, grid=(heads,),
            in_specs=[spec(0), spec(1), spec(2), hs, hs, pl.BlockSpec((1, 1, length), lambda h, info: (h, 0, 0))],
            out_specs=pl.BlockSpec((length, 3*HD), lambda h, info: (0, h)),
            scratch_shapes=[pltpu.VMEM((length, HD), F32), pltpu.VMEM((1, length), F32)]),
        out_shape=jax.ShapeDtypeStruct((length, heads*3*HD), BF),
        compiler_params=pltpu.CompilerParams(vmem_limit_bytes=40<<20), name="attn_bwd",
        cost_estimate=pl.CostEstimate(flops=heads*length*length*HD*5, bytes_accessed=length*heads*HD*16, transcendentals=heads*length*length//2),
    )(info, proj, proj, proj, ctx, dctx, lse)

MESH = pl.DeviceIdType.MESH


def small_kernel(x_ref, a_ref, b_ref, gbuf, tbuf, gs, gr, ts, tr, *, n_grp, n_tp, a_rows):
    t = lax.axis_index("tp")
    g = lax.axis_index("grp")
    bar = pltpu.get_barrier_semaphore()
    for d in range(1, n_grp):
        pl.semaphore_signal(bar, inc=1, device_id=(lax.rem(g + d, n_grp), t), device_id_type=MESH)
    for d in range(1, n_tp):
        pl.semaphore_signal(bar, inc=1, device_id=(g, lax.rem(t + d, n_tp)), device_id_type=MESH)
    pl.semaphore_wait(bar, n_grp + n_tp - 2)
    copies = []
    for d in range(1, n_grp):
        cp = pltpu.make_async_remote_copy(
            x_ref, gbuf.at[g], gs.at[d], gr.at[d],
            device_id=(lax.rem(g + d, n_grp), t), device_id_type=MESH)
        cp.start()
        copies.append(cp)
    gbuf[g] = x_ref[...]
    for cp in copies:
        cp.wait()
    total = gbuf[0]
    for i in range(1, n_grp):
        total = total + gbuf[i]
    tbuf[t] = total
    copies = []
    for d in range(1, n_tp):
        cp = pltpu.make_async_remote_copy(
            tbuf.at[t], tbuf.at[t], ts.at[d], tr.at[d],
            device_id=(g, lax.rem(t + d, n_tp)), device_id_type=MESH)
        cp.start()
        copies.append(cp)
    for cp in copies:
        cp.wait()
    total = tbuf[0, :a_rows]
    for i in range(1, n_tp):
        total = total + tbuf[i, :a_rows]
    a_ref[...] = total
    b_ref[...] = tbuf[:, a_rows:]


def small_sum(common, own):
    n_grp, n_tp = lax.axis_size("grp"), lax.axis_size("tp")
    a_rows = common.shape[0] // 128
    own_rows = own.shape[0] // 128
    pad = -own_rows % 8
    x = jnp.concatenate([common, own, jnp.zeros((pad * 128,), F32)]).reshape(-1, 128)
    rows = x.shape[0]
    vm = pl.BlockSpec(memory_space=pltpu.VMEM)
    a, b = pl.pallas_call(
        functools.partial(small_kernel, n_grp=n_grp, n_tp=n_tp, a_rows=a_rows),
        in_specs=[vm], out_specs=[vm, vm],
        out_shape=[jax.ShapeDtypeStruct((a_rows, 128), F32),
                   jax.ShapeDtypeStruct((n_tp, rows - a_rows, 128), F32)],
        scratch_shapes=[pltpu.VMEM((n_grp, rows, 128), F32), pltpu.VMEM((n_tp, rows, 128), F32),
                        pltpu.SemaphoreType.DMA((n_grp,)), pltpu.SemaphoreType.DMA((n_grp,)),
                        pltpu.SemaphoreType.DMA((n_tp,)), pltpu.SemaphoreType.DMA((n_tp,))],
        compiler_params=pltpu.CompilerParams(collective_id=1, has_side_effects=True),
        name="small_sum",
    )(x)
    return a.reshape(-1), b.reshape(n_tp, -1)[:, : own.shape[0]]


def normalize(rows, gain, bias):
    mean_row = jnp.mean(rows, -1, keepdims=True)
    centred = rows - mean_row
    inverse = lax.rsqrt(jnp.mean(centred * centred, -1, keepdims=True) + 1e-05)
    normed = centred * inverse
    return normed * gain + bias, normed, inverse


def norm_back(grad_norm, normed, inverse, gain):
    scaled = grad_norm * gain
    inner = jnp.mean(scaled, -1, keepdims=True) + normed * jnp.mean(scaled * normed, -1, keepdims=True)
    return inverse * (scaled - inner)


def on_device(layer_input, out_cotangent, seq_group, seq_len, w_qkv, b_qv, w_out, b_out, w_up, b_up,
              w_down, b_down, first_norm_gain, first_norm_bias, second_norm_gain, second_norm_bias):
    tp = lax.axis_index("tp")
    n_tp = lax.axis_size("tp")
    grp = lax.axis_index("grp")
    length, width = layer_input.shape
    share = length // n_tp
    heads = w_out.shape[1] // HD
    hidden_here = w_up.shape[1]

    w_attn = lax.all_gather(w_qkv.astype(BF), "grp", axis=0, tiled=True)
    w_proj = lax.all_gather(w_out.astype(BF), "tp", axis=1, tiled=True)
    w_proj = lax.all_gather(w_proj, "grp", axis=0, tiled=True)
    w_expand = lax.all_gather(w_up.astype(BF), "grp", axis=0, tiled=True)
    w_reduce = lax.all_gather(w_down.astype(BF), "grp", axis=0, tiled=True)

    nb = length // BLK
    in_group = seq_group == grp
    lengths = jnp.where(in_group, seq_len, 0)
    order = jnp.arange(seq_group.shape[0], dtype=jnp.int32)
    offsets = jnp.sum(jnp.where(order[:, None] > order[None, :], lengths[None, :], 0), 1)
    starts = jnp.arange(nb, dtype=jnp.int32) * BLK
    inside = in_group[None] & (starts[:, None] >= offsets[None]) & (starts[:, None] < (offsets + lengths)[None])
    alive = jnp.any(inside, 1)
    first = jnp.sum(jnp.where(inside, (offsets // BLK)[None], 0), 1)
    last = jnp.sum(jnp.where(inside, ((offsets + lengths) // BLK - 1)[None], 0), 1)
    info = jnp.stack([first, last, alive.astype(jnp.int32)]).astype(jnp.int32)
    tokens = jnp.sum(lengths)
    row0 = tp * share
    live = (row0 + jnp.arange(share, dtype=jnp.int32) < tokens).astype(F32)[:, None]
    live_all = (jnp.arange(length, dtype=jnp.int32) < tokens)[:, None]

    def mine(x):
        return lax.dynamic_slice_in_dim(x, row0, share, 0)

    x = layer_input.astype(F32)
    n1 = normalize(x, first_norm_gain, first_norm_bias)[0].astype(BF)
    x_share = mine(layer_input).astype(F32)
    _, xhat1, inverse1 = normalize(x_share, first_norm_gain, first_norm_bias)

    head_bias = lax.dynamic_slice_in_dim(b_qv.reshape(-1, 2, HD), tp * heads, heads, 0)
    bias_three = jnp.stack(
        [head_bias[:, 0], jnp.zeros_like(head_bias[:, 0]), head_bias[:, 1]], 1).reshape(-1)
    proj = (jnp.dot(n1, w_attn, preferred_element_type=F32) + bias_three).astype(BF)
    context, lse = attn_fwd(info, proj)
    context_rows = lax.all_to_all(context, "tp", 0, 1, tiled=True)
    hidden = x_share + dg(context_rows, w_proj, 1, 1) + b_out
    n2_share, xhat2, inverse2 = normalize(hidden, second_norm_gain, second_norm_bias)
    n2 = lax.all_gather(n2_share.astype(BF), "tp", axis=0, tiled=True)

    up_bias = lax.dynamic_slice_in_dim(b_up, tp * hidden_here, hidden_here, 0)
    before = jnp.dot(n2, w_expand, preferred_element_type=F32) + up_bias
    act = functools.partial(jax.nn.gelu, approximate=True)
    active, gelu_back = jax.vjp(act, before)
    active = active.astype(BF)
    gradb = jnp.where(live_all, out_cotangent, jnp.zeros_like(out_cotangent))
    grad_active = jnp.dot(gradb, w_reduce, preferred_element_type=F32)
    dbefore = gelu_back(grad_active)[0].astype(BF)
    dn2 = lax.psum_scatter(dg(dbefore, w_expand, 1, 1).astype(BF), "tp", scatter_dimension=0, tiled=True).astype(F32)
    grad_share = mine(gradb).astype(F32)
    dh = grad_share + norm_back(dn2, xhat2, inverse2, second_norm_gain)
    dhb = dh.astype(BF)
    dcontext_rows = jnp.dot(dhb, w_proj, preferred_element_type=F32).astype(BF)
    dcontext = lax.all_to_all(dcontext_rows, "tp", 1, 0, tiled=True)

    mlp = lax.psum_scatter(dg(active, w_reduce, 1, 1).astype(BF), "tp", scatter_dimension=0, tiled=True).astype(F32)
    result = (live * (hidden + mlp + b_down)).astype(BF)
    scatter = functools.partial(lax.psum_scatter, axis_name="grp", scatter_dimension=0, tiled=True)
    grads_reduce = scatter(dg(gradb, active, 0, 0).astype(BF)).astype(F32)
    grads_expand = scatter(dg(n2, dbefore, 0, 0).astype(BF)).astype(F32)
    dh_all = lax.all_gather(dhb, "tp", axis=0, tiled=True)
    grads_proj = scatter(dg(dh_all, context, 0, 0).astype(BF)).astype(F32)

    dproj = attn_bwd(info, proj, context, dcontext, lse)
    grads_attn = scatter(dg(n1, dproj, 0, 0).astype(BF)).astype(F32)
    dn1 = lax.psum_scatter(dg(dproj, w_attn, 1, 1).astype(BF), "tp", scatter_dimension=0, tiled=True).astype(F32)
    grad_x = dh + norm_back(dn1, xhat1, inverse1, first_norm_gain)

    proj_sums = jnp.sum(dproj.astype(F32), 0).reshape(heads, 3, HD)
    own = jnp.concatenate([jnp.stack([proj_sums[:, 0], proj_sums[:, 2]], 1).reshape(-1),
                           jnp.sum(dbefore.astype(F32), 0)])
    common = jnp.concatenate([jnp.sum(v, 0) for v in
                              (dh, grad_share, dn1 * xhat1, dn1, dn2 * xhat2, dn2)])
    sums, owned = small_sum(common, own)
    sums = sums.reshape(6, width)
    qv = heads * 2 * HD
    return (result, grad_x, grads_attn, owned[:, :qv].reshape(-1), grads_proj, sums[0], grads_expand,
            owned[:, qv:].reshape(-1), grads_reduce, sums[1], sums[2], sums[3], sums[4], sums[5])


def solution(mesh):
    rows, both, flat = P("grp", None), P("grp", "tp"), P()
    in_specs = (rows, rows, flat, flat, both, flat, both, flat, both, flat, both, flat, flat, flat, flat, flat)
    spread = P(("grp", "tp"), None)
    out_specs = (spread, spread, both, flat, both, flat, both, flat, both, flat, flat, flat, flat, flat)
    return jax.shard_map(on_device, mesh=mesh, in_specs=in_specs, out_specs=out_specs, check_vma=False)
```

time: 1350 us -> 1010 us (0.75)
  waiting for transfers between devices: 885 us -> 654 us
  other arithmetic: 157 us -> 64 us
  matrix products: 229 us -> 141 us
  blocking collectives: 0 us -> 57.9 us
  Pallas kernels: 0 us -> 55.2 us
  local copies, waits for them, and re-layouts: 45.5 us -> 13.8 us
  loops' own time: 14.3 us -> 0 us
    psum x4 -> x0, waiting for transfers between devices: 791 us -> none  [the longest x1 325 us: on_device(): lax.psum(contract(active, w_reduce, 1, 1).astype(jnp.bfloat16), 'tp')]
    reduce_scatter x4 -> x7, waiting for transfers between devices: 0.03 us -> 383 us  [the longest x1 90.1 us: on_device(): lax.psum_scatter(dg(dproj, w_attn, 1, 1).astype(BF), 'tp', scatter_dimens...]
    all_gather x4 -> x7, waiting for transfers between devices: 93.4 us -> 244 us  [the longest x1 84.1 us: on_device(): n2 = lax.all_gather(n2_share.astype(BF), 'tp', axis=0, tiled=True)]
    dot_general x40 -> x12, matrix products: 229 us -> 141 us  [the longest x8 91.7 us: dg(): lax.dot_general(a, b, (((ca,), (cb,)), ((), ())), preferred_element_type=...]
    all_to_all x0 -> x1, blocking collectives: none -> 57.9 us  [on_device(): dcontext = lax.all_to_all(dcontext_rows, 'tp', 1, 0, tiled=True)]
    pallas_call x0 -> x3, Pallas kernels: none -> 55.2 us  [the longest x1 21.6 us: attn_bwd(): pl.pallas_call(functools.partial(attn_bwd_kernel, nb=nb), grid_spec=pltpu...]
    reduce_sum x16 -> x12, other arithmetic: 68.8 us -> 25.1 us  [the longest x3 9.18 us: on_device(): jnp.sum(v, 0)]
    mul x2 -> x1, other arithmetic: 30.9 us -> 0.01 us  [on_device(): starts = jnp.arange(nb, dtype=jnp.int32) * BLK]
  transfers between devices with their start and end apart: 12 -> 15, of which waited for: 7 -> 14; matrix products, arithmetic and copies ran while one was open for 24% -> 16% of each run, Pallas kernels for 0% -> 4%
where the time goes in v1:
time: 1010 us
  waiting for transfers between devices  654 us (65%)
  matrix products  141 us (14%)
  other arithmetic  64 us (6%)
  blocking collectives  57.9 us (6%)
  Pallas kernels  55.2 us (5%)
  between operations  14.9 us (1%)
  local copies, waits for them, and re-layouts  13.8 us (1%)
    dot_general x8, matrix products, dg(): lax.dot_general(a, b, (((ca,), (cb,)), ((), ())), preferred_element_type=...  91.7 us
    reduce_scatter x1, waiting for transfers between devices, on_device(): lax.psum_scatter(dg(dproj, w_attn, 1, 1).astype(BF), 'tp', scatter_dimens...  90.1 us
    reduce_scatter x1, waiting for transfers between devices, on_device(): lax.psum_scatter(dg(active, w_reduce, 1, 1).astype(BF), 'tp', scatter_dim...  88.1 us
    all_gather x1, waiting for transfers between devices, on_device(): n2 = lax.all_gather(n2_share.astype(BF), 'tp', axis=0, tiled=True)  84.1 us
    reduce_scatter x1, waiting for transfers between devices, on_device(): lax.psum_scatter(dg(dbefore, w_expand, 1, 1).astype(BF), 'tp', scatter_di...  70.9 us
    all_to_all x1, blocking collectives, on_device(): dcontext = lax.all_to_all(dcontext_rows, 'tp', 1, 0, tiled=True)  57.9 us
    reduce_scatter x1, waiting for transfers between devices, on_device(): grads_reduce = scatter(dg(gradb, active, 0, 0).astype(BF)).astype(F32)  53.2 us
    reduce_scatter x1, waiting for transfers between devices, on_device(): grads_attn = scatter(dg(n1, dproj, 0, 0).astype(BF)).astype(F32)  43.5 us
  transfers between devices with their start and end apart: 15, of which 14 were waited for; matrix products, arithmetic and copies ran while one was open for 16% of the time, Pallas kernels for 4%

profile of v1, /device:TPU:0, one launch (start us, length us, event | category | flops | bytes accessed | tf_op | source)
XLA Modules:
  0.0 1006.7 jit_solution(4917280767371618470)
XLA Ops:
  11.7 32.1 %all-gather.10.cloned.1.call-done = bf16[512,2048]{1,0:T(8,128)(2,1)} async-done(((bf16[512,256]{1,0:T(8,128)(2,1)}), bf16[512,2048]{1,0:T(8,128)(2,1)}) %all-gather.10.cloned.1.call-update) | async-done | bytes 2097168 | tf_op jit(solution)/shard_map/all_gather | solution.py:202
  51.8 6.4 fusion.2
  63.9 25.4 %all-gather.8.cloned.1.call-done = bf16[2048,768]{1,0:T(8,128)(2,1)} async-done(((bf16[512,768]{1,0:T(8,128)(2,1)}), bf16[2048,768]{1,0:T(8,128)(2,1)}) %all-gather.8.cloned.1.call-update) | async-done | bytes 3145744 | tf_op jit(solution)/shard_map/all_gather | solution.py:201
  89.3 10.0 add_convert_fusion.q_ref.k_ref.v_ref
  99.3 16.4 %attn_fwd.1 = (bf16[2048,256]{1,0:T(8,128)(2,1)S(1)}, f32[2,1,2048]{2,1,0:T(1,128)S(1)}) custom-call(s32[3,4]{1,0:T(4,128)S(1)} %pad_add_fusion.info, bf16[2048,768]{1,0:T(8,128)(2,1)S(1)} %add_convert_fusion.q_ref.k_ref.v_ref, bf16[2048,768]{1,0:T(8,128)(2,1)S(1)} %add_convert_fusion.q_ref.k_ref.v_ref, bf16[2048,768]{1,0:T(8,128)(2,1)S(1)} %add_convert_fusion.q_ref.k_ref.v_ref), custom_call_target="tpu_custom_call" | custom-call | flops 2147483648 | bytes 4194304 | tf_op jit(solution)/shard_map/attn_fwd/pallas_call | solution.py:53
  123.4 26.5 %all-to-all-done = bf16[8,256,256]{1,2,0:T(8,128)(2,1)S(1)} async-done(((bf16[8,256,256]{1,2,0:T(8,128)(2,1)}), bf16[8,256,256]{1,2,0:T(8,128)(2,1)S(1)}, u32[]{:S(2)}, u32[]{:S(2)}) %all-to-all-start) | async-done | bytes 1048608 | tf_op jit(solution)/shard_map/all_to_all | solution.py:236
  149.9 28.8 %all-gather.12.cloned.1.call-done = bf16[2048,2048]{1,0:T(8,128)(2,1)} async-done(((bf16[512,2048]{1,0:T(8,128)(2,1)}), bf16[2048,2048]{1,0:T(8,128)(2,1)}) %all-gather.12.cloned.1.call-update) | async-done | bytes 8388624 | tf_op jit(solution)/shard_map/all_gather | solution.py:203
  178.8 6.5 fusion.37
  191.8 7.2 broadcast_select_fusion
  199.0 34.7 %all-gather.16.cloned.1.call-done = bf16[2048,1024]{1,0:T(8,128)(2,1)} async-done(((bf16[512,1024]{1,0:T(8,128)(2,1)}), bf16[2048,1024]{1,0:T(8,128)(2,1)}) %all-gather.16.cloned.1.call-update) | async-done | bytes 4194320 | tf_op jit(solution)/shard_map/all_gather | solution.py:204
  233.8 84.1 %all-gather.14.cloned.1.call-done = bf16[2048,2048]{1,0:T(8,128)(2,1)} async-done(((bf16[256,2048]{1,0:T(8,128)(2,1)}), bf16[2048,2048]{1,0:T(8,128)(2,1)}) %all-gather.14.cloned.1.call-update) | async-done | bytes 8388624 | tf_op jit(solution)/shard_map/all_gather | solution.py:239
  317.9 14.4 %fusion.38 = f32[2048,1024]{1,0:T(8,128)} fusion(bf16[2048,2048]{1,0:T(8,128)(2,1)} %all-gather.14.cloned.1.call-done, bf16[2048,1024]{1,0:T(8,128)(2,1)} %all-gather.16.cloned.1.call-done), kind=kOutput, calls=%fused_computation.123 | convolution fusion | flops 8589934592 | bytes 20971520 | tf_op jit(solution)/shard_map/dot_general | solution.py:242
  332.3 39.1 %all-gather.18.cloned.1.call-done = bf16[2048,1024]{1,0:T(8,128)(2,1)} async-done(((bf16[512,1024]{1,0:T(8,128)(2,1)}), bf16[2048,1024]{1,0:T(8,128)(2,1)}) %all-gather.18.cloned.1.call-update) | async-done | bytes 4194320 | tf_op jit(solution)/shard_map/all_gather | solution.py:205
  371.4 18.6 %convert_reduce_fusion.1 = (f32[1024]{0:T(1024)S(1)}, bf16[2048,1024]{1,0:T(8,128)(2,1)S(1)}) fusion(f32[2048,1024]{1,0:T(8,128)} %fusion.38, f32[1024]{0:T(1024)S(1)} %dynamic_slice.14, bf16[2048,2048]{1,0:T(8,128)(2,1)} %broadcast_select_fusion, bf16[2048,1024]{1,0:T(8,128)(2,1)} %all-gather.18.cloned.1.call-done), kind=kOutput, calls=%fused_computation.17 | convolution fusion | flops 8638168064 | bytes 25174016 | tf_op jit(solution)/shard_map/dot_general | solution.py:247
  392.0 10.9 %convolution_convert_fusion.1 = bf16[2048,2048]{1,0:T(8,128)(2,1)} fusion(bf16[2048,1024]{1,0:T(8,128)(2,1)S(1)} %get-tuple-element.33, bf16[2048,1024]{1,0:T(8,128)(2,1)S(1)} %copy-done.21), kind=kOutput, calls=%fused_computation.21 | convolution fusion | flops 8594128896 | bytes 16777216 | tf_op jit(solution)/shard_map/dot_general | solution.py:17
  402.9 18.1 %convolution_convert_fusion.2 = bf16[2048,2048]{1,0:T(8,128)(2,1)} fusion(bf16[2048,1024]{1,0:T(8,128)(2,1)} %all-gather.18.cloned.1.call-done, f32[2048,1024]{1,0:T(8,128)} %fusion.38, f32[1024]{0:T(1024)S(1)} %dynamic_slice.14), kind=kOutput, calls=%fused_computation.22 | convolution fusion | flops 8615100416 | bytes 20975616 | tf_op jit(solution)/shard_map/dot_general | solution.py:17
  421.7 70.9 %reduce-scatter.10.cloned.1.call-done = bf16[256,2048]{1,0:T(8,128)(2,1)} async-done(((bf16[2048,2048]{1,0:T(8,128)(2,1)}), bf16[256,2048]{1,0:T(8,128)(2,1)}) %reduce-scatter.10.cloned.1.call-update) | async-done | bytes 1048592 | tf_op jit(solution)/shard_map/reduce_scatter | solution.py:249
  494.9 88.1 %reduce-scatter.8.cloned.1.call-done = bf16[256,2048]{1,0:T(8,128)(2,1)} async-done(((bf16[2048,2048]{1,0:T(8,128)(2,1)}), bf16[256,2048]{1,0:T(8,128)(2,1)}) %reduce-scatter.8.cloned.1.call-update) | async-done | bytes 1048592 | tf_op jit(solution)/shard_map/reduce_scatter | solution.py:256
  589.8 14.2 %convolution_convert_fusion.4 = bf16[2048,1024]{1,0:T(8,128)(2,1)} fusion(bf16[2048,2048]{1,0:T(8,128)(2,1)} %all-gather.14.cloned.1.call-done, bf16[2048,1024]{1,0:T(8,128)(2,1)} %copy-done.23), kind=kOutput, calls=%fused_computation.26 | convolution fusion | flops 8592031744 | bytes 16777216 | tf_op jit(solution)/shard_map/dot_general | solution.py:17
  604.1 15.7 %convolution_convert_fusion.3 = bf16[2048,1024]{1,0:T(8,128)(2,1)} fusion(bf16[2048,2048]{1,0:T(8,128)(2,1)} %broadcast_select_fusion, f32[2048,1024]{1,0:T(8,128)} %fusion.38, f32[1024]{0:T(1024)S(1)} %dynamic_slice.14), kind=kOutput, calls=%fused_computation.25 | convolution fusion | flops 8613003264 | bytes 20975616 | tf_op jit(solution)/shard_map/dot_general | solution.py:17
  619.9 6.3 convolution_convert_fusion.7
  626.2 57.9 %all_to_all.38 = bf16[256,8,256]{2,0,1:T(8,128)(2,1)S(1)} all-to-all(bf16[256,8,256]{2,0,1:T(8,128)(2,1)S(1)} %bitcast.71), channel_id=1, replica_groups=mesh['grp'=4,'tp'=8] {'tp'}, dimensions={1} | all-to-all | bytes 2097152 | tf_op jit(solution)/shard_map/all_to_all | solution.py:254
  684.2 21.6 %attn_bwd.1 = bf16[2048,768]{1,0:T(8,128)(2,1)S(1)} custom-call(s32[3,4]{1,0:T(4,128)S(1)} %copy-done.7, bf16[2048,768]{1,0:T(8,128)(2,1)S(1)} %copy-done.1, bf16[2048,768]{1,0:T(8,128)(2,1)S(1)} %copy-done.1, bf16[2048,768]{1,0:T(8,128)(2,1)S(1)} %copy-done.1, bf16[2048,256]{1,0:T(8,128)(2,1)S(1)} %copy-done.5, bf16[2048,256]{1,0:T(8,128)(2,1)S(1)} %bitcast.66, ...), custom_call_target="tpu_custom_call" | custom-call | flops 5368709120 | bytes 8388608 | tf_op jit(solution)/shard_map/attn_bwd/pallas_call | solution.py:103
  707.4 8.2 convolution_convert_fusion.5
  715.9 7.4 convolution_convert_fusion.6
  723.4 10.8 %convolution_convert_fusion = bf16[2048,2048]{1,0:T(8,128)(2,1)} fusion(bf16[2048,768]{1,0:T(8,128)(2,1)S(1)} %copy-done.3, bf16[2048,768]{1,0:T(8,128)(2,1)} %all-gather.8.cloned.1.call-done), kind=kOutput, calls=%fused_computation.20 | convolution fusion | flops 6446645248 | bytes 14680064 | tf_op jit(solution)/shard_map/dot_general | solution.py:17
  737.4 9.2 reduce-scatter.18.cloned.1.call-done
  749.3 53.2 %reduce-scatter.20.cloned.1.call-done = bf16[512,1024]{1,0:T(8,128)(2,1)} async-done(((bf16[2048,1024]{1,0:T(8,128)(2,1)}), bf16[512,1024]{1,0:T(8,128)(2,1)}) %reduce-scatter.20.cloned.1.call-update) | async-done | bytes 1048592 | tf_op jit(solution)/shard_map/reduce_scatter | solution.py:259
  805.9 43.5 %reduce-scatter.14.cloned.1.call-done = bf16[512,768]{1,0:T(8,128)(2,1)} async-done(((bf16[2048,768]{1,0:T(8,128)(2,1)}), bf16[512,768]{1,0:T(8,128)(2,1)}) %reduce-scatter.14.cloned.1.call-update) | async-done | bytes 786448 | tf_op jit(solution)/shard_map/reduce_scatter | solution.py:265
  851.7 28.2 %reduce-scatter.16.cloned.1.call-done = bf16[512,256]{1,0:T(8,128)(2,1)} async-done(((bf16[2048,256]{1,0:T(8,128)(2,1)}), bf16[512,256]{1,0:T(8,128)(2,1)}) %reduce-scatter.16.cloned.1.call-update) | async-done | bytes 262160 | tf_op jit(solution)/shard_map/reduce_scatter | solution.py:262
  881.8 90.1 %reduce-scatter.12.cloned.1.call-done = bf16[256,2048]{1,0:T(8,128)(2,1)} async-done(((bf16[2048,2048]{1,0:T(8,128)(2,1)}), bf16[256,2048]{1,0:T(8,128)(2,1)}) %reduce-scatter.12.cloned.1.call-update) | async-done | bytes 1048592 | tf_op jit(solution)/shard_map/reduce_scatter | solution.py:266
  975.2 17.3 %small_sum.1 = (f32[96,128]{1,0:T(8,128)}, f32[8,16,128]{2,1,0:T(8,128)}) custom-call(f32[112,128]{1,0:T(8,128)} %bitcast.76), custom_call_target="tpu_custom_call" | custom-call | tf_op jit(solution)/shard_map/small_sum/pallas_call | solution.py:163
  (152 shorter events, 70.1 us)
Async XLA Ops:
  7.2 36.7 %copy-start.10 = (f32[512,1024]{1,0:T(8,128)S(1)}, f32[512,1024]{1,0:T(8,128)}, u32[]{:S(2)}) copy-start(f32[512,1024]{1,0:T(8,128)} %param.24) | copy-start | bytes 6291460
  7.2 37.8 %copy-start.20 = (s32[6]{0:T(128)S(1)}, s32[6]{0:T(128)}, u32[]{:S(2)}) copy-start(s32[6]{0:T(128)} %param.18) | copy-start | bytes 76
  7.2 37.8 %copy-start.19 = (s32[6]{0:T(128)S(1)}, s32[6]{0:T(128)}, u32[]{:S(2)}) copy-start(s32[6]{0:T(128)} %param.19) | copy-start | bytes 76
  7.2 36.6 %all-gather.10.cloned.1.call-start = ((), (), s32[]{:S(2)}) async-start(), calls=%async_computation.10 | async-start | bytes 2359296 | tf_op jit(solution)/shard_map/all_gather | solution.py:202
  9.2 80.1 %all-gather.8.cloned.1.call-start = ((), (), s32[]{:S(2)}) async-start(), calls=%async_computation.9 | async-start | bytes 3932160 | tf_op jit(solution)/shard_map/all_gather | solution.py:201
  11.6 167.1 %all-gather.12.cloned.1.call-start = ((), (), s32[]{:S(2)}) async-start(), calls=%async_computation.11 | async-start | bytes 10485760 | tf_op jit(solution)/shard_map/all_gather | solution.py:203
  43.8 190.0 %all-gather.16.cloned.1.call-start = ((), (), s32[]{:S(2)}) async-start(), calls=%async_computation.13 | async-start | bytes 5242880 | tf_op jit(solution)/shard_map/all_gather | solution.py:204
  47.1 11.1 %slice-start = ((s8[8388608]{0:T(1024)(128)(4,1)}), s8[4194304]{0:T(1024)(128)(4,1)S(1)}, s32[]{:S(2)}) async-start(s8[8388608]{0:T(1024)(128)(4,1)} %bitcast.67), calls=%async_computation.23 | async-start | bytes 8388608
  58.2 41.1 %copy-start.6 = (s32[3,4]{1,0:T(4,128)}, s32[3,4]{1,0:T(4,128)S(1)}, u32[]{:S(2)}) copy-start(s32[3,4]{1,0:T(4,128)S(1)} %pad_add_fusion.info) | copy-start | bytes 148
  99.3 79.5 %copy-start.22 = (f32[2048]{0:T(1024)S(1)}, f32[2048]{0:T(1024)}, u32[]{:S(2)}) copy-start(f32[2048]{0:T(1024)} %param.23) | copy-start | bytes 24580
  117.4 67.8 %copy-start.4 = (bf16[2048,256]{1,0:T(8,128)(2,1)}, bf16[2048,256]{1,0:T(8,128)(2,1)S(1)}, u32[]{:S(2)}) copy-start(bf16[2048,256]{1,0:T(8,128)(2,1)S(1)} %get-tuple-element.18.o_ref) | copy-start | bytes 3145732
  118.7 31.2 %all-to-all-start = ((bf16[8,256,256]{1,2,0:T(8,128)(2,1)}), bf16[8,256,256]{1,2,0:T(8,128)(2,1)S(1)}, u32[]{:S(2)}, u32[]{:S(2)}) async-start(bf16[8,256,256]{1,2,0:T(8,128)(2,1)} %copy.33), calls=%async_computation | async-start | bytes 2097152 | tf_op jit(solution)/shard_map/all_to_all | solution.py:236
  123.3 194.6 %all-gather.14.cloned.1.call-start = ((), (), s32[]{:S(2)}) async-start(), calls=%async_computation.12 | async-start | bytes 9437184 | tf_op jit(solution)/shard_map/all_gather | solution.py:239
  149.9 28.8 %copy-start.11 = (bf16[8,256,256]{1,2,0:T(8,128)(2,1)}, bf16[8,256,256]{1,2,0:T(8,128)(2,1)S(1)}, u32[]{:S(2)}) copy-start(bf16[8,256,256]{1,2,0:T(8,128)(2,1)S(1)} %all-to-all-done) | copy-start | bytes 3145732
  187.1 184.3 %all-gather.18.cloned.1.call-start = ((), (), s32[]{:S(2)}) async-start(), calls=%async_computation.14 | async-start | bytes 5242880 | tf_op jit(solution)/shard_map/all_gather | solution.py:205
  190.4 302.3 %reduce-scatter.10.cloned.1.call-start = ((), (), s32[]{:S(2)}) async-start(), calls=%async_computation.16 | async-start | bytes 9437184 | tf_op jit(solution)/shard_map/reduce_scatter | solution.py:249
  371.4 20.6 %copy-start.21 = (bf16[2048,1024]{1,0:T(8,128)(2,1)S(1)}, bf16[2048,1024]{1,0:T(8,128)(2,1)}, u32[]{:S(2)}) copy-start(bf16[2048,1024]{1,0:T(8,128)(2,1)} %all-gather.16.cloned.1.call-done) | copy-start | bytes 12582916
  402.9 180.0 %reduce-scatter.8.cloned.1.call-start = ((), (), s32[]{:S(2)}) async-start(), calls=%async_computation.15 | async-start | bytes 9437184 | tf_op jit(solution)/shard_map/reduce_scatter | solution.py:256
  421.0 161.9 %copy-start.18 = (f32[2048]{0:T(1024)S(1)}, f32[2048]{0:T(1024)}, u32[]{:S(2)}) copy-start(f32[2048]{0:T(1024)} %param.27) | copy-start | bytes 24580
  421.0 294.9 %all-gather.20.cloned.1.call-start = ((), (), s32[]{:S(2)}) async-start(), calls=%async_computation.19 | async-start | bytes 9437184 | tf_op jit(solution)/shard_map/all_gather | solution.py:261
  589.8 156.7 %reduce-scatter.18.cloned.1.call-start = ((), (), s32[]{:S(2)}) async-start(), calls=%async_computation.21 | async-start | bytes 5242880 | tf_op jit(solution)/shard_map/reduce_scatter | solution.py:260
  604.1 198.5 %reduce-scatter.20.cloned.1.call-start = ((), (), s32[]{:S(2)}) async-start(), calls=%async_computation.22 | async-start | bytes 5242880 | tf_op jit(solution)/shard_map/reduce_scatter | solution.py:259
  619.8 64.4 %copy-start.1 = (bf16[2048,768]{1,0:T(8,128)(2,1)S(1)}, bf16[2048,768]{1,0:T(8,128)(2,1)}, u32[]{:S(2)}) copy-start(bf16[2048,768]{1,0:T(8,128)(2,1)} %copy-done) | copy-start | bytes 9437188
  619.8 64.3 %copy-start.7 = (s32[3,4]{1,0:T(4,128)S(1)}, s32[3,4]{1,0:T(4,128)}, u32[]{:S(2)}) copy-start(s32[3,4]{1,0:T(4,128)} %copy-done.6) | copy-start | bytes 148
  619.8 229.5 %reduce-scatter.14.cloned.1.call-start = ((), (), s32[]{:S(2)}) async-start(), calls=%async_computation.18 | async-start | bytes 3932160 | tf_op jit(solution)/shard_map/reduce_scatter | solution.py:265
  619.9 64.3 %copy-start.5 = (bf16[2048,256]{1,0:T(8,128)(2,1)S(1)}, bf16[2048,256]{1,0:T(8,128)(2,1)}, u32[]{:S(2)}) copy-start(bf16[2048,256]{1,0:T(8,128)(2,1)} %copy-done.4) | copy-start | bytes 3145732
  619.9 87.5 %slice-start.2 = ((s8[8388608]{0:T(1024)(128)(4,1)}), s8[4194304]{0:T(1024)(128)(4,1)S(1)}, s32[]{:S(2)}) async-start(s8[8388608]{0:T(1024)(128)(4,1)} %bitcast.69), calls=%async_computation.25 | async-start | bytes 8388608
  626.1 81.2 %slice-start.3 = ((s8[8388608]{0:T(1024)(128)(4,1)}), s8[4194304]{0:T(1024)(128)(4,1)S(1)}, s32[]{:S(2)}) async-start(s8[8388608]{0:T(1024)(128)(4,1)} %bitcast.69), calls=%async_computation.26 | async-start | bytes 8388608
  715.6 164.4 %reduce-scatter.16.cloned.1.call-start = ((), (), s32[]{:S(2)}) async-start(), calls=%async_computation.20 | async-start | bytes 1310720 | tf_op jit(solution)/shard_map/reduce_scatter | solution.py:262
  723.3 248.5 %reduce-scatter.12.cloned.1.call-start = ((), (), s32[]{:S(2)}) async-start(), calls=%async_computation.17 | async-start | bytes 9437184 | tf_op jit(solution)/shard_map/reduce_scatter | solution.py:266
  737.3 234.5 %copy-start.14 = (f32[2048]{0:T(1024)S(1)}, f32[2048]{0:T(1024)}, u32[]{:S(2)}) copy-start(f32[2048]{0:T(1024)} %param.28) | copy-start | bytes 24580
  805.8 190.2 %copy-start.9 = (f32[256,2048]{1,0:T(8,128)S(1)}, f32[256,2048]{1,0:T(8,128)}, u32[]{:S(2)}) copy-start(f32[256,2048]{1,0:T(8,128)} %copy-done.8) | copy-start | bytes 6291460
  (11 other events, 48.1 us)
Sparse Core Ops, SparseCore 0:
  10.2 33.5 all-gather.9
  46.2 43.0 all-gather.7
  91.1 87.5 all-gather.11
  181.0 52.6 all-gather.15
  235.8 82.0 all-gather.13
  320.2 51.2 all-gather.17
  403.0 89.5 reduce-scatter.9
  494.9 87.9 reduce-scatter.7
  589.9 102.6 all-gather.19
  695.4 51.0 reduce-scatter.17
  749.8 52.6 reduce-scatter.19
  805.4 43.9 reduce-scatter.13
  852.2 27.6 reduce-scatter.15
  882.2 89.5 reduce-scatter.11

commit v2 on v1

--- a/solution.py
+++ b/solution.py
@@ -110,7 +110,455 @@
         cost_estimate=pl.CostEstimate(flops=heads*length*length*HD*5, bytes_accessed=length*heads*HD*16, transcendentals=heads*length*length//2),
     )(info, proj, proj, proj, ctx, dctx, lse)
 
+
 MESH = pl.DeviceIdType.MESH
+TILE = 256
+
+
+class Place:
+    def __init__(self, n_tp):
+        self.g = lax.axis_index("grp")
+        t = lax.axis_index("tp")
+        self.t, self.n, self.Z = t, n_tp, n_tp // 2
+        self.z, self.k = t // 2, lax.rem(t, 2)
+        self.right, self.left, self.sib = (self.g, t + 2), (self.g, t - 2), (self.g, t + 1 - 2 * self.k)
+        self.has_right, self.has_left = self.z < self.Z - 1, self.z > 0
+
+    def barrier(self):
+        bar = pltpu.get_barrier_semaphore()
+        pl.semaphore_signal(bar, inc=1, device_id=self.sib, device_id_type=MESH)
+
+        @pl.when(self.has_right)
+        def _():
+            pl.semaphore_signal(bar, inc=1, device_id=self.right, device_id_type=MESH)
+
+        @pl.when(self.has_left)
+        def _():
+            pl.semaphore_signal(bar, inc=1, device_id=self.left, device_id_type=MESH)
+
+        amount = 1 + jnp.where(self.has_right, 1, 0) + jnp.where(self.has_left, 1, 0)
+        pl.semaphore_wait(bar, amount)
+
+
+def remote(src, dst, ssem, rsem, device):
+    return pltpu.make_async_remote_copy(src, dst, ssem, rsem, device_id=device, device_id_type=MESH)
+
+
+class Gather:
+    def __init__(self, at, gat, rows, ls, lr, ss, sr):
+        self.at, self.gat, self.rows = at, gat, rows
+        self.ls, self.lr, self.ss, self.sr = ls, lr, ss, sr
+
+    def block(self, zz, kk, c):
+        return self.gat.at[2 * zz + kk, pl.ds(pl.multiple_of(c * self.rows, self.rows), self.rows), :]
+
+    def line(self, c, side, d):
+        at = self.at
+        sign, device = (-1, at.right) if side == 0 else (1, at.left)
+        b = self.block(at.z + sign * (d - 1), at.k, c)
+        return remote(b, b, self.ls.at[c, side, d - 1], self.lr.at[c, side, d - 1], device)
+
+    def line_in(self, c, side, d):
+        at = self.at
+        sign, device = (-1, at.right) if side == 0 else (1, at.left)
+        b = self.block(at.z + sign * d, at.k, c)
+        return remote(b, b, self.ls.at[c, side, d - 1], self.lr.at[c, side, d - 1], device)
+
+    def across(self, c, zz):
+        b = self.block(zz, self.at.k, c)
+        return remote(b, b, self.ss.at[c, zz], self.sr.at[c, zz], self.at.sib)
+
+    def across_in(self, c, zz):
+        b = self.block(zz, 1 - self.at.k, c)
+        return remote(b, b, self.ss.at[c, zz], self.sr.at[c, zz], self.at.sib)
+
+    def start(self, c):
+        at = self.at
+
+        @pl.when(at.has_right)
+        def _():
+            self.line(c, 0, 1).start()
+
+        @pl.when(at.has_left)
+        def _():
+            self.line(c, 1, 1).start()
+
+        self.across(c, at.z).start()
+
+    def hop(self, c, d):
+        at = self.at
+
+        @pl.when(at.z >= d)
+        def _():
+            self.line_in(c, 0, d).wait_recv()
+            if d < at.Z - 1:
+                @pl.when(at.has_right)
+                def _():
+                    self.line(c, 0, d + 1).start()
+            self.across(c, at.z - d).start()
+
+        @pl.when(at.z + d <= at.Z - 1)
+        def _():
+            self.line_in(c, 1, d).wait_recv()
+            if d < at.Z - 1:
+                @pl.when(at.has_left)
+                def _():
+                    self.line(c, 1, d + 1).start()
+            self.across(c, at.z + d).start()
+
+    def finish(self, c):
+        at = self.at
+        for zz in range(at.Z):
+            self.across_in(c, zz).wait_recv()
+            self.across(c, zz).wait_send()
+        for d in range(1, at.Z):
+            @pl.when(at.has_right & (at.z >= d - 1))
+            def _():
+                self.line(c, 0, d).wait_send()
+
+            @pl.when(at.has_left & (at.z + d - 1 <= at.Z - 1))
+            def _():
+                self.line(c, 1, d).wait_send()
+
+
+class Scatter:
+    def __init__(self, at, parts, pair, hops, cs, cr, hs, hr):
+        self.at, self.parts, self.pair, self.hops = at, parts, pair, hops
+        self.cs, self.cr, self.hs, self.hr = cs, cr, hs, hr
+
+    def across(self, c):
+        return remote(self.parts.at[:, 1 - self.at.k], self.pair.at[c], self.cs.at[c], self.cr.at[c], self.at.sib)
+
+    def line(self, c, side, h, target):
+        device = self.at.right if side == 0 else self.at.left
+        return remote(self.pair.at[c, target], self.hops.at[side, c, h - 1],
+                      self.hs.at[c, side, h - 1], self.hr.at[c, side, h - 1], device)
+
+    def start(self, c):
+        self.across(c).start()
+
+    def meet(self, c):
+        self.across(c).wait()
+        own = self.parts[:, pl.ds(self.at.k, 1)]
+        own = own.reshape(own.shape[0], own.shape[2], own.shape[3])
+        self.pair[c] = (self.pair[c].astype(F32) + own.astype(F32)).astype(BF)
+
+    def hop(self, c, h):
+        at = self.at
+        for side in (0, 1):
+            pos = at.z if side == 0 else at.Z - 1 - at.z
+            target = at.z + at.Z - h if side == 0 else at.z - at.Z + h
+
+            @pl.when((pos <= h - 1) & (pos < at.Z - 1))
+            def _():
+                if h >= 2:
+                    @pl.when(pos >= 1)
+                    def _():
+                        self.line(c, side, h - 1, target).wait_recv()
+                        self.pair[c, target] = (self.pair[c, target].astype(F32)
+                                                + self.hops[side, c, h - 2].astype(F32)).astype(BF)
+                self.line(c, side, h, target).start()
+
+    def finish(self, c, total):
+        at = self.at
+        total[...] = self.pair[c, at.z].astype(F32)
+        for side in (0, 1):
+            pos = at.z if side == 0 else at.Z - 1 - at.z
+
+            @pl.when(pos >= 1)
+            def _():
+                self.line(c, side, at.Z - 1, at.z).wait_recv()
+                total[...] += self.hops[side, c, at.Z - 2].astype(F32)
+
+            for h in range(1, at.Z):
+                @pl.when((pos <= h - 1) & (pos < at.Z - 1))
+                def _():
+                    self.line(c, side, h, at.z).wait_send()
+
+
+def gather_sems(chunks, Z):
+    dma = pltpu.SemaphoreType.DMA
+    return [dma((chunks, 2, Z - 1)), dma((chunks, 2, Z - 1)), dma((chunks, Z)), dma((chunks, Z))]
+
+
+def scatter_scratch(chunks, Z, rows, width):
+    dma = pltpu.SemaphoreType.DMA
+    return [pltpu.VMEM((Z, 2, rows, width), BF), pltpu.VMEM((chunks, Z, rows, width), BF),
+            pltpu.VMEM((2, chunks, Z - 1, rows, width), BF),
+            dma((chunks,)), dma((chunks,)), dma((chunks, 2, Z - 1)), dma((chunks, 2, Z - 1))]
+
+
+def inside(c, chunks):
+    return (c >= 0) & (c < chunks)
+
+
+def chunk_rows(c, rows):
+    return pl.ds(pl.multiple_of(c * rows, rows), rows)
+
+
+def tiles(count, body):
+    def step(i, carry):
+        body(i)
+        return carry
+    lax.fori_loop(0, count, step, 0)
+
+
+def cols(i, size=TILE):
+    return pl.ds(pl.multiple_of(i * size, size), size)
+
+
+def rows_stats(rows):
+    mean = jnp.mean(rows, -1, keepdims=True)
+    centred = rows - mean
+    inverse = lax.rsqrt(jnp.mean(centred * centred, -1, keepdims=True) + 1e-05)
+    return centred * inverse, inverse
+
+
+def out_kernel(ctx, w_out, x_share, vec, hidden, n2, *scratch, n, chunks, rows):
+    total, *sc = scratch
+    at = Place(n)
+    at.barrier()
+    rs = Scatter(at, *sc)
+    width = w_out.shape[0]
+
+    def product(c):
+        lhs = ctx[:, chunk_rows(c, rows), :].reshape(n * rows, ctx.shape[2])
+
+        def tile(i):
+            y = dg(lhs, w_out[cols(i), :], 1, 1)
+            rs.parts[:, :, :, cols(i)] = y.astype(BF).reshape(at.Z, 2, rows, TILE)
+        tiles(width // TILE, tile)
+        rs.start(c)
+
+    def tick(i, carry):
+        c = i - 1
+
+        @pl.when(inside(c, chunks))
+        def _():
+            rs.meet(c)
+            rs.hop(c, 1)
+
+        @pl.when(inside(i, chunks))
+        def _():
+            product(i)
+
+        @pl.when(inside(c, chunks))
+        def _():
+            for h in range(2, at.Z):
+                rs.hop(c, h)
+
+        e = i - 2
+
+        @pl.when(inside(e, chunks))
+        def _():
+            rs.finish(e, total)
+            r = chunk_rows(e, rows)
+            h = x_share[r, :].astype(F32) + total[...] + vec[0:1, :]
+            hidden[r, :] = h
+            n2[r, :] = (rows_stats(h)[0] * vec[1:2, :] + vec[2:3, :]).astype(BF)
+        return carry
+
+    lax.fori_loop(0, chunks + 2, tick, 0)
+
+
+def attn_out(ctx, w_out, x_share, vec, n, chunks):
+    length, hw = ctx.shape
+    share, width = x_share.shape
+    rows = share // chunks
+    vm = pl.BlockSpec(memory_space=pltpu.VMEM)
+    return pl.pallas_call(
+        functools.partial(out_kernel, n=n, chunks=chunks, rows=rows),
+        in_specs=[vm] * 4, out_specs=[vm] * 2,
+        out_shape=[jax.ShapeDtypeStruct((share, width), F32), jax.ShapeDtypeStruct((share, width), BF)],
+        scratch_shapes=[pltpu.VMEM((rows, width), F32)] + scatter_scratch(chunks, n // 2, rows, width),
+        compiler_params=pltpu.CompilerParams(collective_id=2, has_side_effects=True, vmem_limit_bytes=40 << 20),
+        cost_estimate=pl.CostEstimate(flops=2 * length * hw * width, bytes_accessed=1 << 23, transcendentals=0),
+        name="attn_out",
+    )(ctx.reshape(n, share, hw), w_out, x_share, vec)
+
+
+def ffn_kernel(n2_hbm, gradb_hbm, w_up, w_down, w_out, b_up, ctx, hidden, gshare, gain,
+               mlp_hbm, gwu_hbm, gwd_hbm, gwo, dctx, dh, stats, bsum,
+               gat, acc_up, acc_down, gbuf, mst, actb, dbb, total, lsem, gsem, msem, *scratch, n, chunks, rows):
+    at = Place(n)
+    s1, s2, sc = scratch[:4], scratch[4:8], scratch[8:]
+    ag1, ag2 = Gather(at, gat, rows, *s1), Gather(at, gat, rows, *s2)
+    rs = Scatter(at, *sc)
+    width, hid = w_up.shape
+    m = n * rows
+
+    load = pltpu.make_async_copy(n2_hbm, gat.at[at.t], lsem)
+    load.start()
+
+    def fetch(c):
+        slot = lax.rem(c, 2)
+        return pltpu.make_async_copy(gradb_hbm.at[:, chunk_rows(c, rows), :], gbuf.at[slot], gsem.at[slot])
+
+    def put_mlp(c):
+        return pltpu.make_async_copy(mst, mlp_hbm.at[:, chunk_rows(c, rows), :], msem)
+
+    fetch(0).start()
+    acc_up[...] = jnp.zeros_like(acc_up)
+    acc_down[...] = jnp.zeros_like(acc_down)
+    stats[...] = jnp.zeros_like(stats)
+    bsum[...] = jnp.zeros_like(bsum)
+    load.wait()
+    at.barrier()
+
+    a0, a1 = 0.7978845608028654, 0.044715
+
+    def wide(c):
+        return gat[:, chunk_rows(c, rows), :].reshape(m, width)
+
+    def forward(c):
+        fetch(c).wait()
+
+        @pl.when(c + 1 < chunks)
+        def _():
+            fetch(c + 1).start()
+        slot = lax.rem(c, 2)
+
+        def tile(i):
+            v = dg(wide(c), w_up[:, cols(i)], 1, 0) + b_up[:, cols(i)]
+            ga = dg(gbuf[slot].reshape(m, width), w_down[:, cols(i)], 1, 0)
+            v2 = v * v
+            th = jnp.tanh(a0 * (v + a1 * v2 * v))
+            half = 0.5 * (1.0 + th)
+            actb[:, cols(i)] = (v * half).astype(BF)
+            slope = half + 0.5 * v * (1.0 - th * th) * (a0 * (1.0 + 3.0 * a1 * v2))
+            db = (ga * slope).astype(BF)
+            dbb[:, cols(i)] = db
+            bsum[:, cols(i)] += jnp.sum(db.astype(F32), 0, keepdims=True)
+        tiles(hid // TILE, tile)
+
+    def back(c):
+        def tile(i):
+            y = dg(dbb[...], w_up[cols(i), :], 1, 1)
+            rs.parts[:, :, :, cols(i)] = y.astype(BF).reshape(at.Z, 2, rows, TILE)
+        tiles(width // TILE, tile)
+
+    def down(c):
+        @pl.when(c > 0)
+        def _():
+            put_mlp(c - 1).wait()
+
+        def tile(i):
+            y = dg(actb[...], w_down[cols(i), :], 1, 1)
+            mst[:, :, cols(i)] = y.astype(BF).reshape(n, rows, TILE)
+        tiles(width // TILE, tile)
+        put_mlp(c).start()
+
+    def weights(c):
+        slot = lax.rem(c, 2)
+
+        def tile(i):
+            x = gat[:, chunk_rows(c, rows), cols(i)].reshape(m, TILE)
+            acc_up[cols(i), :] += dg(x, dbb[...], 0, 0)
+            y = gbuf[slot, :, :, cols(i)].reshape(m, TILE)
+            acc_down[cols(i), :] += dg(y, actb[...], 0, 0)
+        tiles(width // TILE, tile)
+
+    def norm_grad(c):
+        r = chunk_rows(c, rows)
+        xhat, inverse = rows_stats(hidden[r, :])
+        dn2 = total[...]
+        e = dn2 * gain[...]
+        inner = jnp.mean(e, -1, keepdims=True) + xhat * jnp.mean(e * xhat, -1, keepdims=True)
+        d = gshare[r, :].astype(F32) + inverse * (e - inner)
+        dh[r, :] = d
+        gat[at.t, r, :] = d.astype(BF)
+        stats[0:1, :] += jnp.sum(dn2 * xhat, 0, keepdims=True)
+        stats[1:2, :] += jnp.sum(dn2, 0, keepdims=True)
+        stats[2:3, :] += jnp.sum(d, 0, keepdims=True)
+
+    def heads(c):
+        y = dg(wide(c), w_out[...], 1, 0)
+        dctx[:, chunk_rows(c, rows), :] = y.astype(BF).reshape(n, rows, y.shape[1])
+
+    def at_stage(c, fn):
+        @pl.when(inside(c, chunks))
+        def _():
+            fn(c)
+
+    def hops(i, h):
+        at_stage(i - 3, lambda c: rs.hop(c, h))
+        at_stage(i - 4, lambda c: ag2.hop(c, h))
+        at_stage(i - 1, lambda c: ag1.hop(c, h))
+
+    def tick(i, carry):
+        at_stage(i, ag1.start)
+        at_stage(i - 3, rs.meet)
+        hops(i, 1)
+        at_stage(i - 2, forward)
+        for h in range(2, at.Z):
+            hops(i, h)
+            if h == 2:
+                at_stage(i - 2, back)
+
+        def rest(c):
+            weights(c)
+            rs.start(c)
+            down(c)
+        at_stage(i - 2, rest)
+
+        def gathered(c):
+            ag2.finish(c)
+            heads(c)
+        at_stage(i - 4, gathered)
+
+        def reduced(c):
+            rs.finish(c, total)
+            norm_grad(c)
+            ag2.start(c)
+        at_stage(i - 3, reduced)
+        at_stage(i - 1, ag1.finish)
+        return carry
+
+    lax.fori_loop(0, chunks + 4, tick, 0)
+    put_mlp(chunks - 1).wait()
+
+    def final(i):
+        x = gat[:, :, cols(i)].reshape(-1, TILE)
+        gwo[cols(i), :] = dg(x, ctx[...], 0, 0).astype(BF)
+    tiles(width // TILE, final)
+
+    def store(i):
+        r = cols(i, m)
+        actb[...] = acc_up[r, :].astype(BF)
+        one = pltpu.make_async_copy(actb, gwu_hbm.at[r, :], lsem)
+        one.start()
+        dbb[...] = acc_down[r, :].astype(BF)
+        two = pltpu.make_async_copy(dbb, gwd_hbm.at[r, :], msem)
+        two.start()
+        one.wait()
+        two.wait()
+    tiles(width // m, store)
+
+
+def feed_forward(n2, gradb, w_up, w_down, w_out, b_up, ctx, hidden, gshare, gain, n, chunks):
+    length, width = gradb.shape
+    hid, hw = w_up.shape[1], w_out.shape[1]
+    share = length // n
+    rows = share // chunks
+    Z = n // 2
+    vm, hbm = pl.BlockSpec(memory_space=pltpu.VMEM), pl.BlockSpec(memory_space=pl.ANY)
+    S = jax.ShapeDtypeStruct
+    m = n * rows
+    return pl.pallas_call(
+        functools.partial(ffn_kernel, n=n, chunks=chunks, rows=rows),
+        in_specs=[hbm, hbm] + [vm] * 8,
+        out_specs=[hbm, hbm, hbm] + [vm] * 5,
+        out_shape=[S((n, share, width), BF), S((width, hid), BF), S((width, hid), BF), S((width, hw), BF),
+                   S((n, share, hw), BF), S((share, width), F32), S((8, width), F32), S((1, hid), F32)],
+        scratch_shapes=[pltpu.VMEM((n, share, width), BF), pltpu.VMEM((width, hid), F32), pltpu.VMEM((width, hid), F32),
+                        pltpu.VMEM((2, n, rows, width), BF), pltpu.VMEM((n, rows, width), BF),
+                        pltpu.VMEM((m, hid), BF), pltpu.VMEM((m, hid), BF), pltpu.VMEM((rows, width), F32),
+                        pltpu.SemaphoreType.DMA, pltpu.SemaphoreType.DMA((2,)), pltpu.SemaphoreType.DMA]
+                       + gather_sems(chunks, Z) + gather_sems(chunks, Z) + scatter_scratch(chunks, Z, rows, width),
+        compiler_params=pltpu.CompilerParams(collective_id=3, has_side_effects=True, vmem_limit_bytes=62 << 20),
+        cost_estimate=pl.CostEstimate(flops=12 * length * hid * width, bytes_accessed=1 << 26, transcendentals=0),
+        name="feed_forward",
+    )(n2, gradb.reshape(n, share, width), w_up, w_down, w_out, b_up, ctx, hidden, gshare, gain)
 
 
 def small_kernel(x_ref, a_ref, b_ref, gbuf, tbuf, gs, gr, ts, tr, *, n_grp, n_tp, a_rows):
@@ -199,8 +647,7 @@
     hidden_here = w_up.shape[1]
 
     w_attn = lax.all_gather(w_qkv.astype(BF), "grp", axis=0, tiled=True)
-    w_proj = lax.all_gather(w_out.astype(BF), "tp", axis=1, tiled=True)
-    w_proj = lax.all_gather(w_proj, "grp", axis=0, tiled=True)
+    w_proj = lax.all_gather(w_out.astype(BF), "grp", axis=0, tiled=True)
     w_expand = lax.all_gather(w_up.astype(BF), "grp", axis=0, tiled=True)
     w_reduce = lax.all_gather(w_down.astype(BF), "grp", axis=0, tiled=True)
 
@@ -225,7 +672,8 @@
 
     x = layer_input.astype(F32)
     n1 = normalize(x, first_norm_gain, first_norm_bias)[0].astype(BF)
-    x_share = mine(layer_input).astype(F32)
+    x_share_b = mine(layer_input)
+    x_share = x_share_b.astype(F32)
     _, xhat1, inverse1 = normalize(x_share, first_norm_gain, first_norm_bias)
 
     head_bias = lax.dynamic_slice_in_dim(b_qv.reshape(-1, 2, HD), tp * heads, heads, 0)
@@ -233,33 +681,22 @@
         [head_bias[:, 0], jnp.zeros_like(head_bias[:, 0]), head_bias[:, 1]], 1).reshape(-1)
     proj = (jnp.dot(n1, w_attn, preferred_element_type=F32) + bias_three).astype(BF)
     context, lse = attn_fwd(info, proj)
-    context_rows = lax.all_to_all(context, "tp", 0, 1, tiled=True)
-    hidden = x_share + dg(context_rows, w_proj, 1, 1) + b_out
-    n2_share, xhat2, inverse2 = normalize(hidden, second_norm_gain, second_norm_bias)
-    n2 = lax.all_gather(n2_share.astype(BF), "tp", axis=0, tiled=True)
-
-    up_bias = lax.dynamic_slice_in_dim(b_up, tp * hidden_here, hidden_here, 0)
-    before = jnp.dot(n2, w_expand, preferred_element_type=F32) + up_bias
-    act = functools.partial(jax.nn.gelu, approximate=True)
-    active, gelu_back = jax.vjp(act, before)
-    active = active.astype(BF)
+    vec = jnp.stack([b_out, second_norm_gain, second_norm_bias])
+    hidden, n2_share = attn_out(context, w_proj, x_share_b, vec, n_tp, 8)
+    up_bias = lax.dynamic_slice_in_dim(b_up, tp * hidden_here, hidden_here, 0)[None]
     gradb = jnp.where(live_all, out_cotangent, jnp.zeros_like(out_cotangent))
-    grad_active = jnp.dot(gradb, w_reduce, preferred_element_type=F32)
-    dbefore = gelu_back(grad_active)[0].astype(BF)
-    dn2 = lax.psum_scatter(dg(dbefore, w_expand, 1, 1).astype(BF), "tp", scatter_dimension=0, tiled=True).astype(F32)
-    grad_share = mine(gradb).astype(F32)
-    dh = grad_share + norm_back(dn2, xhat2, inverse2, second_norm_gain)
-    dhb = dh.astype(BF)
-    dcontext_rows = jnp.dot(dhb, w_proj, preferred_element_type=F32).astype(BF)
-    dcontext = lax.all_to_all(dcontext_rows, "tp", 1, 0, tiled=True)
-
-    mlp = lax.psum_scatter(dg(active, w_reduce, 1, 1).astype(BF), "tp", scatter_dimension=0, tiled=True).astype(F32)
+    gradb_share = mine(gradb)
+    grad_share = gradb_share.astype(F32)
+    (mlp_parts, gw_expand, gw_reduce, gw_proj, dcontext, dh, stats, up_sum) = feed_forward(
+        n2_share, gradb, w_expand, w_reduce, w_proj, up_bias, context, hidden, gradb_share,
+        second_norm_gain[None], n_tp, 8)
+    dcontext = dcontext.reshape(length, -1)
+    scatter = functools.partial(lax.psum_scatter, axis_name="grp", scatter_dimension=0, tiled=True)
+    grads_reduce = scatter(gw_reduce).astype(F32)
+    grads_expand = scatter(gw_expand).astype(F32)
+    grads_proj = scatter(gw_proj).astype(F32)
+    mlp = lax.psum_scatter(mlp_parts.reshape(length, width), "tp", scatter_dimension=0, tiled=True).astype(F32)
     result = (live * (hidden + mlp + b_down)).astype(BF)
-    scatter = functools.partial(lax.psum_scatter, axis_name="grp", scatter_dimension=0, tiled=True)
-    grads_reduce = scatter(dg(gradb, active, 0, 0).astype(BF)).astype(F32)
-    grads_expand = scatter(dg(n2, dbefore, 0, 0).astype(BF)).astype(F32)
-    dh_all = lax.all_gather(dhb, "tp", axis=0, tiled=True)
-    grads_proj = scatter(dg(dh_all, context, 0, 0).astype(BF)).astype(F32)
 
     dproj = attn_bwd(info, proj, context, dcontext, lse)
     grads_attn = scatter(dg(n1, dproj, 0, 0).astype(BF)).astype(F32)
@@ -268,9 +705,9 @@
 
     proj_sums = jnp.sum(dproj.astype(F32), 0).reshape(heads, 3, HD)
     own = jnp.concatenate([jnp.stack([proj_sums[:, 0], proj_sums[:, 2]], 1).reshape(-1),
-                           jnp.sum(dbefore.astype(F32), 0)])
-    common = jnp.concatenate([jnp.sum(v, 0) for v in
-                              (dh, grad_share, dn1 * xhat1, dn1, dn2 * xhat2, dn2)])
+                           up_sum[0]])
+    common = jnp.concatenate([stats[2]] + [jnp.sum(v, 0) for v in (grad_share, dn1 * xhat1, dn1)]
+                             + [stats[0], stats[1]])
     sums, owned = small_sum(common, own)
     sums = sums.reshape(6, width)
     qv = heads * 2 * HD

time: 1010 us -> 840 us (0.83)
  waiting for transfers between devices: 654 us -> 325 us
  Pallas kernels: 55.2 us -> 380 us
  matrix products: 141 us -> 32 us
  blocking collectives: 57.9 us -> 0 us
    pallas_call x0 -> x2, Pallas kernels: none -> 319 us  [the longest x1 240 us: feed_forward(): pl.pallas_call(functools.partial(ffn_kernel, n=n, chunks=chunks, rows=row...]
    all_gather x4 -> x1, waiting for transfers between devices: 145 us -> 0.98 us  [on_device(): w_proj = lax.all_gather(w_out.astype(BF), 'grp', axis=0, tiled=True)]
    reduce_scatter x5 -> x4, waiting for transfers between devices: 250 us -> 171 us  [the longest x1 64.1 us: on_device(): lax.psum_scatter(mlp_parts.reshape(length, width), 'tp', scatter_dimensio...]
    dot_general x8 -> x2, matrix products: 91.7 us -> 22 us  [dg(): lax.dot_general(a, b, (((ca,), (cb,)), ((), ())), preferred_element_type=...]
    all_to_all x1 -> x0, blocking collectives: 57.9 us -> none  [on_device(): dcontext = lax.all_to_all(dcontext_rows, 'tp', 1, 0, tiled=True)]
    dot_general x3 -> x0, matrix products: 39.3 us -> none  [the longest x1 18.6 us: on_device(): grad_active = jnp.dot(gradb, w_reduce, preferred_element_type=F32)]
    all_gather x1, waiting for transfers between devices: 39.1 us -> 0.01 us  [on_device(): w_reduce = lax.all_gather(w_down.astype(BF), 'grp', axis=0, tiled=True)]
    all_to_all x1 -> x0, waiting for transfers between devices: 26.5 us -> none  [on_device(): context_rows = lax.all_to_all(context, 'tp', 0, 1, tiled=True)]
  transfers between devices with their start and end apart: 15 -> 10, of which waited for: 14 -> 8; matrix products, arithmetic and copies ran while one was open for 16% -> 11% of each run, Pallas kernels for 4% -> 17%
where the time goes in v2:
time: 840 us; the launch traced here: 830 us
  Pallas kernels  380 us (45%)
  waiting for transfers between devices  325 us (39%)
  other arithmetic  58.2 us (7%)
  matrix products  32 us (4%)
  local copies, waits for them, and re-layouts  18.5 us (2%)
  between operations  15.1 us (2%)
    pallas_call x1, Pallas kernels, feed_forward(): pl.pallas_call(functools.partial(ffn_kernel, n=n, chunks=chunks, rows=row...  240 us
    reduce_scatter x1, waiting for transfers between devices, on_device(): lax.psum_scatter(dg(dproj, w_attn, 1, 1).astype(BF), 'tp', scatter_dimens...  89.2 us
    pallas_call x1, Pallas kernels, attn_out(): pl.pallas_call(functools.partial(out_kernel, n=n, chunks=chunks, rows=row...  79.3 us
    reduce_scatter x1, waiting for transfers between devices, on_device(): lax.psum_scatter(mlp_parts.reshape(length, width), 'tp', scatter_dimensio...  64.1 us
    reduce_scatter x1, waiting for transfers between devices, on_device(): grads_expand = scatter(gw_expand).astype(F32)  53.6 us
    reduce_scatter x1, waiting for transfers between devices, on_device(): grads_reduce = scatter(gw_reduce).astype(F32)  52.9 us
    all_gather x1, waiting for transfers between devices, on_device(): w_expand = lax.all_gather(w_up.astype(BF), 'grp', axis=0, tiled=True)  27.5 us
    pallas_call x1, Pallas kernels, small_sum(): pl.pallas_call(functools.partial(small_kernel, n_grp=n_grp, n_tp=n_tp, a_...  22.9 us
  transfers between devices with their start and end apart: 10, of which 8 were waited for; matrix products, arithmetic and copies ran while one was open for 11% of the time, Pallas kernels for 17%

profile of v2, /device:TPU:0, one launch (start us, length us, event | category | flops | bytes accessed | tf_op | source)
XLA Modules:
  0.0 829.6 jit_solution(16505860722324706177)
XLA Ops:
  7.2 2.5 convert_element_type.82
  11.9 2.7 convert_element_type.85
  16.5 7.4 broadcast_select_fusion
  26.0 3.0 convert_reduce_fusion.3
  29.0 4.7 convert_reduce_fusion
  33.8 5.8 fusion.2
  39.7 5.6 fusion.5
  45.3 11.8 %all-gather.5.cloned.1.call-done = bf16[2048,768]{1,0:T(8,128)(2,1)} async-done(((bf16[512,768]{1,0:T(8,128)(2,1)}), bf16[2048,768]{1,0:T(8,128)(2,1)}) %all-gather.5.cloned.1.call-update) | async-done | bytes 3145744 | tf_op jit(solution)/shard_map/all_gather | solution.py:649
  57.2 10.0 %add_convert_fusion.q_ref.k_ref.v_ref = bf16[2048,768]{1,0:T(8,128)(2,1)S(1)} fusion(f32[768]{0:T(1024)S(1)} %add.113, bf16[2048,2048]{1,0:T(8,128)(2,1)} %fusion.5, bf16[2048,768]{1,0:T(8,128)(2,1)} %all-gather.5.cloned.1.call-done), kind=kOutput, calls=%fused_computation.11 | convolution fusion | flops 6445596672 | bytes 14683136 | tf_op jit(solution)/shard_map/dot_general | solution.py:682
  67.2 16.4 %attn_fwd.1 = (bf16[2048,256]{1,0:T(8,128)(2,1)S(1)}, f32[2,1,2048]{2,1,0:T(1,128)S(1)}) custom-call(s32[3,4]{1,0:T(4,128)S(1)} %pad_add_fusion.info, bf16[2048,768]{1,0:T(8,128)(2,1)S(1)} %add_convert_fusion.q_ref.k_ref.v_ref, bf16[2048,768]{1,0:T(8,128)(2,1)S(1)} %add_convert_fusion.q_ref.k_ref.v_ref, bf16[2048,768]{1,0:T(8,128)(2,1)S(1)} %add_convert_fusion.q_ref.k_ref.v_ref), custom_call_target="tpu_custom_call" | custom-call | flops 2147483648 | bytes 4194304 | tf_op jit(solution)/shard_map/attn_fwd/pallas_call | solution.py:53
  83.6 1.7 copy-done
  87.5 79.3 %attn_out.1 = (f32[256,2048]{1,0:T(8,128)S(1)}, bf16[256,2048]{1,0:T(8,128)(2,1)S(1)}) custom-call(bf16[8,256,256]{2,1,0:T(8,128)(2,1)S(1)} %bitcast.50, bf16[2048,256]{1,0:T(8,128)(2,1)S(1)} %copy-done.4, bf16[256,2048]{1,0:T(8,128)(2,1)S(1)} %get-tuple-element.51.x_share, f32[3,2048]{1,0:T(4,128)S(1)} %pad_maximum_fusion.vec), custom_call_target="tpu_custom_call" | custom-call | flops 2147483648 | bytes 8388608 | tf_op jit(solution)/shard_map/attn_out/pallas_call | solution.py:369
  169.1 27.5 %all-gather.9.cloned.1.call-done.w_up = bf16[2048,1024]{1,0:T(8,128)(2,1)} async-done(((bf16[512,1024]{1,0:T(8,128)(2,1)}), bf16[2048,1024]{1,0:T(8,128)(2,1)}) %all-gather.9.cloned.1.call-update) | async-done | bytes 4194320 | tf_op jit(solution)/shard_map/all_gather | solution.py:651
  196.6 240.2 %feed_forward.1 = (bf16[8,256,2048]{2,1,0:T(8,128)(2,1)}, bf16[2048,1024]{1,0:T(8,128)(2,1)}, bf16[2048,1024]{1,0:T(8,128)(2,1)}, bf16[2048,256]{1,0:T(8,128)(2,...) custom-call(bf16[256,2048]{1,0:T(8,128)(2,1)} %copy-done.8, ...), custom_call_target="tpu_custom_call" | custom-call | flops 51539607552 | bytes 67108864 | tf_op jit(solution)/shard_map/feed_forward/pallas_call | solution.py:547
  436.9 1.9 copy-done.1
  441.2 21.6 %attn_bwd.1 = bf16[2048,768]{1,0:T(8,128)(2,1)S(1)} custom-call(s32[3,4]{1,0:T(4,128)S(1)} %pad_add_fusion.info, bf16[2048,768]{1,0:T(8,128)(2,1)S(1)} %copy-done.1, bf16[2048,768]{1,0:T(8,128)(2,1)S(1)} %copy-done.1, bf16[2048,768]{1,0:T(8,128)(2,1)S(1)} %copy-done.1, bf16[2048,256]{1,0:T(8,128)(2,1)S(1)} %copy-done.6, bf16[2048,256]{1,0:T(8,128)(2,1)S(1)} %bitcast.51, ...), custom_call_target="tpu_custom_call" | custom-call | flops 5368709120 | bytes 8388608 | tf_op jit(solution)/shard_map/attn_bwd/pallas_call | solution.py:103
  464.5 10.4 %convolution_convert_fusion.1 = bf16[2048,768]{1,0:T(8,128)(2,1)} fusion(bf16[2048,2048]{1,0:T(8,128)(2,1)} %fusion.5, bf16[2048,768]{1,0:T(8,128)(2,1)S(1)} %attn_bwd.1), kind=kOutput, calls=%fused_computation.12 | convolution fusion | flops 6444023808 | bytes 14680064 | tf_op jit(solution)/shard_map/dot_general | solution.py:17
  476.4 11.6 %convolution_convert_fusion = bf16[2048,2048]{1,0:T(8,128)(2,1)} fusion(bf16[2048,768]{1,0:T(8,128)(2,1)} %copy-done.2, bf16[2048,768]{1,0:T(8,128)(2,1)} %all-gather.5.cloned.1.call-done), kind=kOutput, calls=%fused_computation.9 | convolution fusion | flops 6446645248 | bytes 14680064 | tf_op jit(solution)/shard_map/dot_general | solution.py:17
  489.8 2.6 convert_reduce_fusion.1
  493.4 1.8 convert_element_type.96
  495.2 22.7 %reduce-scatter.11.cloned.1.call-done = bf16[512,768]{1,0:T(8,128)(2,1)} async-done(((bf16[2048,768]{1,0:T(8,128)(2,1)}), bf16[512,768]{1,0:T(8,128)(2,1)}) %reduce-scatter.11.cloned.1.call-update) | async-done | bytes 786448 | tf_op jit(solution)/shard_map/reduce_scatter | solution.py:702
  517.8 2.4 convert_element_type.93
  520.2 53.6 %reduce-scatter.15.cloned.1.call-done = bf16[512,1024]{1,0:T(8,128)(2,1)} async-done(((bf16[2048,1024]{1,0:T(8,128)(2,1)}), bf16[512,1024]{1,0:T(8,128)(2,1)}) %reduce-scatter.15.cloned.1.call-update) | async-done | bytes 1048592 | tf_op jit(solution)/shard_map/reduce_scatter | solution.py:696
  573.8 2.8 convert_element_type.97
  576.6 52.9 %reduce-scatter.17.cloned.1.call-done = bf16[512,1024]{1,0:T(8,128)(2,1)} async-done(((bf16[2048,1024]{1,0:T(8,128)(2,1)}), bf16[512,1024]{1,0:T(8,128)(2,1)}) %reduce-scatter.17.cloned.1.call-update) | async-done | bytes 1048592 | tf_op jit(solution)/shard_map/reduce_scatter | solution.py:695
  629.5 2.8 convert_element_type.98
  632.3 89.2 %reduce-scatter.9.cloned.1.call-done = bf16[256,2048]{1,0:T(8,128)(2,1)} async-done(((bf16[2048,2048]{1,0:T(8,128)(2,1)}), bf16[256,2048]{1,0:T(8,128)(2,1)}) %reduce-scatter.9.cloned.1.call-update) | async-done | bytes 1048592 | tf_op jit(solution)/shard_map/reduce_scatter | solution.py:703
  721.6 2.4 fusion.17
  724.7 22.9 %small_sum.1 = (f32[96,128]{1,0:T(8,128)}, f32[8,16,128]{2,1,0:T(8,128)}) custom-call(f32[112,128]{1,0:T(8,128)} %bitcast.58), custom_call_target="tpu_custom_call" | custom-call | tf_op jit(solution)/shard_map/small_sum/pallas_call | solution.py:611
  751.1 3.9 fusion.16
  755.0 64.1 %reduce-scatter.7.cloned.1.call-done = bf16[256,2048]{1,0:T(8,128)(2,1)} async-done(((bf16[2048,2048]{1,0:T(8,128)(2,1)}), bf16[256,2048]{1,0:T(8,128)(2,1)}) %reduce-scatter.7.cloned.1.call-update) | async-done | bytes 1048592 | tf_op jit(solution)/shard_map/reduce_scatter | solution.py:698
  819.2 3.1 multiply_convert_fusion
  (114 shorter events, 23.2 us)
Async XLA Ops:
  7.2 2.7 copy-start.11
  7.2 3.5 copy-start.10
  7.2 50.0 %all-gather.5.cloned.1.call-start = ((), (), s32[]{:S(2)}) async-start(), calls=%async_computation.6 | async-start | bytes 3932160 | tf_op jit(solution)/shard_map/all_gather | solution.py:649
  9.8 76.5 %all-gather.7.cloned.1.call-start = ((), (), s32[]{:S(2)}) async-start(), calls=%async_computation.7 | async-start | bytes 1310720 | tf_op jit(solution)/shard_map/all_gather | solution.py:650
  10.6 158.5 %all-gather.11.cloned.1.call-start = ((), (), s32[]{:S(2)}) async-start(), calls=%async_computation.9 | async-start | bytes 5242880 | tf_op jit(solution)/shard_map/all_gather | solution.py:652
  11.8 2.9 copy-start.20
  11.8 2.9 copy-start.21
  11.8 184.8 %all-gather.9.cloned.1.call-start = ((), (), s32[]{:S(2)}) async-start(), calls=%async_computation.8 | async-start | bytes 5242880 | tf_op jit(solution)/shard_map/all_gather | solution.py:651
  14.6 478.7 %reduce-scatter.13.cloned.1.call-start = ((), (), s32[]{:S(2)}) async-start(), calls=%async_computation.13 | async-start | bytes 1310720 | tf_op jit(solution)/shard_map/reduce_scatter | solution.py:697
  29.0 10.7 %slice-start = ((s8[8388608]{0:T(1024)(128)(4,1)}), s8[4194304]{0:T(1024)(128)(4,1)S(1)}, s32[]{:S(2)}) async-start(s8[8388608]{0:T(1024)(128)(4,1)} %bitcast.52), calls=%async_computation.16 | async-start | bytes 8388608
  33.7 5.9 copy-start.16
  33.7 5.9 copy-start.17
  33.7 5.9 copy-start.18
  33.7 6.0 slice-start.1
  33.7 6.0 copy-start.13
  33.7 6.0 copy-start.14
  83.6 1.7 copy-start
  85.3 81.5 %copy-start.5 = (bf16[2048,256]{1,0:T(8,128)(2,1)}, bf16[2048,256]{1,0:T(8,128)(2,1)S(1)}, u32[]{:S(2)}) copy-start(bf16[2048,256]{1,0:T(8,128)(2,1)S(1)} %get-tuple-element.28.ctx.o_ref) | copy-start | bytes 3145732
  86.2 1.2 copy-start.4
  166.8 1.3 copy-start.3
  436.8 81.0 %reduce-scatter.11.cloned.1.call-start = ((), (), s32[]{:S(2)}) async-start(), calls=%async_computation.12 | async-start | bytes 3932160 | tf_op jit(solution)/shard_map/reduce_scatter | solution.py:702
  436.9 1.9 copy-start.1
  438.7 1.2 copy-start.6
  440.0 1.2 copy-start.7
  462.8 1.7 copy-start.2
  474.9 98.9 %reduce-scatter.15.cloned.1.call-start = ((), (), s32[]{:S(2)}) async-start(), calls=%async_computation.14 | async-start | bytes 5242880 | tf_op jit(solution)/shard_map/reduce_scatter | solution.py:696
  475.6 153.9 %reduce-scatter.17.cloned.1.call-start = ((), (), s32[]{:S(2)}) async-start(), calls=%async_computation.15 | async-start | bytes 5242880 | tf_op jit(solution)/shard_map/reduce_scatter | solution.py:695
  476.4 245.2 %reduce-scatter.9.cloned.1.call-start = ((), (), s32[]{:S(2)}) async-start(), calls=%async_computation.11 | async-start | bytes 9437184 | tf_op jit(solution)/shard_map/reduce_scatter | solution.py:703
  488.1 331.1 %reduce-scatter.7.cloned.1.call-start = ((), (), s32[]{:S(2)}) async-start(), calls=%async_computation.10 | async-start | bytes 9437184 | tf_op jit(solution)/shard_map/reduce_scatter | solution.py:698
  576.6 147.4 %copy-start.19 = (f32[1,1024]{1,0:T(1,128)S(1)}, f32[1,1024]{1,0:T(1,128)}, u32[]{:S(2)}) copy-start(f32[1,1024]{1,0:T(1,128)} %get-tuple-element.36) | copy-start | bytes 12292
  721.6 29.5 %copy-start.9 = (bf16[256,2048]{1,0:T(8,128)(2,1)S(1)}, bf16[256,2048]{1,0:T(8,128)(2,1)}, u32[]{:S(2)}) copy-start(bf16[256,2048]{1,0:T(8,128)(2,1)} %reduce-scatter.9.cloned.1.call-done) | copy-start | bytes 3145732
  751.1 68.0 %copy-start.15 = (f32[2048]{0:T(1024)S(1)}, f32[2048]{0:T(1024)}, u32[]{:S(2)}) copy-start(f32[2048]{0:T(1024)} %param.27) | copy-start | bytes 24580
  (2 other events, 1.6 us)
Sparse Core Ops, SparseCore 0:
  10.4 46.6 all-gather.4
  59.6 26.6 all-gather.6
  88.7 52.9 all-gather.10
  143.9 52.6 all-gather.8
  436.9 26.5 reduce-scatter.12
  475.0 42.7 reduce-scatter.10
  521.1 52.6 reduce-scatter.14
  576.8 52.6 reduce-scatter.16
  631.9 89.5 reduce-scatter.8
  723.8 95.2 reduce-scatter.6

commit v3 on v2

--- a/solution.py
+++ b/solution.py
@@ -224,12 +224,15 @@
 class Scatter:
     def __init__(self, at, parts, pair, hops, cs, cr, hs, hr):
         self.at, self.parts, self.pair, self.hops = at, parts, pair, hops
+        self.slots = pair.shape[0]
         self.cs, self.cr, self.hs, self.hr = cs, cr, hs, hr
 
     def across(self, c):
+        c = lax.rem(c, self.slots)
         return remote(self.parts.at[:, 1 - self.at.k], self.pair.at[c], self.cs.at[c], self.cr.at[c], self.at.sib)
 
     def line(self, c, side, h, target):
+        c = lax.rem(c, self.slots)
         device = self.at.right if side == 0 else self.at.left
         return remote(self.pair.at[c, target], self.hops.at[side, c, h - 1],
                       self.hs.at[c, side, h - 1], self.hr.at[c, side, h - 1], device)
@@ -241,6 +244,7 @@
         self.across(c).wait()
         own = self.parts[:, pl.ds(self.at.k, 1)]
         own = own.reshape(own.shape[0], own.shape[2], own.shape[3])
+        c = lax.rem(c, self.slots)
         self.pair[c] = (self.pair[c].astype(F32) + own.astype(F32)).astype(BF)
 
     def hop(self, c, h):
@@ -255,20 +259,22 @@
                     @pl.when(pos >= 1)
                     def _():
                         self.line(c, side, h - 1, target).wait_recv()
-                        self.pair[c, target] = (self.pair[c, target].astype(F32)
-                                                + self.hops[side, c, h - 2].astype(F32)).astype(BF)
+                        b = lax.rem(c, self.slots)
+                        self.pair[b, target] = (self.pair[b, target].astype(F32)
+                                                + self.hops[side, b, h - 2].astype(F32)).astype(BF)
                 self.line(c, side, h, target).start()
 
     def finish(self, c, total):
         at = self.at
-        total[...] = self.pair[c, at.z].astype(F32)
+        b = lax.rem(c, self.slots)
+        total[...] = self.pair[b, at.z].astype(F32)
         for side in (0, 1):
             pos = at.z if side == 0 else at.Z - 1 - at.z
 
             @pl.when(pos >= 1)
             def _():
                 self.line(c, side, at.Z - 1, at.z).wait_recv()
-                total[...] += self.hops[side, c, at.Z - 2].astype(F32)
+                total[...] += self.hops[side, b, at.Z - 2].astype(F32)
 
             for h in range(1, at.Z):
                 @pl.when((pos <= h - 1) & (pos < at.Z - 1))
@@ -282,6 +288,7 @@
 
 
 def scatter_scratch(chunks, Z, rows, width):
+    chunks = min(chunks, 4)
     dma = pltpu.SemaphoreType.DMA
     return [pltpu.VMEM((Z, 2, rows, width), BF), pltpu.VMEM((chunks, Z, rows, width), BF),
             pltpu.VMEM((2, chunks, Z - 1, rows, width), BF),
@@ -314,51 +321,81 @@
     return centred * inverse, inverse
 
 
-def out_kernel(ctx, w_out, x_share, vec, hidden, n2, *scratch, n, chunks, rows):
-    total, *sc = scratch
+def product_scatter(at, rs, lhs_ref, w_ref, total, chunks, rows, epilogue):
+    def product(c):
+        lhs = lhs_ref[:, chunk_rows(c, rows), :].reshape(at.n * rows, lhs_ref.shape[2])
+
+        def tile(i):
+            y = dg(lhs, w_ref[cols(i), :], 1, 1)
+            rs.parts[:, :, :, cols(i)] = y.astype(BF).reshape(at.Z, 2, rows, TILE)
+        tiles(w_ref.shape[0] // TILE, tile)
+        rs.start(c)
+
+    def tick(i, carry):
+        c = i - 1
+
+        @pl.when(inside(c, chunks))
+        def _():
+            rs.meet(c)
+            rs.hop(c, 1)
+
+        @pl.when(inside(i, chunks))
+        def _():
+            product(i)
+
+        @pl.when(inside(c, chunks))
+        def _():
+            for h in range(2, at.Z):
+                rs.hop(c, h)
+
+        e = i - 2
+
+        @pl.when(inside(e, chunks))
+        def _():
+            rs.finish(e, total)
+            epilogue(e)
+        return carry
+
+    lax.fori_loop(0, chunks + 2, tick, 0)
+
+
+def out_kernel(ctx, w_out, x_share, vec, hidden, n2, total, *sc, n, chunks, rows):
     at = Place(n)
     at.barrier()
-    rs = Scatter(at, *sc)
-    width = w_out.shape[0]
-
-    def product(c):
-        lhs = ctx[:, chunk_rows(c, rows), :].reshape(n * rows, ctx.shape[2])
-
-        def tile(i):
-            y = dg(lhs, w_out[cols(i), :], 1, 1)
-            rs.parts[:, :, :, cols(i)] = y.astype(BF).reshape(at.Z, 2, rows, TILE)
-        tiles(width // TILE, tile)
-        rs.start(c)
-
-    def tick(i, carry):
-        c = i - 1
-
-        @pl.when(inside(c, chunks))
-        def _():
-            rs.meet(c)
-            rs.hop(c, 1)
-
-        @pl.when(inside(i, chunks))
-        def _():
-            product(i)
-
-        @pl.when(inside(c, chunks))
-        def _():
-            for h in range(2, at.Z):
-                rs.hop(c, h)
-
-        e = i - 2
-
-        @pl.when(inside(e, chunks))
-        def _():
-            rs.finish(e, total)
-            r = chunk_rows(e, rows)
-            h = x_share[r, :].astype(F32) + total[...] + vec[0:1, :]
-            hidden[r, :] = h
-            n2[r, :] = (rows_stats(h)[0] * vec[1:2, :] + vec[2:3, :]).astype(BF)
-        return carry
-
-    lax.fori_loop(0, chunks + 2, tick, 0)
+
+    def epilogue(c):
+        r = chunk_rows(c, rows)
+        h = x_share[r, :].astype(F32) + total[...] + vec[0:1, :]
+        hidden[r, :] = h
+        n2[r, :] = (rows_stats(h)[0] * vec[1:2, :] + vec[2:3, :]).astype(BF)
+
+    product_scatter(at, Scatter(at, *sc), ctx, w_out, total, chunks, rows, epilogue)
+
+
+def back_kernel(dproj, w_attn, dn1, total, *sc, n, chunks, rows):
+    at = Place(n)
+    at.barrier()
+
+    def epilogue(c):
+        dn1[chunk_rows(c, rows), :] = total[...]
+
+    product_scatter(at, Scatter(at, *sc), dproj, w_attn, total, chunks, rows, epilogue)
+
+
+def project_back(dproj, w_attn, n, chunks):
+    length, hw = dproj.shape
+    width = w_attn.shape[0]
+    share = length // n
+    rows = share // chunks
+    vm = pl.BlockSpec(memory_space=pltpu.VMEM)
+    return pl.pallas_call(
+        functools.partial(back_kernel, n=n, chunks=chunks, rows=rows),
+        in_specs=[vm] * 2, out_specs=vm, out_shape=jax.ShapeDtypeStruct((share, width), F32),
+        scratch_shapes=[pltpu.VMEM((rows, width), F32)] + scatter_scratch(chunks, n // 2, rows, width),
+        compiler_params=pltpu.CompilerParams(collective_id=4, has_side_effects=True, vmem_limit_bytes=40 << 20),
+        cost_estimate=pl.CostEstimate(flops=2 * length * hw * width, bytes_accessed=1 << 23, transcendentals=0),
+        name="project_back",
+    )(dproj.reshape(n, share, hw), w_attn)
 
 
 def attn_out(ctx, w_out, x_share, vec, n, chunks):
@@ -377,13 +414,12 @@
     )(ctx.reshape(n, share, hw), w_out, x_share, vec)
 
 
-def ffn_kernel(n2_hbm, gradb_hbm, w_up, w_down, w_out, b_up, ctx, hidden, gshare, gain,
-               mlp_hbm, gwu_hbm, gwd_hbm, gwo, dctx, dh, stats, bsum,
-               gat, acc_up, acc_down, gbuf, mst, actb, dbb, total, lsem, gsem, msem, *scratch, n, chunks, rows):
+def ffn_kernel(n2_hbm, gradb_hbm, w_up, w_down, w_out, b_up, ctx, hidden, gshare, vec, live,
+               gw_hbm, gwo, dctx, dh, res, stats, bsum,
+               gat, acc_up, acc_down, gbuf, actb, dbb, total, lsem, gsem, msem, *scratch, n, chunks, rows):
     at = Place(n)
-    s1, s2, sc = scratch[:4], scratch[4:8], scratch[8:]
-    ag1, ag2 = Gather(at, gat, rows, *s1), Gather(at, gat, rows, *s2)
-    rs = Scatter(at, *sc)
+    ag1, ag2 = Gather(at, gat, rows, *scratch[:4]), Gather(at, gat, rows, *scratch[4:8])
+    rs, mlp = Scatter(at, *scratch[8:15]), Scatter(at, *scratch[15:])
     width, hid = w_up.shape
     m = n * rows
 
@@ -393,9 +429,6 @@
     def fetch(c):
         slot = lax.rem(c, 2)
         return pltpu.make_async_copy(gradb_hbm.at[:, chunk_rows(c, rows), :], gbuf.at[slot], gsem.at[slot])
-
-    def put_mlp(c):
-        return pltpu.make_async_copy(mst, mlp_hbm.at[:, chunk_rows(c, rows), :], msem)
 
     fetch(0).start()
     acc_up[...] = jnp.zeros_like(acc_up)
@@ -438,15 +471,10 @@
         tiles(width // TILE, tile)
 
     def down(c):
-        @pl.when(c > 0)
-        def _():
-            put_mlp(c - 1).wait()
-
         def tile(i):
             y = dg(actb[...], w_down[cols(i), :], 1, 1)
-            mst[:, :, cols(i)] = y.astype(BF).reshape(n, rows, TILE)
+            mlp.parts[:, :, :, cols(i)] = y.astype(BF).reshape(at.Z, 2, rows, TILE)
         tiles(width // TILE, tile)
-        put_mlp(c).start()
 
     def weights(c):
         slot = lax.rem(c, 2)
@@ -462,7 +490,7 @@
         r = chunk_rows(c, rows)
         xhat, inverse = rows_stats(hidden[r, :])
         dn2 = total[...]
-        e = dn2 * gain[...]
+        e = dn2 * vec[0:1, :]
         inner = jnp.mean(e, -1, keepdims=True) + xhat * jnp.mean(e * xhat, -1, keepdims=True)
         d = gshare[r, :].astype(F32) + inverse * (e - inner)
         dh[r, :] = d
@@ -480,31 +508,38 @@
         def _():
             fn(c)
 
-    def hops(i, h):
-        at_stage(i - 3, lambda c: rs.hop(c, h))
-        at_stage(i - 4, lambda c: ag2.hop(c, h))
-        at_stage(i - 1, lambda c: ag1.hop(c, h))
-
     def tick(i, carry):
         at_stage(i, ag1.start)
         at_stage(i - 3, rs.meet)
-        hops(i, 1)
-        at_stage(i - 2, forward)
-        for h in range(2, at.Z):
-            hops(i, h)
-            if h == 2:
-                at_stage(i - 2, back)
+        for h in range(1, at.Z):
+            at_stage(i - 3, lambda c: rs.hop(c, h))
+            at_stage(i - 1, lambda c: ag1.hop(c, h))
+            if h == 1:
+                at_stage(i - 4, lambda c: mlp.hop(c, at.Z - 1))
+                at_stage(i - 5, lambda c: ag2.hop(c, at.Z - 1))
+                at_stage(i - 2, forward)
+            else:
+                if h == 2:
+                    def served(c):
+                        mlp.finish(c, total)
+                        r = chunk_rows(c, rows)
+                        res[r, :] = (live[r, :] * (hidden[r, :] + total[...] + vec[1:2, :])).astype(BF)
+                    at_stage(i - 4, served)
+                    at_stage(i - 3, mlp.meet)
+                at_stage(i - 3, lambda c: mlp.hop(c, h - 1))
+                at_stage(i - 4, lambda c: ag2.hop(c, h - 1))
+                if h == 2:
+                    at_stage(i - 2, back)
+
+                    def gathered(c):
+                        ag2.finish(c)
+                        heads(c)
+                    at_stage(i - 5, gathered)
 
         def rest(c):
             weights(c)
             rs.start(c)
-            down(c)
         at_stage(i - 2, rest)
-
-        def gathered(c):
-            ag2.finish(c)
-            heads(c)
-        at_stage(i - 4, gathered)
 
         def reduced(c):
             rs.finish(c, total)
@@ -512,30 +547,37 @@
             ag2.start(c)
         at_stage(i - 3, reduced)
         at_stage(i - 1, ag1.finish)
+
+        def send_mlp(c):
+            down(c)
+            mlp.start(c)
+        at_stage(i - 2, send_mlp)
+
+        @pl.when(i == chunks + 2)
+        def _():
+            tiles(width // m, store)
         return carry
 
-    lax.fori_loop(0, chunks + 4, tick, 0)
-    put_mlp(chunks - 1).wait()
+    def store(i):
+        r = cols(i, m)
+        actb[...] = acc_up[r, :].astype(BF)
+        one = pltpu.make_async_copy(actb, gw_hbm.at[r, pl.ds(0, hid)], lsem)
+        one.start()
+        dbb[...] = acc_down[r, :].astype(BF)
+        two = pltpu.make_async_copy(dbb, gw_hbm.at[r, pl.ds(hid, hid)], msem)
+        two.start()
+        one.wait()
+        two.wait()
+
+    lax.fori_loop(0, chunks + 5, tick, 0)
 
     def final(i):
         x = gat[:, :, cols(i)].reshape(-1, TILE)
         gwo[cols(i), :] = dg(x, ctx[...], 0, 0).astype(BF)
     tiles(width // TILE, final)
 
-    def store(i):
-        r = cols(i, m)
-        actb[...] = acc_up[r, :].astype(BF)
-        one = pltpu.make_async_copy(actb, gwu_hbm.at[r, :], lsem)
-        one.start()
-        dbb[...] = acc_down[r, :].astype(BF)
-        two = pltpu.make_async_copy(dbb, gwd_hbm.at[r, :], msem)
-        two.start()
-        one.wait()
-        two.wait()
-    tiles(width // m, store)
-
-
-def feed_forward(n2, gradb, w_up, w_down, w_out, b_up, ctx, hidden, gshare, gain, n, chunks):
+
+def feed_forward(n2, gradb, w_up, w_down, w_out, b_up, ctx, hidden, gshare, vec, live, n, chunks):
     length, width = gradb.shape
     hid, hw = w_up.shape[1], w_out.shape[1]
     share = length // n
@@ -546,19 +588,19 @@
     m = n * rows
     return pl.pallas_call(
         functools.partial(ffn_kernel, n=n, chunks=chunks, rows=rows),
-        in_specs=[hbm, hbm] + [vm] * 8,
-        out_specs=[hbm, hbm, hbm] + [vm] * 5,
-        out_shape=[S((n, share, width), BF), S((width, hid), BF), S((width, hid), BF), S((width, hw), BF),
-                   S((n, share, hw), BF), S((share, width), F32), S((8, width), F32), S((1, hid), F32)],
+        in_specs=[hbm, hbm] + [vm] * 9,
+        out_specs=[hbm] + [vm] * 6,
+        out_shape=[S((width, 2 * hid), BF), S((width, hw), BF), S((n, share, hw), BF), S((share, width), F32),
+                   S((share, width), BF), S((8, width), F32), S((1, hid), F32)],
         scratch_shapes=[pltpu.VMEM((n, share, width), BF), pltpu.VMEM((width, hid), F32), pltpu.VMEM((width, hid), F32),
-                        pltpu.VMEM((2, n, rows, width), BF), pltpu.VMEM((n, rows, width), BF),
+                        pltpu.VMEM((2, n, rows, width), BF),
                         pltpu.VMEM((m, hid), BF), pltpu.VMEM((m, hid), BF), pltpu.VMEM((rows, width), F32),
                         pltpu.SemaphoreType.DMA, pltpu.SemaphoreType.DMA((2,)), pltpu.SemaphoreType.DMA]
-                       + gather_sems(chunks, Z) + gather_sems(chunks, Z) + scatter_scratch(chunks, Z, rows, width),
+                       + gather_sems(chunks, Z) + gather_sems(chunks, Z) + scatter_scratch(chunks, Z, rows, width) * 2,
         compiler_params=pltpu.CompilerParams(collective_id=3, has_side_effects=True, vmem_limit_bytes=62 << 20),
         cost_estimate=pl.CostEstimate(flops=12 * length * hid * width, bytes_accessed=1 << 26, transcendentals=0),
         name="feed_forward",
-    )(n2, gradb.reshape(n, share, width), w_up, w_down, w_out, b_up, ctx, hidden, gshare, gain)
+    )(n2, gradb.reshape(n, share, width), w_up, w_down, w_out, b_up, ctx, hidden, gshare, vec, live)
 
 
 def small_kernel(x_ref, a_ref, b_ref, gbuf, tbuf, gs, gr, ts, tr, *, n_grp, n_tp, a_rows):
@@ -687,20 +729,19 @@
     gradb = jnp.where(live_all, out_cotangent, jnp.zeros_like(out_cotangent))
     gradb_share = mine(gradb)
     grad_share = gradb_share.astype(F32)
-    (mlp_parts, gw_expand, gw_reduce, gw_proj, dcontext, dh, stats, up_sum) = feed_forward(
+    gw_ffn, gw_proj, dcontext, dh, result, stats, up_sum = feed_forward(
         n2_share, gradb, w_expand, w_reduce, w_proj, up_bias, context, hidden, gradb_share,
-        second_norm_gain[None], n_tp, 8)
+        jnp.stack([second_norm_gain, b_down]), live, n_tp, 8)
     dcontext = dcontext.reshape(length, -1)
     scatter = functools.partial(lax.psum_scatter, axis_name="grp", scatter_dimension=0, tiled=True)
-    grads_reduce = scatter(gw_reduce).astype(F32)
-    grads_expand = scatter(gw_expand).astype(F32)
-    grads_proj = scatter(gw_proj).astype(F32)
-    mlp = lax.psum_scatter(mlp_parts.reshape(length, width), "tp", scatter_dimension=0, tiled=True).astype(F32)
-    result = (live * (hidden + mlp + b_down)).astype(BF)
+    grads_ffn = scatter(gw_ffn).astype(F32)
+    grads_expand, grads_reduce = grads_ffn[:, :hidden_here], grads_ffn[:, hidden_here:]
 
     dproj = attn_bwd(info, proj, context, dcontext, lse)
-    grads_attn = scatter(dg(n1, dproj, 0, 0).astype(BF)).astype(F32)
-    dn1 = lax.psum_scatter(dg(dproj, w_attn, 1, 1).astype(BF), "tp", scatter_dimension=0, tiled=True).astype(F32)
+    gw_attn = dg(n1, dproj, 0, 0).astype(BF)
+    grads_late = scatter(jnp.concatenate([gw_attn, gw_proj], 1)).astype(F32)
+    grads_attn, grads_proj = grads_late[:, :gw_attn.shape[1]], grads_late[:, gw_attn.shape[1]:]
+    dn1 = project_back(dproj, w_attn, n_tp, 8)
     grad_x = dh + norm_back(dn1, xhat1, inverse1, first_norm_gain)
 
     proj_sums = jnp.sum(dproj.astype(F32), 0).reshape(heads, 3, HD)

time: 840 us -> 654 us (0.78)
  waiting for transfers between devices: 325 us -> 61.8 us
  Pallas kernels: 380 us -> 460 us
  local copies, waits for them, and re-layouts: 18.5 us -> 33.4 us
  matrix products: 32 us -> 21.5 us
    reduce_scatter x6 -> x2, waiting for transfers between devices: 283 us -> 23.6 us  [the longest x1 23.6 us: on_device(): grads_ffn = scatter(gw_ffn).astype(F32)]
    pallas_call x0 -> x1, Pallas kernels: none -> 77.8 us  [project_back(): pl.pallas_call(functools.partial(back_kernel, n=n, chunks=chunks, rows=ro...]
    convert_element_type x5 -> x0, other arithmetic: 12.9 us -> none  [the longest x1 3.14 us: on_device(): result = (live * (hidden + mlp + b_down)).astype(BF)]
    dot_general x2 -> x1, matrix products: 22 us -> 11.5 us  [dg(): lax.dot_general(a, b, (((ca,), (cb,)), ((), ())), preferred_element_type=...]
    unnamed x61 -> x72, local copies, waits for them, and re-layouts: 14 us -> 21.6 us
  transfers between devices with their start and end apart: 10 -> 6, of which waited for: 8 -> 4; matrix products, arithmetic and copies ran while one was open for 11% -> 10% of each run, Pallas kernels for 17% -> 30%
where the time goes in v3:
time: 654 us; the launch traced here: 644 us
  Pallas kernels  460 us (70%)
  waiting for transfers between devices  61.8 us (9%)
  other arithmetic  51.3 us (8%)
  local copies, waits for them, and re-layouts  33.4 us (5%)
  matrix products  21.5 us (3%)
  between operations  15 us (2%)
    pallas_call x1, Pallas kernels, feed_forward(): pl.pallas_call(functools.partial(ffn_kernel, n=n, chunks=chunks, rows=row...  248 us
    pallas_call x1, Pallas kernels, attn_out(): pl.pallas_call(functools.partial(out_kernel, n=n, chunks=chunks, rows=row...  78.9 us
    pallas_call x1, Pallas kernels, project_back(): pl.pallas_call(functools.partial(back_kernel, n=n, chunks=chunks, rows=ro...  77.8 us
    all_gather x1, waiting for transfers between devices, on_device(): w_expand = lax.all_gather(w_up.astype(BF), 'grp', axis=0, tiled=True)  27.8 us
    reduce_scatter x1, waiting for transfers between devices, on_device(): grads_ffn = scatter(gw_ffn).astype(F32)  23.6 us
    unnamed x72, local copies, waits for them, and re-layouts  21.6 us
    pallas_call x1, Pallas kernels, attn_bwd(): pl.pallas_call(functools.partial(attn_bwd_kernel, nb=nb), grid_spec=pltpu...  21.6 us
    pallas_call x1, Pallas kernels, small_sum(): pl.pallas_call(functools.partial(small_kernel, n_grp=n_grp, n_tp=n_tp, a_...  18.1 us
  transfers between devices with their start and end apart: 6, of which 4 were waited for; matrix products, arithmetic and copies ran while one was open for 10% of the time, Pallas kernels for 30%

profile of v3, /device:TPU:0, one launch (start us, length us, event | category | flops | bytes accessed | tf_op | source)
XLA Modules:
  0.0 643.5 jit_solution(17922756157878869504)
XLA Ops:
  7.2 2.5 convert_element_type.66
  11.9 2.7 convert_element_type.69
  16.5 1.3 fusion.18.live
  18.7 8.0 %broadcast_select_fusion = bf16[2048,2048]{1,0:T(8,128)(2,1)} fusion(bf16[2048,2048]{1,0:T(8,128)(2,1)} %param.17, pred[2048]{0:T(1024)(128)(4,1)S(1)} %iota_compare_fusion), kind=kLoop, calls=%fused_computation.8 | loop fusion | flops 4194304 | bytes 16779264 | tf_op jit(solution)/shard_map/jit(_where)/select_n | solution.py:729
  28.0 3.0 convert_reduce_fusion.2
  30.9 4.7 convert_reduce_fusion
  35.7 6.4 fusion.2
  42.8 5.6 fusion.5
  48.4 8.7 %all-gather.5.cloned.1.call-done.w_attn = bf16[2048,768]{1,0:T(8,128)(2,1)} async-done(((bf16[512,768]{1,0:T(8,128)(2,1)}), bf16[2048,768]{1,0:T(8,128)(2,1)}) %all-gather.5.cloned.1.call-update) | async-done | bytes 3145744 | tf_op jit(solution)/shard_map/all_gather | solution.py:691
  57.2 10.0 %add_convert_fusion.q_ref.k_ref.v_ref = bf16[2048,768]{1,0:T(8,128)(2,1)S(1)} fusion(f32[768]{0:T(1024)S(1)} %add.95, bf16[2048,2048]{1,0:T(8,128)(2,1)} %fusion.5, bf16[2048,768]{1,0:T(8,128)(2,1)} %all-gather.5.cloned.1.call-done.w_attn), kind=kOutput, calls=%fused_computation.10 | convolution fusion | flops 6445596672 | bytes 14683136 | tf_op jit(solution)/shard_map/dot_general | solution.py:724
  67.2 16.4 %attn_fwd.1 = (bf16[2048,256]{1,0:T(8,128)(2,1)S(1)}, f32[2,1,2048]{2,1,0:T(1,128)S(1)}) custom-call(s32[3,4]{1,0:T(4,128)S(1)} %pad_add_fusion.info, bf16[2048,768]{1,0:T(8,128)(2,1)S(1)} %add_convert_fusion.q_ref.k_ref.v_ref, bf16[2048,768]{1,0:T(8,128)(2,1)S(1)} %add_convert_fusion.q_ref.k_ref.v_ref, bf16[2048,768]{1,0:T(8,128)(2,1)S(1)} %add_convert_fusion.q_ref.k_ref.v_ref), custom_call_target="tpu_custom_call" | custom-call | flops 2147483648 | bytes 4194304 | tf_op jit(solution)/shard_map/attn_fwd/pallas_call | solution.py:53
  83.6 1.6 copy-done
  87.5 78.9 %attn_out.1 = (f32[256,2048]{1,0:T(8,128)S(1)}, bf16[256,2048]{1,0:T(8,128)(2,1)S(1)}) custom-call(bf16[8,256,256]{2,1,0:T(8,128)(2,1)S(1)} %bitcast.50, bf16[2048,256]{1,0:T(8,128)(2,1)S(1)} %copy-done.6, bf16[256,2048]{1,0:T(8,128)(2,1)S(1)} %get-tuple-element.105.x_share, f32[3,2048]{1,0:T(4,128)S(1)} %pad_maximum_fusion.1.vec), custom_call_target="tpu_custom_call" | custom-call | flops 2147483648 | bytes 8388608 | tf_op jit(solution)/shard_map/attn_out/pallas_call | solution.py:406
  166.4 1.3 copy-done.10
  168.7 27.8 %all-gather.9.cloned.1.call-done.w_up = bf16[2048,1024]{1,0:T(8,128)(2,1)} async-done(((bf16[512,1024]{1,0:T(8,128)(2,1)}), bf16[2048,1024]{1,0:T(8,128)(2,1)}) %all-gather.9.cloned.1.call-update) | async-done | bytes 4194320 | tf_op jit(solution)/shard_map/all_gather | solution.py:693
  196.4 247.6 %feed_forward.1 = (bf16[2048,2048]{1,0:T(8,128)(2,1)}, bf16[2048,256]{1,0:T(8,128)(2,1)}, bf16[8,256,256]{2,1,0:T(8,128)(2,1)}, f32[256,2048]{1,0:T(8,128)}, bf1...) custom-call(bf16[256,2048]{1,0:T(8,128)(2,1)} %copy-done.11, bf16[8,256,2048]{2,1,0:T(8,128)(2,1)} %bitcast.54, ...), custom_call_target="tpu_custom_call" | custom-call | flops 51539607552 | bytes 67108864 | tf_op jit(solution)/shard_map/feed_forward/pallas_call | solution.py:589
  444.0 1.9 copy-done.1
  448.4 21.6 %attn_bwd.1 = bf16[2048,768]{1,0:T(8,128)(2,1)S(1)} custom-call(s32[3,4]{1,0:T(4,128)S(1)} %pad_add_fusion.info, bf16[2048,768]{1,0:T(8,128)(2,1)S(1)} %copy-done.1, bf16[2048,768]{1,0:T(8,128)(2,1)S(1)} %copy-done.1, bf16[2048,768]{1,0:T(8,128)(2,1)S(1)} %copy-done.1, bf16[2048,256]{1,0:T(8,128)(2,1)S(1)} %copy-done.8, bf16[2048,256]{1,0:T(8,128)(2,1)S(1)} %bitcast.51, ...), custom_call_target="tpu_custom_call" | custom-call | flops 5368709120 | bytes 8388608 | tf_op jit(solution)/shard_map/attn_bwd/pallas_call | solution.py:103
  469.9 11.5 %convolution_convert_fusion = bf16[2048,768]{0,1:T(8,128)(2,1)} fusion(bf16[2048,2048]{1,0:T(8,128)(2,1)} %fusion.5, bf16[2048,768]{1,0:T(8,128)(2,1)S(1)} %attn_bwd.1), kind=kOutput, calls=%fused_computation.12 | convolution fusion | flops 6444023808 | bytes 14680064 | tf_op jit(solution)/shard_map/dot_general | solution.py:17
  481.5 1.7 copy.40
  483.2 4.4 pad_maximum_fusion
  488.7 2.4 convert_reduce_fusion.1
  492.1 2.5 copy-done.4
  494.7 1.9 copy-done.5
  496.6 77.8 %project_back.1 = f32[256,2048]{1,0:T(8,128)S(1)} custom-call(bf16[8,256,768]{2,1,0:T(8,128)(2,1)S(1)} %bitcast.49, bf16[2048,768]{1,0:T(8,128)(2,1)S(1)} %copy-done.5), custom_call_target="tpu_custom_call" | custom-call | flops 6442450944 | bytes 8388608 | tf_op jit(solution)/shard_map/project_back/pallas_call | solution.py:391
  577.4 18.1 %small_sum.1 = (f32[96,128]{1,0:T(8,128)}, f32[8,16,128]{2,1,0:T(8,128)}) custom-call(f32[112,128]{1,0:T(8,128)} %bitcast.57), custom_call_target="tpu_custom_call" | custom-call | tf_op jit(solution)/shard_map/small_sum/pallas_call | solution.py:653
  597.6 1.4 slice_bitcast_fusion.2
  599.0 4.5 fusion.15
  603.5 1.4 slice.85
  605.0 1.6 copy.41
  607.6 23.6 %reduce-scatter.5.cloned.1.call-done = bf16[512,2048]{1,0:T(8,128)(2,1)} async-done(((bf16[2048,2048]{1,0:T(8,128)(2,1)}), bf16[512,2048]{1,0:T(8,128)(2,1)}) %reduce-scatter.5.cloned.1.call-update) | async-done | bytes 2097168 | tf_op jit(solution)/shard_map/reduce_scatter | solution.py:737
  631.3 4.0 fusion.21
  (114 shorter events, 21.6 us)
Async XLA Ops:
  7.2 2.7 copy-start.15
  7.2 3.5 copy-start.13
  7.2 50.0 %all-gather.5.cloned.1.call-start = ((), (), s32[]{:S(2)}) async-start(), calls=%async_computation.2 | async-start | bytes 3932160 | tf_op jit(solution)/shard_map/all_gather | solution.py:691
  9.8 76.5 %all-gather.7.cloned.1.call-start = ((), (), s32[]{:S(2)}) async-start(), calls=%async_computation.3 | async-start | bytes 1310720 | tf_op jit(solution)/shard_map/all_gather | solution.py:692
  10.6 158.1 %all-gather.11.cloned.1.call-start = ((), (), s32[]{:S(2)}) async-start(), calls=%async_computation.5 | async-start | bytes 5242880 | tf_op jit(solution)/shard_map/all_gather | solution.py:694
  11.8 2.9 copy-start.24
  11.8 2.9 copy-start.25
  11.8 184.6 %all-gather.9.cloned.1.call-start = ((), (), s32[]{:S(2)}) async-start(), calls=%async_computation.4 | async-start | bytes 5242880 | tf_op jit(solution)/shard_map/all_gather | solution.py:693
  14.6 588.9 %reduce-scatter.3.cloned.1.call-start = ((), (), s32[]{:S(2)}) async-start(), calls=%async_computation.6 | async-start | bytes 5242880 | tf_op jit(solution)/shard_map/reduce_scatter | solution.py:742
  30.9 11.9 %slice-start = ((s8[8388608]{0:T(1024)(128)(4,1)}), s8[4194304]{0:T(1024)(128)(4,1)S(1)}, s32[]{:S(2)}) async-start(s8[8388608]{0:T(1024)(128)(4,1)} %bitcast.52), calls=%async_computation.8 | async-start | bytes 8388608
  35.6 6.5 %copy-start.18 = (f32[2048]{0:T(1024)S(1)}, f32[2048]{0:T(1024)}, u32[]{:S(2)}) copy-start(f32[2048]{0:T(1024)} %param.30) | copy-start | bytes 24580
  35.7 6.5 %copy-start.22 = (f32[2048]{0:T(1024)S(1)}, f32[2048]{0:T(1024)}, u32[]{:S(2)}) copy-start(f32[2048]{0:T(1024)} %param.27) | copy-start | bytes 24580
  35.7 7.1 %copy-start.20 = (f32[2048]{0:T(1024)S(1)}, f32[2048]{0:T(1024)}, u32[]{:S(2)}) copy-start(f32[2048]{0:T(1024)} %param.31) | copy-start | bytes 24580
  35.7 7.1 %copy-start.21 = (f32[2048]{0:T(1024)S(1)}, f32[2048]{0:T(1024)}, u32[]{:S(2)}) copy-start(f32[2048]{0:T(1024)} %param.23) | copy-start | bytes 24580
  35.7 7.1 %slice-start.1 = ((s8[8388608]{0:T(1024)(128)(4,1)}), s8[4194304]{0:T(1024)(128)(4,1)S(1)}, s32[]{:S(2)}) async-start(s8[8388608]{0:T(1024)(128)(4,1)} %bitcast.52), calls=%async_computation.9 | async-start | bytes 8388608
  35.7 7.1 %copy-start.17 = (f32[2048]{0:T(1024)S(1)}, f32[2048]{0:T(1024)}, u32[]{:S(2)}) copy-start(f32[2048]{0:T(1024)} %param.28) | copy-start | bytes 24580
  35.7 7.1 %copy-start.19 = (f32[2048]{0:T(1024)S(1)}, f32[2048]{0:T(1024)}, u32[]{:S(2)}) copy-start(f32[2048]{0:T(1024)} %param.29) | copy-start | bytes 24580
  83.6 1.6 copy-start
  85.2 81.1 %copy-start.7 = (bf16[2048,256]{1,0:T(8,128)(2,1)}, bf16[2048,256]{1,0:T(8,128)(2,1)S(1)}, u32[]{:S(2)}) copy-start(bf16[2048,256]{1,0:T(8,128)(2,1)S(1)} %get-tuple-element.27.ctx.o_ref) | copy-start | bytes 3145732
  86.3 1.2 copy-start.6
  166.4 1.3 copy-start.10
  444.0 1.9 copy-start.1
  445.9 1.2 copy-start.8
  447.1 1.2 copy-start.9
  469.9 11.5 %copy-start.3 = (bf16[2048,768]{1,0:T(8,128)(2,1)}, bf16[2048,768]{1,0:T(8,128)(2,1)S(1)}, u32[]{:S(2)}) copy-start(bf16[2048,768]{1,0:T(8,128)(2,1)S(1)} %attn_bwd.1) | copy-start | bytes 9437188
  487.7 143.6 %reduce-scatter.5.cloned.1.call-start = ((), (), s32[]{:S(2)}) async-start(), calls=%async_computation.7 | async-start | bytes 10485760 | tf_op jit(solution)/shard_map/reduce_scatter | solution.py:737
  492.1 2.6 copy-start.4
  494.7 1.9 copy-start.5
  574.4 1.3 copy-start.2
  575.7 1.0 copy-start.23
  603.5 3.1 copy-start.12
  607.6 27.6 %copy-start.14 = (bf16[256,2048]{1,0:T(8,128)(2,1)S(1)}, bf16[256,2048]{1,0:T(8,128)(2,1)}, u32[]{:S(2)}) copy-start(bf16[256,2048]{1,0:T(8,128)(2,1)} %get-tuple-element.144) | copy-start | bytes 3145732
  (2 other events, 1.6 us)
Sparse Core Ops, SparseCore 0:
  10.4 46.6 all-gather.4
  59.6 26.6 all-gather.6
  88.7 52.7 all-gather.10
  143.8 52.6 all-gather.8
  487.8 51.3 reduce-scatter.2
  542.4 88.7 reduce-scatter.4

commit v4 on v3

--- a/solution.py
+++ b/solution.py
@@ -372,30 +372,220 @@
     product_scatter(at, Scatter(at, *sc), ctx, w_out, total, chunks, rows, epilogue)
 
 
-def back_kernel(dproj, w_attn, dn1, total, *sc, n, chunks, rows):
+class AllSum:
+    def __init__(self, at, n_grp, x, gbuf, tbuf, gs, gr, ts, tr):
+        self.at, self.n_grp, self.x, self.gbuf, self.tbuf = at, n_grp, x, gbuf, tbuf
+        self.gs, self.gr, self.ts, self.tr = gs, gr, ts, tr
+
+    def over_grp(self, d):
+        at = self.at
+        return remote(self.x, self.gbuf.at[at.g], self.gs.at[d - 1], self.gr.at[d - 1],
+                      (lax.rem(at.g + d, self.n_grp), at.t))
+
+    def over_tp(self, d):
+        at = self.at
+        return remote(self.tbuf.at[at.t], self.tbuf.at[at.t], self.ts.at[d - 1], self.tr.at[d - 1],
+                      (at.g, lax.rem(at.t + d, at.n)))
+
+    def start(self):
+        for d in range(1, self.n_grp):
+            self.over_grp(d).start()
+        self.gbuf[self.at.g] = self.x[...]
+
+    def turn(self):
+        for d in range(1, self.n_grp):
+            self.over_grp(d).wait()
+        total = self.gbuf[0]
+        for i in range(1, self.n_grp):
+            total = total + self.gbuf[i]
+        self.tbuf[self.at.t] = total
+        for d in range(1, self.at.n):
+            self.over_tp(d).start()
+
+    def finish(self):
+        for d in range(1, self.at.n):
+            self.over_tp(d).wait()
+
+    def total(self, lo, hi):
+        out = self.tbuf[0, lo:hi, :]
+        for i in range(1, self.at.n):
+            out = out + self.tbuf[i, lo:hi, :]
+        return out
+
+
+def all_sum_scratch(n_grp, n, shape):
+    dma = pltpu.SemaphoreType.DMA
+    return [pltpu.VMEM(shape, F32), pltpu.VMEM((n_grp,) + shape, F32), pltpu.VMEM((n,) + shape, F32),
+            dma((n_grp - 1,)), dma((n_grp - 1,)), dma((n - 1,)), dma((n - 1,))]
+
+
+def back_kernel(dproj, w_attn, n1_hbm, gw_proj, x_share, dh, gain, stats, up_sum,
+                grad_x, g_attn, g_proj, sums, owned,
+                n1, gw, got, got_proj, total, qv, ln_sum, nsem, ws, wr, ps, pr, *scratch, n, n_grp, chunks, rows):
     at = Place(n)
-    at.barrier()
-
-    def epilogue(c):
-        dn1[chunk_rows(c, rows), :] = total[...]
-
-    product_scatter(at, Scatter(at, *sc), dproj, w_attn, total, chunks, rows, epilogue)
-
-
-def project_back(dproj, w_attn, n, chunks):
+    width, hw = w_attn.shape
+    block = width // n_grp
+    per = block // TILE
+    heads = hw // (3 * HD)
+    hid = up_sum.shape[1]
+    load = pltpu.make_async_copy(n1_hbm, n1, nsem)
+    load.start()
+    rs, early, late = Scatter(at, *scratch[:7]), AllSum(at, n_grp, *scratch[7:14]), AllSum(at, n_grp, *scratch[14:])
+    bar = pltpu.get_barrier_semaphore()
+    for d in range(1, n_grp):
+        pl.semaphore_signal(bar, inc=1, device_id=(lax.rem(at.g + d, n_grp), at.t), device_id_type=MESH)
+    for d in range(1, n):
+        pl.semaphore_signal(bar, inc=1, device_id=(at.g, lax.rem(at.t + d, n)), device_id_type=MESH)
+    pl.semaphore_wait(bar, n_grp + n - 2)
+
+    def owner(k):
+        return lax.rem(at.g + 1 + k, n_grp)
+
+    def send(k):
+        r = chunk_rows(owner(k), block)
+        return remote(gw.at[r, :], got.at[k], ws.at[k], wr.at[k], (owner(k), at.t))
+
+    def send_proj(k):
+        r = chunk_rows(owner(k), block)
+        return remote(gw_proj.at[r, :], got_proj.at[k], ps.at[k], pr.at[k], (owner(k), at.t))
+
+    for k in range(n_grp - 1):
+        send_proj(k).start()
+    qv[...] = jnp.zeros_like(qv)
+    ln_sum[...] = jnp.zeros_like(ln_sum)
+
+    def product(c):
+        lhs = dproj[:, chunk_rows(c, rows), :].reshape(n * rows, hw)
+        qv[...] += jnp.sum(lhs.astype(F32), 0, keepdims=True)
+
+        def tile(i):
+            y = dg(lhs, w_attn[cols(i), :], 1, 1)
+            rs.parts[:, :, :, cols(i)] = y.astype(BF).reshape(at.Z, 2, rows, TILE)
+        tiles(width // TILE, tile)
+        rs.start(c)
+
+    def weights(i):
+        k = i // per
+        first = pl.multiple_of(owner(k) * block + lax.rem(i, per) * TILE, TILE)
+        y = dg(n1[:, pl.ds(first, TILE)], dproj[...].reshape(-1, hw), 0, 0)
+
+        @pl.when(k < n_grp - 1)
+        def _():
+            gw[pl.ds(first, TILE), :] = y.astype(BF)
+
+            @pl.when(lax.rem(i, per) == per - 1)
+            def _():
+                send(k).start()
+
+        @pl.when(k == n_grp - 1)
+        def _():
+            g_attn[cols(lax.rem(i, per)), :] = y
+
+    def norm_grad(c):
+        r = chunk_rows(c, rows)
+        xhat, inverse = rows_stats(x_share[r, :].astype(F32))
+        dn = total[...]
+        e = dn * gain[...]
+        inner = jnp.mean(e, -1, keepdims=True) + xhat * jnp.mean(e * xhat, -1, keepdims=True)
+        grad_x[r, :] = dh[r, :] + inverse * (e - inner)
+        ln_sum[0:1, :] += jnp.sum(dn * xhat, 0, keepdims=True)
+        ln_sum[1:2, :] += jnp.sum(dn, 0, keepdims=True)
+
+    load.wait()
+
+    def tick(i, carry):
+        c = i - 1
+
+        @pl.when(inside(c, chunks))
+        def _():
+            rs.meet(c)
+            rs.hop(c, 1)
+
+        @pl.when(inside(i, chunks))
+        def _():
+            product(i)
+
+        @pl.when(inside(c, chunks))
+        def _():
+            rs.hop(c, 2)
+
+        @pl.when(i < width // TILE)
+        def _():
+            weights(i)
+
+        @pl.when(inside(c, chunks))
+        def _():
+            for h in range(3, at.Z):
+                rs.hop(c, h)
+
+        @pl.when(i == chunks)
+        def _():
+            early.x[...] = stats[...]
+            early.x[4:5, 0:hid] = up_sum[...]
+            for h in range(heads):
+                for j, src in ((0, 3 * h), (1, 3 * h + 2)):
+                    early.x[4:5, hid + (2 * h + j) * HD:hid + (2 * h + j + 1) * HD] = qv[:, src * HD:(src + 1) * HD]
+            early.start()
+
+        @pl.when(i == chunks + 1)
+        def _():
+            early.turn()
+        e = i - 2
+
+        @pl.when(inside(e, chunks))
+        def _():
+            rs.finish(e, total)
+            norm_grad(e)
+        return carry
+
+    lax.fori_loop(0, chunks + 2, tick, 0)
+    part = width // 4
+    for j in range(4):
+        late.x[j:j + 1, :] = ln_sum[0:1, j * part:(j + 1) * part]
+        late.x[j + 4:j + 5, :] = ln_sum[1:2, j * part:(j + 1) * part]
+    late.start()
+    mine = chunk_rows(at.g, block)
+    g_proj[...] = gw_proj[mine, :].astype(F32)
+    for k in range(n_grp - 1):
+        send(k).wait()
+        send_proj(k).wait()
+        g_attn[...] += got[k].astype(F32)
+        g_proj[...] += got_proj[k].astype(F32)
+    late.turn()
+    early.finish()
+    sums[0:4, :] = early.total(0, 4)
+    owned[...] = early.tbuf[:, 4, :]
+    late.finish()
+    ln = late.total(0, 8)
+    for j in range(4):
+        sums[4:5, j * part:(j + 1) * part] = ln[j:j + 1, :]
+        sums[5:6, j * part:(j + 1) * part] = ln[j + 4:j + 5, :]
+    sums[6:8, :] = jnp.zeros_like(sums[6:8, :])
+
+
+def project_back(dproj, w_attn, n1, gw_proj, x_share, dh, gain, stats, up_sum, n, n_grp, chunks):
     length, hw = dproj.shape
     width = w_attn.shape[0]
     share = length // n
     rows = share // chunks
-    vm = pl.BlockSpec(memory_space=pltpu.VMEM)
+    block = width // n_grp
+    pw = gw_proj.shape[1]
+    vm, hbm = pl.BlockSpec(memory_space=pltpu.VMEM), pl.BlockSpec(memory_space=pl.ANY)
+    S, dma = jax.ShapeDtypeStruct, pltpu.SemaphoreType.DMA
     return pl.pallas_call(
-        functools.partial(back_kernel, n=n, chunks=chunks, rows=rows),
-        in_specs=[vm] * 2, out_specs=vm, out_shape=jax.ShapeDtypeStruct((share, width), F32),
-        scratch_shapes=[pltpu.VMEM((rows, width), F32)] + scatter_scratch(chunks, n // 2, rows, width),
-        compiler_params=pltpu.CompilerParams(collective_id=4, has_side_effects=True, vmem_limit_bytes=40 << 20),
-        cost_estimate=pl.CostEstimate(flops=2 * length * hw * width, bytes_accessed=1 << 23, transcendentals=0),
+        functools.partial(back_kernel, n=n, n_grp=n_grp, chunks=chunks, rows=rows),
+        in_specs=[vm, vm, hbm] + [vm] * 6, out_specs=[vm] * 5,
+        out_shape=[S((share, width), F32), S((block, hw), F32), S((block, pw), F32), S((8, width), F32),
+                   S((n, width), F32)],
+        scratch_shapes=[pltpu.VMEM((length, width), BF), pltpu.VMEM((width, hw), BF),
+                        pltpu.VMEM((n_grp - 1, block, hw), BF), pltpu.VMEM((n_grp - 1, block, pw), BF),
+                        pltpu.VMEM((rows, width), F32), pltpu.VMEM((1, hw), F32), pltpu.VMEM((8, width), F32), dma]
+                       + [dma((n_grp - 1,))] * 4 + scatter_scratch(chunks, n // 2, rows, width)
+                       + all_sum_scratch(n_grp, n, (8, width)) + all_sum_scratch(n_grp, n, (8, width // 4)),
+        compiler_params=pltpu.CompilerParams(collective_id=4, has_side_effects=True, vmem_limit_bytes=50 << 20),
+        cost_estimate=pl.CostEstimate(flops=4 * length * hw * width, bytes_accessed=1 << 24, transcendentals=0),
         name="project_back",
-    )(dproj.reshape(n, share, hw), w_attn)
+    )(dproj.reshape(n, share, hw), w_attn, n1, gw_proj, x_share, dh, gain, stats, up_sum)
 
 
 def attn_out(ctx, w_out, x_share, vec, n, chunks):
@@ -498,6 +688,7 @@
         stats[0:1, :] += jnp.sum(dn2 * xhat, 0, keepdims=True)
         stats[1:2, :] += jnp.sum(dn2, 0, keepdims=True)
         stats[2:3, :] += jnp.sum(d, 0, keepdims=True)
+        stats[3:4, :] += jnp.sum(gshare[r, :].astype(F32), 0, keepdims=True)
 
     def heads(c):
         y = dg(wide(c), w_out[...], 1, 0)
@@ -603,79 +794,10 @@
     )(n2, gradb.reshape(n, share, width), w_up, w_down, w_out, b_up, ctx, hidden, gshare, vec, live)
 
 
-def small_kernel(x_ref, a_ref, b_ref, gbuf, tbuf, gs, gr, ts, tr, *, n_grp, n_tp, a_rows):
-    t = lax.axis_index("tp")
-    g = lax.axis_index("grp")
-    bar = pltpu.get_barrier_semaphore()
-    for d in range(1, n_grp):
-        pl.semaphore_signal(bar, inc=1, device_id=(lax.rem(g + d, n_grp), t), device_id_type=MESH)
-    for d in range(1, n_tp):
-        pl.semaphore_signal(bar, inc=1, device_id=(g, lax.rem(t + d, n_tp)), device_id_type=MESH)
-    pl.semaphore_wait(bar, n_grp + n_tp - 2)
-    copies = []
-    for d in range(1, n_grp):
-        cp = pltpu.make_async_remote_copy(
-            x_ref, gbuf.at[g], gs.at[d], gr.at[d],
-            device_id=(lax.rem(g + d, n_grp), t), device_id_type=MESH)
-        cp.start()
-        copies.append(cp)
-    gbuf[g] = x_ref[...]
-    for cp in copies:
-        cp.wait()
-    total = gbuf[0]
-    for i in range(1, n_grp):
-        total = total + gbuf[i]
-    tbuf[t] = total
-    copies = []
-    for d in range(1, n_tp):
-        cp = pltpu.make_async_remote_copy(
-            tbuf.at[t], tbuf.at[t], ts.at[d], tr.at[d],
-            device_id=(g, lax.rem(t + d, n_tp)), device_id_type=MESH)
-        cp.start()
-        copies.append(cp)
-    for cp in copies:
-        cp.wait()
-    total = tbuf[0, :a_rows]
-    for i in range(1, n_tp):
-        total = total + tbuf[i, :a_rows]
-    a_ref[...] = total
-    b_ref[...] = tbuf[:, a_rows:]
-
-
-def small_sum(common, own):
-    n_grp, n_tp = lax.axis_size("grp"), lax.axis_size("tp")
-    a_rows = common.shape[0] // 128
-    own_rows = own.shape[0] // 128
-    pad = -own_rows % 8
-    x = jnp.concatenate([common, own, jnp.zeros((pad * 128,), F32)]).reshape(-1, 128)
-    rows = x.shape[0]
-    vm = pl.BlockSpec(memory_space=pltpu.VMEM)
-    a, b = pl.pallas_call(
-        functools.partial(small_kernel, n_grp=n_grp, n_tp=n_tp, a_rows=a_rows),
-        in_specs=[vm], out_specs=[vm, vm],
-        out_shape=[jax.ShapeDtypeStruct((a_rows, 128), F32),
-                   jax.ShapeDtypeStruct((n_tp, rows - a_rows, 128), F32)],
-        scratch_shapes=[pltpu.VMEM((n_grp, rows, 128), F32), pltpu.VMEM((n_tp, rows, 128), F32),
-                        pltpu.SemaphoreType.DMA((n_grp,)), pltpu.SemaphoreType.DMA((n_grp,)),
-                        pltpu.SemaphoreType.DMA((n_tp,)), pltpu.SemaphoreType.DMA((n_tp,))],
-        compiler_params=pltpu.CompilerParams(collective_id=1, has_side_effects=True),
-        name="small_sum",
-    )(x)
-    return a.reshape(-1), b.reshape(n_tp, -1)[:, : own.shape[0]]
-
-
 def normalize(rows, gain, bias):
     mean_row = jnp.mean(rows, -1, keepdims=True)
     centred = rows - mean_row
-    inverse = lax.rsqrt(jnp.mean(centred * centred, -1, keepdims=True) + 1e-05)
-    normed = centred * inverse
-    return normed * gain + bias, normed, inverse
-
-
-def norm_back(grad_norm, normed, inverse, gain):
-    scaled = grad_norm * gain
-    inner = jnp.mean(scaled, -1, keepdims=True) + normed * jnp.mean(scaled * normed, -1, keepdims=True)
-    return inverse * (scaled - inner)
+    return centred * lax.rsqrt(jnp.mean(centred * centred, -1, keepdims=True) + 1e-05) * gain + bias
 
 
 def on_device(layer_input, out_cotangent, seq_group, seq_len, w_qkv, b_qv, w_out, b_out, w_up, b_up,
@@ -713,10 +835,8 @@
         return lax.dynamic_slice_in_dim(x, row0, share, 0)
 
     x = layer_input.astype(F32)
-    n1 = normalize(x, first_norm_gain, first_norm_bias)[0].astype(BF)
+    n1 = normalize(x, first_norm_gain, first_norm_bias).astype(BF)
     x_share_b = mine(layer_input)
-    x_share = x_share_b.astype(F32)
-    _, xhat1, inverse1 = normalize(x_share, first_norm_gain, first_norm_bias)
 
     head_bias = lax.dynamic_slice_in_dim(b_qv.reshape(-1, 2, HD), tp * heads, heads, 0)
     bias_three = jnp.stack(
@@ -728,7 +848,6 @@
     up_bias = lax.dynamic_slice_in_dim(b_up, tp * hidden_here, hidden_here, 0)[None]
     gradb = jnp.where(live_all, out_cotangent, jnp.zeros_like(out_cotangent))
     gradb_share = mine(gradb)
-    grad_share = gradb_share.astype(F32)
     gw_ffn, gw_proj, dcontext, dh, result, stats, up_sum = feed_forward(
         n2_share, gradb, w_expand, w_reduce, w_proj, up_bias, context, hidden, gradb_share,
         jnp.stack([second_norm_gain, b_down]), live, n_tp, 8)
@@ -738,22 +857,13 @@
     grads_expand, grads_reduce = grads_ffn[:, :hidden_here], grads_ffn[:, hidden_here:]
 
     dproj = attn_bwd(info, proj, context, dcontext, lse)
-    gw_attn = dg(n1, dproj, 0, 0).astype(BF)
-    grads_late = scatter(jnp.concatenate([gw_attn, gw_proj], 1)).astype(F32)
-    grads_attn, grads_proj = grads_late[:, :gw_attn.shape[1]], grads_late[:, gw_attn.shape[1]:]
-    dn1 = project_back(dproj, w_attn, n_tp, 8)
-    grad_x = dh + norm_back(dn1, xhat1, inverse1, first_norm_gain)
-
-    proj_sums = jnp.sum(dproj.astype(F32), 0).reshape(heads, 3, HD)
-    own = jnp.concatenate([jnp.stack([proj_sums[:, 0], proj_sums[:, 2]], 1).reshape(-1),
-                           up_sum[0]])
-    common = jnp.concatenate([stats[2]] + [jnp.sum(v, 0) for v in (grad_share, dn1 * xhat1, dn1)]
-                             + [stats[0], stats[1]])
-    sums, owned = small_sum(common, own)
-    sums = sums.reshape(6, width)
+    grad_x, grads_attn, grads_proj, sums, owned = project_back(
+        dproj, w_attn, n1, gw_proj, x_share_b, dh, first_norm_gain[None], stats, up_sum,
+        n_tp, lax.axis_size("grp"), 8)
     qv = heads * 2 * HD
-    return (result, grad_x, grads_attn, owned[:, :qv].reshape(-1), grads_proj, sums[0], grads_expand,
-            owned[:, qv:].reshape(-1), grads_reduce, sums[1], sums[2], sums[3], sums[4], sums[5])
+    return (result, grad_x, grads_attn, owned[:, hidden_here:hidden_here + qv].reshape(-1), grads_proj, sums[2],
+            grads_expand, owned[:, :hidden_here].reshape(-1), grads_reduce, sums[3], sums[4], sums[5],
+            sums[0], sums[1])
 
 
 def solution(mesh):

time: 654 us -> 591 us (0.904); the launches traced: 644 us -> 590 us
  waiting for transfers between devices: 61.8 us -> 31.4 us
  other arithmetic: 51.3 us -> 39.3 us
  matrix products: 21.5 us -> 10 us
    all_gather x1, waiting for transfers between devices: 27.8 us -> 0.01 us  [on_device(): w_expand = lax.all_gather(w_up.astype(BF), 'grp', axis=0, tiled=True)]
    all_gather x1, waiting for transfers between devices: 0.01 us -> 26.8 us  [on_device(): w_reduce = lax.all_gather(w_down.astype(BF), 'grp', axis=0, tiled=True)]
    reduce_scatter x1, waiting for transfers between devices: 23.6 us -> 0.01 us  [on_device(): grads_ffn = scatter(gw_ffn).astype(F32)]
    dot_general x1 -> x0, matrix products: 11.5 us -> none  [dg(): lax.dot_general(a, b, (((ca,), (cb,)), ((), ())), preferred_element_type=...]
    pallas_call x2 -> x1, Pallas kernels: 95.9 us -> 101 us  [project_back(): pl.pallas_call(functools.partial(back_kernel, n=n, n_grp=n_grp, chunks=ch...]
    unnamed x72 -> x62, local copies, waits for them, and re-layouts: 21.6 us -> 18.8 us
  transfers between devices with their start and end apart: 6 -> 5, of which waited for: 4 -> 2; matrix products, arithmetic and copies ran while one was open for 10% -> 9% of each run, Pallas kernels for 30% -> 37%
where the time goes in v4:
time: 591 us; the launch traced here: 590 us
  Pallas kernels  466 us (79%)
  other arithmetic  39.3 us (7%)
  waiting for transfers between devices  31.4 us (5%)
  local copies, waits for them, and re-layouts  29.4 us (5%)
  between operations  14.1 us (2%)
  matrix products  10 us (2%)
    pallas_call x1, Pallas kernels, feed_forward(): pl.pallas_call(functools.partial(ffn_kernel, n=n, chunks=chunks, rows=row...  248 us
    pallas_call x1, Pallas kernels, project_back(): pl.pallas_call(functools.partial(back_kernel, n=n, n_grp=n_grp, chunks=ch...  101 us
    pallas_call x1, Pallas kernels, attn_out(): pl.pallas_call(functools.partial(out_kernel, n=n, chunks=chunks, rows=row...  78.9 us
    all_gather x1, waiting for transfers between devices, on_device(): w_reduce = lax.all_gather(w_down.astype(BF), 'grp', axis=0, tiled=True)  26.8 us
    pallas_call x1, Pallas kernels, attn_bwd(): pl.pallas_call(functools.partial(attn_bwd_kernel, nb=nb), grid_spec=pltpu...  21.6 us
    unnamed x62, local copies, waits for them, and re-layouts  18.8 us
    pallas_call x1, Pallas kernels, attn_fwd(): pl.pallas_call(functools.partial(attn_fwd_kernel, nb=nb), grid_spec=pltpu...  16.4 us
  transfers between devices with their start and end apart: 5, of which 2 were waited for; matrix products, arithmetic and copies ran while one was open for 9% of the time, Pallas kernels for 37%

profile of v4, /device:TPU:0, one launch (start us, length us, event | category | flops | bytes accessed | tf_op | source)
XLA Modules:
  0.0 589.9 jit_solution(1331178627965999672)
XLA Ops:
  7.3 2.5 convert_element_type.51
  9.8 1.8 convert_element_type.53
  11.7 2.7 convert_element_type.54
  14.5 1.1 convert_element_type.55
  17.0 1.3 fusion.6.live
  19.7 5.1 convert_reduce_fusion
  24.9 5.7 fusion.2
  30.6 1.3 dynamic_slice.14
  32.6 1.3 constant_dynamic-slice_fusion.2.x_share
  33.9 7.7 %broadcast_select_fusion = bf16[2048,2048]{1,0:T(8,128)(2,1)} fusion(bf16[2048,2048]{1,0:T(8,128)(2,1)} %param.17, pred[2048]{0:T(1024)(128)(4,1)S(1)} %iota_compare_fusion), kind=kLoop, calls=%fused_computation.8 | loop fusion | flops 4194304 | bytes 16779264 | tf_op jit(solution)/shard_map/jit(_where)/select_n | solution.py:849
  41.6 2.3 constant_dynamic-slice_fusion.1.gshare
  43.9 8.9 %fusion.5.n1_hbm = bf16[2048,2048]{1,0:T(8,128)(2,1)} fusion(bf16[2048,2048]{1,0:T(8,128)(2,1)} %param.16, f32[2048]{0:T(1024)S(1)} %copy-done.21, f32[2048]{0:T(1024)S(1)} %copy-done.4, f32[2048]{0:T(1024)S(1)} %add_rsqrt_fusion, f32[2048]{0:T(1024)S(1)} %broadcast_multiply_fusion), kind=kLoop, calls=%fused_computation.7 | loop fusion | flops 25165824 | bytes 16809984 | tf_op jit(solution)/shard_map/convert_element_type | solution.py:838
  52.8 4.4 all-gather.5.cloned.1.call-done.w_attn
  57.2 10.0 %add_convert_fusion.q_ref.k_ref.v_ref = bf16[2048,768]{1,0:T(8,128)(2,1)S(1)} fusion(f32[768]{0:T(1024)S(1)} %add.71, bf16[2048,2048]{1,0:T(8,128)(2,1)} %fusion.5.n1_hbm, bf16[2048,768]{1,0:T(8,128)(2,1)} %all-gather.5.cloned.1.call-done.w_attn), kind=kOutput, calls=%fused_computation.9 | convolution fusion | flops 6445596672 | bytes 14683136 | tf_op jit(solution)/shard_map/dot_general | solution.py:844
  67.2 16.4 %attn_fwd.1 = (bf16[2048,256]{1,0:T(8,128)(2,1)S(1)}, f32[2,1,2048]{2,1,0:T(1,128)S(1)}) custom-call(s32[3,4]{1,0:T(4,128)S(1)} %pad_add_fusion.info, bf16[2048,768]{1,0:T(8,128)(2,1)S(1)} %add_convert_fusion.q_ref.k_ref.v_ref, bf16[2048,768]{1,0:T(8,128)(2,1)S(1)} %add_convert_fusion.q_ref.k_ref.v_ref, bf16[2048,768]{1,0:T(8,128)(2,1)S(1)} %add_convert_fusion.q_ref.k_ref.v_ref), custom_call_target="tpu_custom_call" | custom-call | flops 2147483648 | bytes 4194304 | tf_op jit(solution)/shard_map/attn_fwd/pallas_call | solution.py:53
  83.6 1.7 copy-done
  86.3 1.2 copy-done.5
  87.5 1.2 copy-done.7
  88.7 78.9 %attn_out.1 = (f32[256,2048]{1,0:T(8,128)S(1)}, bf16[256,2048]{1,0:T(8,128)(2,1)S(1)}) custom-call(bf16[8,256,256]{2,1,0:T(8,128)(2,1)S(1)} %bitcast.33, bf16[2048,256]{1,0:T(8,128)(2,1)S(1)} %copy-done.5, bf16[256,2048]{1,0:T(8,128)(2,1)S(1)} %constant_dynamic-slice_fusion.2.x_share, f32[3,2048]{1,0:T(4,128)S(1)} %pad_maximum_fusion.vec), custom_call_target="tpu_custom_call" | custom-call | flops 2147483648 | bytes 8388608 | tf_op jit(solution)/shard_map/attn_out/pallas_call | solution.py:596
  167.6 1.3 copy-done.11
  169.9 26.8 %all-gather.11.cloned.1.call-done.w_down = bf16[2048,1024]{1,0:T(8,128)(2,1)} async-done(((bf16[512,1024]{1,0:T(8,128)(2,1)}), bf16[2048,1024]{1,0:T(8,128)(2,1)}) %all-gather.11.cloned.1.call-update) | async-done | bytes 4194320 | tf_op jit(solution)/shard_map/all_gather | solution.py:816
  196.7 247.8 %feed_forward.1 = (bf16[2048,2048]{1,0:T(8,128)(2,1)}, bf16[2048,256]{1,0:T(8,128)(2,1)}, bf16[8,256,256]{2,1,0:T(8,128)(2,1)}, f32[256,2048]{1,0:T(8,128)}, bf1...) custom-call(bf16[256,2048]{1,0:T(8,128)(2,1)} %copy-done.12, bf16[8,256,2048]{2,1,0:T(8,128)(2,1)} %bitcast.36, ...), custom_call_target="tpu_custom_call" | custom-call | flops 51539607552 | bytes 67108864 | tf_op jit(solution)/shard_map/feed_forward/pallas_call | solution.py:780
  444.6 1.9 copy-done.1
  446.4 1.2 copy-done.8
  447.7 1.2 copy-done.10
  448.9 21.6 %attn_bwd.1 = bf16[2048,768]{1,0:T(8,128)(2,1)S(1)} custom-call(s32[3,4]{1,0:T(4,128)S(1)} %pad_add_fusion.info, bf16[2048,768]{1,0:T(8,128)(2,1)S(1)} %copy-done.1, bf16[2048,768]{1,0:T(8,128)(2,1)S(1)} %copy-done.1, bf16[2048,768]{1,0:T(8,128)(2,1)S(1)} %copy-done.1, bf16[2048,256]{1,0:T(8,128)(2,1)S(1)} %copy-done.8, bf16[2048,256]{1,0:T(8,128)(2,1)S(1)} %bitcast.35, ...), custom_call_target="tpu_custom_call" | custom-call | flops 5368709120 | bytes 8388608 | tf_op jit(solution)/shard_map/attn_bwd/pallas_call | solution.py:103
  470.5 1.6 copy-done.9
  472.1 101.0 %project_back.1 = (f32[256,2048]{1,0:T(8,128)}, f32[512,768]{1,0:T(8,128)}, f32[512,256]{1,0:T(8,128)S(1)}, f32[8,2048]{1,0:T(8,128)S(1)}, f32[8,2048]{1,0:T(8,128)S(1)}) custom-call(bf16[8,256,768]{2,1,0:T(8,128)(2,1)} %bitcast.34, bf16[2048,768]{1,0:T(8,128)(2,1)} %all-gather.5.cloned.1.call-done.w_attn, bf16[2048,2048]{1,0:T(8,128)(2,1)} %fusion.5.n1_hbm, ...), custom_call_target="tpu_custom_call" | custom-call | flops 12884901888 | bytes 16777216 | tf_op jit(solution)/shard_map/project_back/pallas_call | solution.py:575
  575.0 4.2 fusion.9
  579.2 1.0 copy.42
  580.2 1.3 copy.43
  581.5 1.1 copy.44
  (82 shorter events, 8.3 us)
Async XLA Ops:
  7.2 7.3 %copy-start.16 = (f32[512,1024]{1,0:T(8,128)S(1)}, f32[512,1024]{1,0:T(8,128)}, u32[]{:S(2)}) copy-start(f32[512,1024]{1,0:T(8,128)} %param.26) | copy-start | bytes 6291460
  7.2 8.5 %copy-start.25 = (s32[6]{0:T(128)S(1)}, s32[6]{0:T(128)}, u32[]{:S(2)}) copy-start(s32[6]{0:T(128)} %param.19) | copy-start | bytes 76
  7.2 8.5 %copy-start.26 = (s32[6]{0:T(128)S(1)}, s32[6]{0:T(128)}, u32[]{:S(2)}) copy-start(s32[6]{0:T(128)} %param.18) | copy-start | bytes 76
  7.2 50.0 %all-gather.5.cloned.1.call-start = ((), (), s32[]{:S(2)}) async-start(), calls=%async_computation.1 | async-start | bytes 3932160 | tf_op jit(solution)/shard_map/all_gather | solution.py:813
  9.8 76.5 %all-gather.7.cloned.1.call-start = ((), (), s32[]{:S(2)}) async-start(), calls=%async_computation.2 | async-start | bytes 1310720 | tf_op jit(solution)/shard_map/all_gather | solution.py:814
  11.6 158.3 %all-gather.9.cloned.1.call-start = ((), (), s32[]{:S(2)}) async-start(), calls=%async_computation.3 | async-start | bytes 5242880 | tf_op jit(solution)/shard_map/all_gather | solution.py:815
  14.4 182.3 %all-gather.11.cloned.1.call-start = ((), (), s32[]{:S(2)}) async-start(), calls=%async_computation.4 | async-start | bytes 5242880 | tf_op jit(solution)/shard_map/all_gather | solution.py:816
  15.7 559.4 %reduce-scatter.2.cloned.1.call-start = ((), (), s32[]{:S(2)}) async-start(), calls=%async_computation.5 | async-start | bytes 10485760 | tf_op jit(solution)/shard_map/reduce_scatter | solution.py:856
  19.7 12.2 %copy-start.20 = (f32[2048]{0:T(1024)S(1)}, f32[2048]{0:T(1024)}, u32[]{:S(2)}) copy-start(f32[2048]{0:T(1024)} %param.30) | copy-start | bytes 24580
  19.7 12.2 %copy-start.24 = (f32[2048]{0:T(1024)S(1)}, f32[2048]{0:T(1024)}, u32[]{:S(2)}) copy-start(f32[2048]{0:T(1024)} %param.27) | copy-start | bytes 24580
  19.7 12.8 %copy-start.22 = (f32[2048]{0:T(1024)S(1)}, f32[2048]{0:T(1024)}, u32[]{:S(2)}) copy-start(f32[2048]{0:T(1024)} %param.31) | copy-start | bytes 24580
  19.7 12.8 %copy-start.23 = (f32[2048]{0:T(1024)S(1)}, f32[2048]{0:T(1024)}, u32[]{:S(2)}) copy-start(f32[2048]{0:T(1024)} %param.23) | copy-start | bytes 24580
  33.9 52.4 %copy-start.2 = (bf16[256,2048]{1,0:T(8,128)(2,1)}, bf16[256,2048]{1,0:T(8,128)(2,1)S(1)}, u32[]{:S(2)}) copy-start(bf16[256,2048]{1,0:T(8,128)(2,1)S(1)} %constant_dynamic-slice_fusion.2.x_share) | copy-start | bytes 3145732
  33.9 10.1 %copy-start.4 = (f32[2048]{0:T(1024)S(1)}, f32[2048]{0:T(1024)}, u32[]{:S(2)}) copy-start(f32[2048]{0:T(1024)} %param.28) | copy-start | bytes 24580
  33.9 10.0 %copy-start.21 = (f32[2048]{0:T(1024)S(1)}, f32[2048]{0:T(1024)}, u32[]{:S(2)}) copy-start(f32[2048]{0:T(1024)} %param.29) | copy-start | bytes 24580
  83.6 1.7 copy-start
  85.3 1.0 copy-start.6
  86.3 1.2 copy-start.5
  87.5 1.2 copy-start.7
  167.6 1.3 copy-start.11
  168.9 1.0 copy-start.12
  444.6 1.9 copy-start.1
  446.4 1.2 copy-start.8
  447.7 1.2 copy-start.10
  448.9 23.2 %copy-start.3 = (bf16[256,2048]{1,0:T(8,128)(2,1)S(1)}, bf16[256,2048]{1,0:T(8,128)(2,1)}, u32[]{:S(2)}) copy-start(bf16[256,2048]{1,0:T(8,128)(2,1)} %copy-done.2) | copy-start | bytes 3145732
  448.9 23.2 %copy-start.13 = (bf16[2048,256]{1,0:T(8,128)(2,1)S(1)}, bf16[2048,256]{1,0:T(8,128)(2,1)}, u32[]{:S(2)}) copy-start(bf16[2048,256]{1,0:T(8,128)(2,1)} %get-tuple-element.36.gw_proj) | copy-start | bytes 3145732
  448.9 23.2 %copy-start.14 = (f32[8,2048]{1,0:T(8,128)S(1)}, f32[8,2048]{1,0:T(8,128)}, u32[]{:S(2)}) copy-start(f32[8,2048]{1,0:T(8,128)} %get-tuple-element.38.stats) | copy-start | bytes 196612
  448.9 23.2 %copy-start.15 = (f32[1,1024]{1,0:T(1,128)S(1)}, f32[1,1024]{1,0:T(1,128)}, u32[]{:S(2)}) copy-start(f32[1,1024]{1,0:T(1,128)} %get-tuple-element.39.up_sum) | copy-start | bytes 12292
  470.5 1.6 copy-start.9
  573.1 7.0 %copy-start.17 = (f32[256,2048]{1,0:T(8,128)S(1)}, f32[256,2048]{1,0:T(8,128)}, u32[]{:S(2)}) copy-start(f32[256,2048]{1,0:T(8,128)} %get-tuple-element.80) | copy-start | bytes 6291460
  575.0 4.2 copy-start.19
  575.0 6.5 %copy-start.18 = (f32[512,768]{1,0:T(8,128)S(1)}, f32[512,768]{1,0:T(8,128)}, u32[]{:S(2)}) copy-start(f32[512,768]{1,0:T(8,128)} %get-tuple-element.81) | copy-start | bytes 4718596
Sparse Core Ops, SparseCore 0:
  10.5 46.6 all-gather.4
  59.6 26.6 all-gather.6
  88.7 52.8 all-gather.8
  143.9 52.7 all-gather.10
  444.7 124.5 reduce-scatter.1

commit v5 on v4

--- a/solution.py
+++ b/solution.py
@@ -16,11 +16,26 @@
 def dg(a,b,ca,cb):
     return lax.dot_general(a,b,(((ca,),(cb,)),((),())),preferred_element_type=F32)
 
-def attn_fwd_kernel(info, q_ref, k_ref, v_ref, o_ref, lse_ref, *, nb):
+def block_info(grps, lens, nb, seqs):
+    g = lax.axis_index("grp")
+    found = [[jnp.int32(0), jnp.int32(0), jnp.int32(0)] for _ in range(nb)]
+    start = jnp.int32(0)
+    for s in range(seqs):
+        count = jnp.where(grps[s] == g, lens[s] // BLK, 0)
+        for b in range(nb):
+            hit = (start <= b) & (b < start + count)
+            found[b] = [jnp.where(hit, start, found[b][0]), jnp.where(hit, start + count - 1, found[b][1]),
+                        jnp.where(hit, 1, found[b][2])]
+        start = start + count
+    return found
+
+
+def attn_fwd_kernel(grps, lens, q_ref, k_ref, v_ref, o_ref, lse_ref, *, nb, seqs):
+    info = block_info(grps, lens, nb, seqs)
     c = HD ** -0.5 * LOG2E
     for qi in range(nb):
         rows = pl.ds(qi*BLK, BLK)
-        @pl.when(info[2, qi] > 0)
+        @pl.when(info[qi][2] > 0)
         def _():
             q = q_ref[rows, :]
             def step(j, carry, diag=False):
@@ -39,27 +54,28 @@
                 return mn, l, acc
             init = (jnp.full((1, BLK), -1e30, F32), jnp.zeros((1, BLK), F32), jnp.zeros((HD, BLK), F32))
             carry = step(qi, init, True)
-            m, l, acc = lax.fori_loop(info[0, qi], qi, step, carry)
+            m, l, acc = lax.fori_loop(info[qi][0], qi, step, carry)
             o_ref[rows, :] = jnp.transpose(acc / l).astype(BF)
             lse_ref[0, :, rows] = m*c + jnp.log2(l)
-        @pl.when(info[2, qi] <= 0)
+        @pl.when(info[qi][2] <= 0)
         def _():
             o_ref[rows, :] = jnp.zeros((BLK, HD), BF)
             lse_ref[0, :, rows] = jnp.zeros((1, BLK), F32)
 
-def attn_fwd(info, proj):
+def attn_fwd(grps, lens, proj):
     length = proj.shape[0]; heads = proj.shape[1]//(3*HD); nb = length//BLK
-    spec = lambda o: pl.BlockSpec((length, HD), lambda h, info: (0, 3*h+o))
-    return pl.pallas_call(functools.partial(attn_fwd_kernel, nb=nb),
-        grid_spec=pltpu.PrefetchScalarGridSpec(num_scalar_prefetch=1, grid=(heads,),
+    spec = lambda o: pl.BlockSpec((length, HD), lambda h, grps, lens: (0, 3*h+o))
+    return pl.pallas_call(functools.partial(attn_fwd_kernel, nb=nb, seqs=grps.shape[0]),
+        grid_spec=pltpu.PrefetchScalarGridSpec(num_scalar_prefetch=2, grid=(heads,),
             in_specs=[spec(0), spec(1), spec(2)],
-            out_specs=[pl.BlockSpec((length, HD), lambda h, info: (0, h)), pl.BlockSpec((1, 1, length), lambda h, info: (h, 0, 0))]),
+            out_specs=[pl.BlockSpec((length, HD), lambda h, grps, lens: (0, h)), pl.BlockSpec((1, 1, length), lambda h, grps, lens: (h, 0, 0))]),
         out_shape=[jax.ShapeDtypeStruct((length, heads*HD), BF), jax.ShapeDtypeStruct((heads, 1, length), F32)],
         compiler_params=pltpu.CompilerParams(vmem_limit_bytes=40<<20), name="attn_fwd",
         cost_estimate=pl.CostEstimate(flops=heads*length*length*HD*2, bytes_accessed=length*heads*HD*8, transcendentals=heads*length*length//2),
-    )(info, proj, proj, proj)
-
-def attn_bwd_kernel(info, q_ref, k_ref, v_ref, o_ref, do_ref, lse_ref, dp_ref, dq_sc, dl_sc, *, nb):
+    )(grps, lens, proj, proj, proj)
+
+def attn_bwd_kernel(grps, lens, q_ref, k_ref, v_ref, o_ref, do_ref, lse_ref, dp_ref, dq_sc, dl_sc, *, nb, seqs):
+    info = block_info(grps, lens, nb, seqs)
     sc = HD ** -0.5
     c = sc * LOG2E
     prod = do_ref[...].astype(F32) * o_ref[...].astype(F32)
@@ -67,7 +83,7 @@
     dq_sc[...] = jnp.zeros_like(dq_sc)
     for j in range(nb):
         kr = pl.ds(j*BLK, BLK)
-        @pl.when(info[2, j] > 0)
+        @pl.when(info[j][2] > 0)
         def _():
             k = k_ref[kr, :]; v = v_ref[kr, :]
             def step(i, carry, diag=False):
@@ -88,27 +104,27 @@
                 return dk, dv
             z = jnp.zeros((BLK, HD), F32)
             carry = step(j, (z, z), True)
-            dk, dv = lax.fori_loop(j+1, info[1, j]+1, step, carry)
+            dk, dv = lax.fori_loop(j+1, info[j][1]+1, step, carry)
             dp_ref[kr, HD:2*HD] = (dk*sc).astype(BF)
             dp_ref[kr, 2*HD:] = dv.astype(BF)
-        @pl.when(info[2, j] <= 0)
+        @pl.when(info[j][2] <= 0)
         def _():
             dp_ref[kr, HD:] = jnp.zeros((BLK, 2*HD), BF)
     dp_ref[:, :HD] = (dq_sc[...]*sc).astype(BF)
 
-def attn_bwd(info, proj, ctx, dctx, lse):
+def attn_bwd(grps, lens, proj, ctx, dctx, lse):
     length = proj.shape[0]; heads = proj.shape[1]//(3*HD); nb = length//BLK
-    spec = lambda o: pl.BlockSpec((length, HD), lambda h, info: (0, 3*h+o))
-    hs = pl.BlockSpec((length, HD), lambda h, info: (0, h))
-    return pl.pallas_call(functools.partial(attn_bwd_kernel, nb=nb),
-        grid_spec=pltpu.PrefetchScalarGridSpec(num_scalar_prefetch=1, grid=(heads,),
-            in_specs=[spec(0), spec(1), spec(2), hs, hs, pl.BlockSpec((1, 1, length), lambda h, info: (h, 0, 0))],
-            out_specs=pl.BlockSpec((length, 3*HD), lambda h, info: (0, h)),
+    spec = lambda o: pl.BlockSpec((length, HD), lambda h, grps, lens: (0, 3*h+o))
+    hs = pl.BlockSpec((length, HD), lambda h, grps, lens: (0, h))
+    return pl.pallas_call(functools.partial(attn_bwd_kernel, nb=nb, seqs=grps.shape[0]),
+        grid_spec=pltpu.PrefetchScalarGridSpec(num_scalar_prefetch=2, grid=(heads,),
+            in_specs=[spec(0), spec(1), spec(2), hs, hs, pl.BlockSpec((1, 1, length), lambda h, grps, lens: (h, 0, 0))],
+            out_specs=pl.BlockSpec((length, 3*HD), lambda h, grps, lens: (0, h)),
             scratch_shapes=[pltpu.VMEM((length, HD), F32), pltpu.VMEM((1, length), F32)]),
         out_shape=jax.ShapeDtypeStruct((length, heads*3*HD), BF),
         compiler_params=pltpu.CompilerParams(vmem_limit_bytes=40<<20), name="attn_bwd",
         cost_estimate=pl.CostEstimate(flops=heads*length*length*HD*5, bytes_accessed=length*heads*HD*16, transcendentals=heads*length*length//2),
-    )(info, proj, proj, proj, ctx, dctx, lse)
+    )(grps, lens, proj, proj, proj, ctx, dctx, lse)
 
 
 MESH = pl.DeviceIdType.MESH
@@ -124,8 +140,9 @@
         self.right, self.left, self.sib = (self.g, t + 2), (self.g, t - 2), (self.g, t + 1 - 2 * self.k)
         self.has_right, self.has_left = self.z < self.Z - 1, self.z > 0
 
-    def barrier(self):
+    def barrier(self, n_grp=0):
         bar = pltpu.get_barrier_semaphore()
+        extra = grp_signal(self, n_grp) if n_grp else 0
         pl.semaphore_signal(bar, inc=1, device_id=self.sib, device_id_type=MESH)
 
         @pl.when(self.has_right)
@@ -136,7 +153,7 @@
         def _():
             pl.semaphore_signal(bar, inc=1, device_id=self.left, device_id_type=MESH)
 
-        amount = 1 + jnp.where(self.has_right, 1, 0) + jnp.where(self.has_left, 1, 0)
+        amount = 1 + extra + jnp.where(self.has_right, 1, 0) + jnp.where(self.has_left, 1, 0)
         pl.semaphore_wait(bar, amount)
 
 
@@ -282,6 +299,73 @@
                     self.line(c, side, h, at.z).wait_send()
 
 
+class GroupGather:
+    def __init__(self, at, n_grp, full, ss, sr):
+        self.at, self.full, self.ss, self.sr = at, full, ss, sr
+        self.P = n_grp // 2
+        self.size = full.shape[0] // n_grp
+        self.p, self.q = at.g // 2, lax.rem(at.g, 2)
+        self.partner = (at.g + 1 - 2 * self.q, at.t)
+
+    def peer(self, j):
+        return lax.rem(self.p + j, self.P)
+
+    def rows(self, p, q, half=None):
+        size = self.size if half is None else self.size // 2
+        first = (2 * p + q) * self.size + (size if half == 1 else 0)
+        return self.full.at[pl.ds(pl.multiple_of(first, size), size), :]
+
+    def copy(self, kind, j, incoming=False):
+        p, q = self.p, self.q
+        src = lax.rem(p + self.P - j, self.P)
+        if kind == 0:
+            b, k, dev = self.rows(p, 1 - q if incoming else q), 0, self.partner
+        elif kind == 1:
+            b, k, dev = self.rows(src if incoming else p, q), j, (2 * self.peer(j) + q, self.at.t)
+        elif kind == 2:
+            b, k = self.rows(src if incoming else p, 1 - q, 1), self.P - 1 + j
+            dev = (2 * self.peer(j) + q, self.at.t)
+        else:
+            b, k = self.rows(src, 1 - q if incoming else q, 0), 2 * (self.P - 1) + j
+            dev = self.partner
+        return remote(b, b, self.ss.at[k], self.sr.at[k], dev)
+
+    def start(self):
+        self.copy(0, 0).start()
+        for j in range(1, self.P):
+            self.copy(1, j).start()
+
+    def forward(self):
+        self.copy(0, 0, True).wait_recv()
+        for j in range(1, self.P):
+            self.copy(2, j).start()
+        for j in range(1, self.P):
+            self.copy(1, j, True).wait_recv()
+            self.copy(3, j).start()
+
+    def finish(self):
+        for j in range(1, self.P):
+            for kind in (2, 3):
+                self.copy(kind, j, True).wait_recv()
+                self.copy(kind, j).wait_send()
+            self.copy(1, j).wait_send()
+        self.copy(0, 0).wait_send()
+
+
+def group_sems(n_grp):
+    k = 1 + 3 * (n_grp // 2 - 1)
+    return [pltpu.SemaphoreType.DMA((k,)), pltpu.SemaphoreType.DMA((k,))]
+
+
+def grp_signal(at, n_grp):
+    bar = pltpu.get_barrier_semaphore()
+    p, q = at.g // 2, lax.rem(at.g, 2)
+    pl.semaphore_signal(bar, inc=1, device_id=(at.g + 1 - 2 * q, at.t), device_id_type=MESH)
+    for j in range(1, n_grp // 2):
+        pl.semaphore_signal(bar, inc=1, device_id=(2 * lax.rem(p + j, n_grp // 2) + q, at.t), device_id_type=MESH)
+    return n_grp // 2
+
+
 def gather_sems(chunks, Z):
     dma = pltpu.SemaphoreType.DMA
     return [dma((chunks, 2, Z - 1)), dma((chunks, 2, Z - 1)), dma((chunks, Z)), dma((chunks, Z))]
@@ -321,7 +405,7 @@
     return centred * inverse, inverse
 
 
-def product_scatter(at, rs, lhs_ref, w_ref, total, chunks, rows, epilogue):
+def product_scatter(at, rs, lhs_ref, w_ref, total, chunks, rows, epilogue, extra):
     def product(c):
         lhs = lhs_ref[:, chunk_rows(c, rows), :].reshape(at.n * rows, lhs_ref.shape[2])
 
@@ -354,14 +438,29 @@
         def _():
             rs.finish(e, total)
             epilogue(e)
+        extra(i)
         return carry
 
     lax.fori_loop(0, chunks + 2, tick, 0)
 
 
-def out_kernel(ctx, w_out, x_share, vec, hidden, n2, total, *sc, n, chunks, rows):
+def out_kernel(ctx, w_out, vec, x_hbm, up16, down16, hidden, n2, up_hbm, down_hbm,
+               x_share, total, lsem, *sc, n, n_grp, chunks, rows):
     at = Place(n)
-    at.barrier()
+    load = pltpu.make_async_copy(x_hbm.at[at.t], x_share, lsem.at[0])
+    load.start()
+    up, down = GroupGather(at, n_grp, up_hbm, *sc[:2]), GroupGather(at, n_grp, down_hbm, *sc[2:4])
+    own = chunk_rows(at.g, up.size)
+    put_up = pltpu.make_async_copy(up16, up_hbm.at[own, :], lsem.at[1])
+    put_down = pltpu.make_async_copy(down16, down_hbm.at[own, :], lsem.at[2])
+    put_up.start()
+    put_down.start()
+    at.barrier(n_grp)
+    load.wait()
+    put_up.wait()
+    put_down.wait()
+    up.start()
+    down.start()
 
     def epilogue(c):
         r = chunk_rows(c, rows)
@@ -369,7 +468,138 @@
         hidden[r, :] = h
         n2[r, :] = (rows_stats(h)[0] * vec[1:2, :] + vec[2:3, :]).astype(BF)
 
-    product_scatter(at, Scatter(at, *sc), ctx, w_out, total, chunks, rows, epilogue)
+    def extra(i):
+        @pl.when(i == chunks // 2)
+        def _():
+            up.forward()
+
+        @pl.when(i == chunks - 1)
+        def _():
+            down.forward()
+
+    product_scatter(at, Scatter(at, *sc[4:]), ctx, w_out, total, chunks, rows, epilogue, extra)
+    up.finish()
+    down.finish()
+
+
+def attn_out(ctx, w_out, vec, x, up16, down16, n, n_grp, chunks):
+    length, hw = ctx.shape
+    width = x.shape[1]
+    share = length // n
+    rows = share // chunks
+    hid = up16.shape[1]
+    vm, hbm = pl.BlockSpec(memory_space=pltpu.VMEM), pl.BlockSpec(memory_space=pl.ANY)
+    S = jax.ShapeDtypeStruct
+    return pl.pallas_call(
+        functools.partial(out_kernel, n=n, n_grp=n_grp, chunks=chunks, rows=rows),
+        in_specs=[vm] * 3 + [hbm] * 3, out_specs=[vm] * 2 + [hbm] * 2,
+        out_shape=[S((share, width), F32), S((share, width), BF), S((width, hid), BF), S((width, hid), BF)],
+        scratch_shapes=[pltpu.VMEM((share, width), BF), pltpu.VMEM((rows, width), F32), pltpu.SemaphoreType.DMA((3,))]
+                       + group_sems(n_grp) * 2 + scatter_scratch(chunks, n // 2, rows, width),
+        compiler_params=pltpu.CompilerParams(collective_id=2, has_side_effects=True, vmem_limit_bytes=40 << 20),
+        cost_estimate=pl.CostEstimate(flops=2 * length * hw * width, bytes_accessed=1 << 23, transcendentals=0),
+        name="attn_out",
+    )(ctx.reshape(n, share, hw), w_out, vec, x.reshape(n, share, width), up16, down16)
+
+
+def front_kernel(x_hbm, w_qkv, w_out, w_up, w_down, vec, bias_hbm, proj, n1_hbm, w_attn, w_proj, up16, down16,
+                 xbuf, n1, acc, bias, xsem, osem, bsem, *sc, n, n_grp, parts):
+    at = Place(n)
+    width, hw = w_attn.shape
+    block = width // n_grp
+    length = n1.shape[0]
+    rows = length // parts
+    heads = hw // (3 * HD)
+
+    def fetch(i):
+        slot = lax.rem(i, 2)
+        return pltpu.make_async_copy(x_hbm.at[chunk_rows(i, rows), :], xbuf.at[slot], xsem.at[slot])
+
+    def put(i):
+        r = chunk_rows(i, rows)
+        return pltpu.make_async_copy(n1.at[r, :], n1_hbm.at[r, :], osem)
+
+    get_bias = pltpu.make_async_copy(bias_hbm.at[at.t], bias, bsem)
+    get_bias.start()
+    fetch(0).start()
+    own = chunk_rows(at.g, block)
+    w_attn[own, :] = w_qkv[...].astype(BF)
+    bar = pltpu.get_barrier_semaphore()
+    pl.semaphore_wait(bar, grp_signal(at, n_grp))
+    qkv, out = GroupGather(at, n_grp, w_attn, *sc[:2]), GroupGather(at, n_grp, w_proj, *sc[2:])
+    qkv.start()
+    w_proj[own, :] = w_out[...].astype(BF)
+    up16[...] = w_up[...].astype(BF)
+    down16[...] = w_down[...].astype(BF)
+
+    def norm(i):
+        fetch(i).wait()
+
+        @pl.when(i + 1 < parts)
+        def _():
+            fetch(i + 1).start()
+        y = rows_stats(xbuf[lax.rem(i, 2)].astype(F32))[0] * vec[0:1, :] + vec[1:2, :]
+        n1[chunk_rows(i, rows), :] = y.astype(BF)
+        put(i).start()
+    tiles(parts, norm)
+
+    def partial(b, first=False, last=False):
+        r = chunk_rows(b, block)
+
+        def tile(i):
+            m = chunk_rows(i, rows)
+            y = dg(n1[m, r], w_attn[r, :], 1, 0)
+            if not first:
+                y = y + acc[m, :]
+            acc[m, :] = y
+        tiles(parts, tile)
+
+    p, q, P = at.g // 2, lax.rem(at.g, 2), n_grp // 2
+    partial(at.g, True)
+    qkv.forward()
+    out.start()
+    partial(2 * p + 1 - q)
+    for j in range(1, P):
+        partial(2 * lax.rem(p + j, P) + q)
+    out.forward()
+    qkv.finish()
+    for j in range(1, P):
+        partial(2 * lax.rem(p + j, P) + 1 - q)
+    get_bias.wait()
+
+    def write(i):
+        m = chunk_rows(i, rows)
+        for h in range(heads):
+            c = 3 * h * HD
+            proj[m, c:c + HD] = (acc[m, c:c + HD] + bias[:, 2 * h * HD:(2 * h + 1) * HD]).astype(BF)
+            c += HD
+            proj[m, c:c + HD] = acc[m, c:c + HD].astype(BF)
+            c += HD
+            proj[m, c:c + HD] = (acc[m, c:c + HD] + bias[:, (2 * h + 1) * HD:(2 * h + 2) * HD]).astype(BF)
+        put(i).wait()
+    tiles(parts, write)
+    out.finish()
+
+
+def front(x, w_qkv, w_out, w_up, w_down, vec, b_qv, n, n_grp):
+    length, width = x.shape
+    block, hw = w_qkv.shape
+    pw, hid = w_out.shape[1], w_up.shape[1]
+    parts = length // TILE
+    vm, hbm = pl.BlockSpec(memory_space=pltpu.VMEM), pl.BlockSpec(memory_space=pl.ANY)
+    S, dma = jax.ShapeDtypeStruct, pltpu.SemaphoreType.DMA
+    return pl.pallas_call(
+        functools.partial(front_kernel, n=n, n_grp=n_grp, parts=parts),
+        in_specs=[hbm] + [vm] * 5 + [hbm], out_specs=[vm, hbm] + [vm] * 4,
+        out_shape=[S((length, hw), BF), S((length, width), BF), S((width, hw), BF), S((width, pw), BF),
+                   S((block, hid), BF), S((block, hid), BF)],
+        scratch_shapes=[pltpu.VMEM((2, length // parts, width), BF), pltpu.VMEM((length, width), BF),
+                        pltpu.VMEM((length, hw), F32), pltpu.VMEM((1, b_qv.shape[0] // n), F32),
+                        dma((2,)), dma, dma] + group_sems(n_grp) * 2,
+        compiler_params=pltpu.CompilerParams(collective_id=5, has_side_effects=True, vmem_limit_bytes=50 << 20),
+        cost_estimate=pl.CostEstimate(flops=2 * length * hw * width, bytes_accessed=1 << 24, transcendentals=0),
+        name="front",
+    )(x, w_qkv, w_out, w_up, w_down, vec, b_qv.reshape(n, 1, -1))
 
 
 class AllSum:
@@ -419,17 +649,19 @@
             dma((n_grp - 1,)), dma((n_grp - 1,)), dma((n - 1,)), dma((n - 1,))]
 
 
-def back_kernel(dproj, w_attn, n1_hbm, gw_proj, x_share, dh, gain, stats, up_sum,
+def back_kernel(dproj, w_attn, n1_hbm, gw_proj, x_hbm, dh, gain, stats, up_sum,
                 grad_x, g_attn, g_proj, sums, owned,
-                n1, gw, got, got_proj, total, qv, ln_sum, nsem, ws, wr, ps, pr, *scratch, n, n_grp, chunks, rows):
+                n1, x_share, gw, got, got_proj, total, qv, ln_sum, nsem, ws, wr, ps, pr, *scratch, n, n_grp, chunks, rows):
     at = Place(n)
     width, hw = w_attn.shape
     block = width // n_grp
     per = block // TILE
     heads = hw // (3 * HD)
     hid = up_sum.shape[1]
-    load = pltpu.make_async_copy(n1_hbm, n1, nsem)
+    load = pltpu.make_async_copy(n1_hbm, n1, nsem.at[0])
     load.start()
+    load_x = pltpu.make_async_copy(x_hbm.at[at.t], x_share, nsem.at[1])
+    load_x.start()
     rs, early, late = Scatter(at, *scratch[:7]), AllSum(at, n_grp, *scratch[7:14]), AllSum(at, n_grp, *scratch[14:])
     bar = pltpu.get_barrier_semaphore()
     for d in range(1, n_grp):
@@ -492,6 +724,7 @@
         ln_sum[1:2, :] += jnp.sum(dn, 0, keepdims=True)
 
     load.wait()
+    load_x.wait()
 
     def tick(i, carry):
         c = i - 1
@@ -563,7 +796,7 @@
     sums[6:8, :] = jnp.zeros_like(sums[6:8, :])
 
 
-def project_back(dproj, w_attn, n1, gw_proj, x_share, dh, gain, stats, up_sum, n, n_grp, chunks):
+def project_back(dproj, w_attn, n1, gw_proj, x, dh, gain, stats, up_sum, n, n_grp, chunks):
     length, hw = dproj.shape
     width = w_attn.shape[0]
     share = length // n
@@ -574,39 +807,23 @@
     S, dma = jax.ShapeDtypeStruct, pltpu.SemaphoreType.DMA
     return pl.pallas_call(
         functools.partial(back_kernel, n=n, n_grp=n_grp, chunks=chunks, rows=rows),
-        in_specs=[vm, vm, hbm] + [vm] * 6, out_specs=[vm] * 5,
+        in_specs=[vm, vm, hbm, vm, hbm] + [vm] * 4, out_specs=[vm] * 5,
         out_shape=[S((share, width), F32), S((block, hw), F32), S((block, pw), F32), S((8, width), F32),
                    S((n, width), F32)],
-        scratch_shapes=[pltpu.VMEM((length, width), BF), pltpu.VMEM((width, hw), BF),
+        scratch_shapes=[pltpu.VMEM((length, width), BF), pltpu.VMEM((share, width), BF), pltpu.VMEM((width, hw), BF),
                         pltpu.VMEM((n_grp - 1, block, hw), BF), pltpu.VMEM((n_grp - 1, block, pw), BF),
-                        pltpu.VMEM((rows, width), F32), pltpu.VMEM((1, hw), F32), pltpu.VMEM((8, width), F32), dma]
+                        pltpu.VMEM((rows, width), F32), pltpu.VMEM((1, hw), F32), pltpu.VMEM((8, width), F32), dma((2,))]
                        + [dma((n_grp - 1,))] * 4 + scatter_scratch(chunks, n // 2, rows, width)
                        + all_sum_scratch(n_grp, n, (8, width)) + all_sum_scratch(n_grp, n, (8, width // 4)),
         compiler_params=pltpu.CompilerParams(collective_id=4, has_side_effects=True, vmem_limit_bytes=50 << 20),
         cost_estimate=pl.CostEstimate(flops=4 * length * hw * width, bytes_accessed=1 << 24, transcendentals=0),
         name="project_back",
-    )(dproj.reshape(n, share, hw), w_attn, n1, gw_proj, x_share, dh, gain, stats, up_sum)
-
-
-def attn_out(ctx, w_out, x_share, vec, n, chunks):
-    length, hw = ctx.shape
-    share, width = x_share.shape
-    rows = share // chunks
-    vm = pl.BlockSpec(memory_space=pltpu.VMEM)
-    return pl.pallas_call(
-        functools.partial(out_kernel, n=n, chunks=chunks, rows=rows),
-        in_specs=[vm] * 4, out_specs=[vm] * 2,
-        out_shape=[jax.ShapeDtypeStruct((share, width), F32), jax.ShapeDtypeStruct((share, width), BF)],
-        scratch_shapes=[pltpu.VMEM((rows, width), F32)] + scatter_scratch(chunks, n // 2, rows, width),
-        compiler_params=pltpu.CompilerParams(collective_id=2, has_side_effects=True, vmem_limit_bytes=40 << 20),
-        cost_estimate=pl.CostEstimate(flops=2 * length * hw * width, bytes_accessed=1 << 23, transcendentals=0),
-        name="attn_out",
-    )(ctx.reshape(n, share, hw), w_out, x_share, vec)
-
-
-def ffn_kernel(n2_hbm, gradb_hbm, w_up, w_down, w_out, b_up, ctx, hidden, gshare, vec, live,
+    )(dproj.reshape(n, share, hw), w_attn, n1, gw_proj, x.reshape(n, share, width), dh, gain, stats, up_sum)
+
+
+def ffn_kernel(n2_hbm, gradb_hbm, bias_hbm, w_up, w_down, w_out, ctx, hidden, vec, tokens,
                gw_hbm, gwo, dctx, dh, res, stats, bsum,
-               gat, acc_up, acc_down, gbuf, actb, dbb, total, lsem, gsem, msem, *scratch, n, chunks, rows):
+               gat, acc_up, acc_down, gbuf, actb, dbb, total, gshare, b_up, keep, lsem, gsem, msem, *scratch, n, chunks, rows):
     at = Place(n)
     ag1, ag2 = Gather(at, gat, rows, *scratch[:4]), Gather(at, gat, rows, *scratch[4:8])
     rs, mlp = Scatter(at, *scratch[8:15]), Scatter(at, *scratch[15:])
@@ -615,6 +832,17 @@
 
     load = pltpu.make_async_copy(n2_hbm, gat.at[at.t], lsem)
     load.start()
+    load_g = pltpu.make_async_copy(gradb_hbm.at[at.t], gshare, msem.at[0])
+    load_g.start()
+    load_b = pltpu.make_async_copy(bias_hbm.at[at.t], b_up, msem.at[1])
+    load_b.start()
+    share = hidden.shape[0]
+
+    def alive(ranks, first, c):
+        shape = (ranks, rows, 1)
+        place = ((first + lax.broadcasted_iota(jnp.int32, shape, 0)) * share + c * rows
+                 + lax.broadcasted_iota(jnp.int32, shape, 1))
+        return jnp.where(place < tokens[...].reshape(1, 1, 1), 1.0, 0.0).reshape(ranks * rows, 1)
 
     def fetch(c):
         slot = lax.rem(c, 2)
@@ -626,6 +854,8 @@
     stats[...] = jnp.zeros_like(stats)
     bsum[...] = jnp.zeros_like(bsum)
     load.wait()
+    load_g.wait()
+    load_b.wait()
     at.barrier()
 
     a0, a1 = 0.7978845608028654, 0.044715
@@ -640,6 +870,7 @@
         def _():
             fetch(c + 1).start()
         slot = lax.rem(c, 2)
+        keep[...] = alive(n, 0, c)
 
         def tile(i):
             v = dg(wide(c), w_up[:, cols(i)], 1, 0) + b_up[:, cols(i)]
@@ -647,9 +878,9 @@
             v2 = v * v
             th = jnp.tanh(a0 * (v + a1 * v2 * v))
             half = 0.5 * (1.0 + th)
-            actb[:, cols(i)] = (v * half).astype(BF)
+            actb[:, cols(i)] = (v * half * keep[...]).astype(BF)
             slope = half + 0.5 * v * (1.0 - th * th) * (a0 * (1.0 + 3.0 * a1 * v2))
-            db = (ga * slope).astype(BF)
+            db = (ga * slope * keep[...]).astype(BF)
             dbb[:, cols(i)] = db
             bsum[:, cols(i)] += jnp.sum(db.astype(F32), 0, keepdims=True)
         tiles(hid // TILE, tile)
@@ -682,13 +913,14 @@
         dn2 = total[...]
         e = dn2 * vec[0:1, :]
         inner = jnp.mean(e, -1, keepdims=True) + xhat * jnp.mean(e * xhat, -1, keepdims=True)
-        d = gshare[r, :].astype(F32) + inverse * (e - inner)
+        grad = gshare[r, :].astype(F32) * alive(1, at.t, c)
+        d = grad + inverse * (e - inner)
         dh[r, :] = d
         gat[at.t, r, :] = d.astype(BF)
         stats[0:1, :] += jnp.sum(dn2 * xhat, 0, keepdims=True)
         stats[1:2, :] += jnp.sum(dn2, 0, keepdims=True)
         stats[2:3, :] += jnp.sum(d, 0, keepdims=True)
-        stats[3:4, :] += jnp.sum(gshare[r, :].astype(F32), 0, keepdims=True)
+        stats[3:4, :] += jnp.sum(grad, 0, keepdims=True)
 
     def heads(c):
         y = dg(wide(c), w_out[...], 1, 0)
@@ -714,7 +946,7 @@
                     def served(c):
                         mlp.finish(c, total)
                         r = chunk_rows(c, rows)
-                        res[r, :] = (live[r, :] * (hidden[r, :] + total[...] + vec[1:2, :])).astype(BF)
+                        res[r, :] = (alive(1, at.t, c) * (hidden[r, :] + total[...] + vec[1:2, :])).astype(BF)
                     at_stage(i - 4, served)
                     at_stage(i - 3, mlp.meet)
                 at_stage(i - 3, lambda c: mlp.hop(c, h - 1))
@@ -755,7 +987,7 @@
         one = pltpu.make_async_copy(actb, gw_hbm.at[r, pl.ds(0, hid)], lsem)
         one.start()
         dbb[...] = acc_down[r, :].astype(BF)
-        two = pltpu.make_async_copy(dbb, gw_hbm.at[r, pl.ds(hid, hid)], msem)
+        two = pltpu.make_async_copy(dbb, gw_hbm.at[r, pl.ds(hid, hid)], msem.at[0])
         two.start()
         one.wait()
         two.wait()
@@ -768,7 +1000,7 @@
     tiles(width // TILE, final)
 
 
-def feed_forward(n2, gradb, w_up, w_down, w_out, b_up, ctx, hidden, gshare, vec, live, n, chunks):
+def feed_forward(n2, gradb, b_up, w_up, w_down, w_out, ctx, hidden, vec, tokens, n, chunks):
     length, width = gradb.shape
     hid, hw = w_up.shape[1], w_out.shape[1]
     share = length // n
@@ -779,90 +1011,47 @@
     m = n * rows
     return pl.pallas_call(
         functools.partial(ffn_kernel, n=n, chunks=chunks, rows=rows),
-        in_specs=[hbm, hbm] + [vm] * 9,
+        in_specs=[hbm] * 3 + [vm] * 7,
         out_specs=[hbm] + [vm] * 6,
         out_shape=[S((width, 2 * hid), BF), S((width, hw), BF), S((n, share, hw), BF), S((share, width), F32),
                    S((share, width), BF), S((8, width), F32), S((1, hid), F32)],
         scratch_shapes=[pltpu.VMEM((n, share, width), BF), pltpu.VMEM((width, hid), F32), pltpu.VMEM((width, hid), F32),
                         pltpu.VMEM((2, n, rows, width), BF),
                         pltpu.VMEM((m, hid), BF), pltpu.VMEM((m, hid), BF), pltpu.VMEM((rows, width), F32),
-                        pltpu.SemaphoreType.DMA, pltpu.SemaphoreType.DMA((2,)), pltpu.SemaphoreType.DMA]
+                        pltpu.VMEM((share, width), BF), pltpu.VMEM((1, hid), F32), pltpu.VMEM((m, 1), F32),
+                        pltpu.SemaphoreType.DMA, pltpu.SemaphoreType.DMA((2,)), pltpu.SemaphoreType.DMA((2,))]
                        + gather_sems(chunks, Z) + gather_sems(chunks, Z) + scatter_scratch(chunks, Z, rows, width) * 2,
         compiler_params=pltpu.CompilerParams(collective_id=3, has_side_effects=True, vmem_limit_bytes=62 << 20),
         cost_estimate=pl.CostEstimate(flops=12 * length * hid * width, bytes_accessed=1 << 26, transcendentals=0),
         name="feed_forward",
-    )(n2, gradb.reshape(n, share, width), w_up, w_down, w_out, b_up, ctx, hidden, gshare, vec, live)
-
-
-def normalize(rows, gain, bias):
-    mean_row = jnp.mean(rows, -1, keepdims=True)
-    centred = rows - mean_row
-    return centred * lax.rsqrt(jnp.mean(centred * centred, -1, keepdims=True) + 1e-05) * gain + bias
+    )(n2, gradb.reshape(n, share, width), b_up.reshape(n, 1, hid), w_up, w_down, w_out, ctx, hidden, vec, tokens)
 
 
 def on_device(layer_input, out_cotangent, seq_group, seq_len, w_qkv, b_qv, w_out, b_out, w_up, b_up,
               w_down, b_down, first_norm_gain, first_norm_bias, second_norm_gain, second_norm_bias):
-    tp = lax.axis_index("tp")
-    n_tp = lax.axis_size("tp")
+    n_tp, n_grp = lax.axis_size("tp"), lax.axis_size("grp")
     grp = lax.axis_index("grp")
     length, width = layer_input.shape
-    share = length // n_tp
-    heads = w_out.shape[1] // HD
-    hidden_here = w_up.shape[1]
-
-    w_attn = lax.all_gather(w_qkv.astype(BF), "grp", axis=0, tiled=True)
-    w_proj = lax.all_gather(w_out.astype(BF), "grp", axis=0, tiled=True)
-    w_expand = lax.all_gather(w_up.astype(BF), "grp", axis=0, tiled=True)
-    w_reduce = lax.all_gather(w_down.astype(BF), "grp", axis=0, tiled=True)
-
-    nb = length // BLK
-    in_group = seq_group == grp
-    lengths = jnp.where(in_group, seq_len, 0)
-    order = jnp.arange(seq_group.shape[0], dtype=jnp.int32)
-    offsets = jnp.sum(jnp.where(order[:, None] > order[None, :], lengths[None, :], 0), 1)
-    starts = jnp.arange(nb, dtype=jnp.int32) * BLK
-    inside = in_group[None] & (starts[:, None] >= offsets[None]) & (starts[:, None] < (offsets + lengths)[None])
-    alive = jnp.any(inside, 1)
-    first = jnp.sum(jnp.where(inside, (offsets // BLK)[None], 0), 1)
-    last = jnp.sum(jnp.where(inside, ((offsets + lengths) // BLK - 1)[None], 0), 1)
-    info = jnp.stack([first, last, alive.astype(jnp.int32)]).astype(jnp.int32)
-    tokens = jnp.sum(lengths)
-    row0 = tp * share
-    live = (row0 + jnp.arange(share, dtype=jnp.int32) < tokens).astype(F32)[:, None]
-    live_all = (jnp.arange(length, dtype=jnp.int32) < tokens)[:, None]
-
-    def mine(x):
-        return lax.dynamic_slice_in_dim(x, row0, share, 0)
-
-    x = layer_input.astype(F32)
-    n1 = normalize(x, first_norm_gain, first_norm_bias).astype(BF)
-    x_share_b = mine(layer_input)
-
-    head_bias = lax.dynamic_slice_in_dim(b_qv.reshape(-1, 2, HD), tp * heads, heads, 0)
-    bias_three = jnp.stack(
-        [head_bias[:, 0], jnp.zeros_like(head_bias[:, 0]), head_bias[:, 1]], 1).reshape(-1)
-    proj = (jnp.dot(n1, w_attn, preferred_element_type=F32) + bias_three).astype(BF)
-    context, lse = attn_fwd(info, proj)
-    vec = jnp.stack([b_out, second_norm_gain, second_norm_bias])
-    hidden, n2_share = attn_out(context, w_proj, x_share_b, vec, n_tp, 8)
-    up_bias = lax.dynamic_slice_in_dim(b_up, tp * hidden_here, hidden_here, 0)[None]
-    gradb = jnp.where(live_all, out_cotangent, jnp.zeros_like(out_cotangent))
-    gradb_share = mine(gradb)
+    hid, qv = w_up.shape[1], b_qv.shape[0] // n_tp
+
+    proj, n1, w_attn, w_proj, up16, down16 = front(
+        layer_input, w_qkv, w_out, w_up, w_down, jnp.stack([first_norm_gain, first_norm_bias]), b_qv, n_tp, n_grp)
+    context, lse = attn_fwd(seq_group, seq_len, proj)
+    hidden, n2, w_expand, w_reduce = attn_out(
+        context, w_proj, jnp.stack([b_out, second_norm_gain, second_norm_bias]), layer_input, up16, down16,
+        n_tp, n_grp, 8)
+    tokens = jnp.sum(jnp.where(seq_group == grp, seq_len, 0)).reshape(1, 1)
     gw_ffn, gw_proj, dcontext, dh, result, stats, up_sum = feed_forward(
-        n2_share, gradb, w_expand, w_reduce, w_proj, up_bias, context, hidden, gradb_share,
-        jnp.stack([second_norm_gain, b_down]), live, n_tp, 8)
-    dcontext = dcontext.reshape(length, -1)
-    scatter = functools.partial(lax.psum_scatter, axis_name="grp", scatter_dimension=0, tiled=True)
-    grads_ffn = scatter(gw_ffn).astype(F32)
-    grads_expand, grads_reduce = grads_ffn[:, :hidden_here], grads_ffn[:, hidden_here:]
-
-    dproj = attn_bwd(info, proj, context, dcontext, lse)
+        n2, out_cotangent, b_up, w_expand, w_reduce, w_proj, context, hidden,
+        jnp.stack([second_norm_gain, b_down]), tokens, n_tp, 8)
+    grads_ffn = lax.psum_scatter(gw_ffn, "grp", scatter_dimension=0, tiled=True).astype(F32)
+    grads_expand, grads_reduce = grads_ffn[:, :hid], grads_ffn[:, hid:]
+
+    dproj = attn_bwd(seq_group, seq_len, proj, context, dcontext.reshape(length, -1), lse)
     grad_x, grads_attn, grads_proj, sums, owned = project_back(
-        dproj, w_attn, n1, gw_proj, x_share_b, dh, first_norm_gain[None], stats, up_sum,
-        n_tp, lax.axis_size("grp"), 8)
-    qv = heads * 2 * HD
-    return (result, grad_x, grads_attn, owned[:, hidden_here:hidden_here + qv].reshape(-1), grads_proj, sums[2],
-            grads_expand, owned[:, :hidden_here].reshape(-1), grads_reduce, sums[3], sums[4], sums[5],
+        dproj, w_attn, n1, gw_proj, layer_input, dh, first_norm_gain[None], stats, up_sum, n_tp, n_grp, 8)
+    return (result, grad_x, grads_attn, owned[:, hid:hid + qv].reshape(-1), grads_proj, sums[2],
+            grads_expand, owned[:, :hid].reshape(-1), grads_reduce, sums[3], sums[4], sums[5],
             sums[0], sums[1])
 
 

time: 591 us -> 555 us (0.939)
  Pallas kernels: 466 us -> 512 us
  other arithmetic: 39.3 us -> 2.77 us
  waiting for transfers between devices: 31.4 us -> 0.02 us
  matrix products: 10 us -> 0 us
    pallas_call x3 -> x4, Pallas kernels: 117 us -> 151 us  [the longest x1 90.2 us: attn_out(): pl.pallas_call(functools.partial(out_kernel, n=n, n_grp=n_grp, chunks=chu...]
    all_gather x4 -> x0, waiting for transfers between devices: 31.3 us -> none  [the longest x1 26.8 us: on_device(): w_reduce = lax.all_gather(w_down.astype(BF), 'grp', axis=0, tiled=True)]
    convert_element_type x7 -> x0, other arithmetic: 18.3 us -> none  [the longest x1 8.86 us: on_device(): n1 = normalize(x, first_norm_gain, first_norm_bias).astype(BF)]
    pallas_call x1, Pallas kernels: 101 us -> 113 us  [project_back(): pl.pallas_call(functools.partial(back_kernel, n=n, n_grp=n_grp, chunks=ch...]
    reduce_sum x5 -> x1, other arithmetic: 11.8 us -> 1.31 us  [on_device(): tokens = jnp.sum(jnp.where(seq_group == grp, seq_len, 0)).reshape(1, 1)]
    dot_general x1 -> x0, matrix products: 10 us -> none  [on_device(): jnp.dot(n1, w_attn, preferred_element_type=F32) + bias_three]
    select_n x1 -> x0, other arithmetic: 7.71 us -> none  [on_device(): gradb = jnp.where(live_all, out_cotangent, jnp.zeros_like(out_cotangent))]
    unnamed x62 -> x56, local copies, waits for them, and re-layouts: 18.8 us -> 20.8 us
  transfers between devices with their start and end apart: 5 -> 1, of which waited for: 2 -> 0; matrix products, arithmetic and copies ran while one was open for 9% -> 0% of each run, Pallas kernels for 37% -> 22%
where the time goes in v5:
time: 555 us; the launch traced here: 554 us
  Pallas kernels  512 us (92%)
  local copies, waits for them, and re-layouts  25.5 us (5%)
  between operations  14.2 us (3%)
    pallas_call x1, Pallas kernels, feed_forward(): pl.pallas_call(functools.partial(ffn_kernel, n=n, chunks=chunks, rows=row...  248 us
    pallas_call x1, Pallas kernels, project_back(): pl.pallas_call(functools.partial(back_kernel, n=n, n_grp=n_grp, chunks=ch...  113 us
    pallas_call x1, Pallas kernels, attn_out(): pl.pallas_call(functools.partial(out_kernel, n=n, n_grp=n_grp, chunks=chu...  90.2 us
    pallas_call x1, Pallas kernels, front(): pl.pallas_call(functools.partial(front_kernel, n=n, n_grp=n_grp, parts=pa...  46.4 us
    unnamed x56, local copies, waits for them, and re-layouts  20.8 us
  transfers between devices with their start and end apart: 1, of which 0 were waited for; matrix products, arithmetic and copies ran while one was open for 0% of the time, Pallas kernels for 22%

profile of v5, /device:TPU:0, one launch (start us, length us, event | category | flops | bytes accessed | tf_op | source)
XLA Modules:
  0.0 554.1 jit_solution(16347496821066976891)
XLA Ops:
  7.2 0.0 reduce-scatter.2.cloned.1.call-start
  7.2 0.7 pad_maximum_fusion.1.vec
  8.0 1.3 fusion
  9.3 1.0 copy-done.11
  10.3 0.7 copy-done.12
  11.0 46.4 %front.1 = (bf16[2048,768]{1,0:T(8,128)(2,1)}, bf16[2048,2048]{1,0:T(8,128)(2,1)}, bf16[2048,768]{1,0:T(8,128)(2,1)}, bf16[2048,256]{1,0:T(8,128)(2,1)S(1)}, bf1...) custom-call(bf16[2048,2048]{1,0:T(8,128)(2,1)} %x_hbm.1, f32[512,768]{1,0:T(8,128)} %w_qkv.1, ...), custom_call_target="tpu_custom_call" | custom-call | flops 6442450944 | bytes 16777216 | tf_op jit(solution)/shard_map/front/pallas_call | solution.py:591
  57.5 0.0 copy-start.4
  57.5 2.2 copy-done
  59.8 5.8 %attn_fwd.1 = (bf16[2048,256]{1,0:T(8,128)(2,1)S(1)}, f32[2,1,2048]{2,1,0:T(1,128)S(1)}) custom-call(s32[6]{0:T(128)S(1)} %copy-done.6, s32[6]{0:T(128)S(1)} %copy-done.7, bf16[2048,768]{1,0:T(8,128)(2,1)S(1)} %copy-done, bf16[2048,768]{1,0:T(8,128)(2,1)S(1)} %copy-done, bf16[2048,768]{1,0:T(8,128)(2,1)S(1)} %copy-done), custom_call_target="tpu_custom_call" | custom-call | flops 2147483648 | bytes 4194304 | tf_op jit(solution)/shard_map/attn_fwd/pallas_call | solution.py:68
  65.6 0.0 copy-start.2
  65.6 0.7 pad_maximum_fusion.2.vec
  66.4 90.2 %attn_out.1 = (f32[256,2048]{1,0:T(8,128)S(1)}, bf16[256,2048]{1,0:T(8,128)(2,1)S(1)}, bf16[2048,1024]{1,0:T(8,128)(2,1)S(1)}, bf16[2048,1024]{1,0:T(8,128)(2,1)}) custom-call(bf16[8,256,256]{2,1,0:T(8,128)(2,1)S(1)} %bitcast.28, bf16[2048,256]{1,0:T(8,128)(2,1)S(1)} %get-tuple-element.40.w_out, f32[3,2048]{1,0:T(4,128)S(1)} %pad_maximum_fusion.vec, ...), custom_call_target="tpu_custom_call" | custom-call | flops 2147483648 | bytes 8388608 | tf_op jit(solution)/shard_map/attn_out/pallas_call | solution.py:493
  156.6 2.0 copy-done.8
  158.6 1.3 copy-done.9
  159.9 1.0 copy-done.10
  160.9 247.8 %feed_forward.1 = (bf16[2048,2048]{1,0:T(8,128)(2,1)}, bf16[2048,256]{1,0:T(8,128)(2,1)}, bf16[8,256,256]{2,1,0:T(8,128)(2,1)}, f32[256,2048]{1,0:T(8,128)}, bf1...) custom-call(bf16[256,2048]{1,0:T(8,128)(2,1)} %copy-done.10, bf16[8,256,2048]{2,1,0:T(8,128)(2,1)} %bitcast.50, ...), custom_call_target="tpu_custom_call" | custom-call | flops 51539607552 | bytes 67108864 | tf_op jit(solution)/shard_map/feed_forward/pallas_call | solution.py:1012
  408.8 0.0 reduce-scatter.2.cloned.1.call-update
  408.8 1.9 copy-done.1
  410.7 1.2 copy-done.3
  411.9 1.2 copy-done.14
  413.1 8.5 %attn_bwd.1 = bf16[2048,768]{1,0:T(8,128)(2,1)S(1)} custom-call(s32[6]{0:T(128)S(1)} %copy-done.6, s32[6]{0:T(128)S(1)} %copy-done.7, bf16[2048,768]{1,0:T(8,128)(2,1)S(1)} %copy-done.1, bf16[2048,768]{1,0:T(8,128)(2,1)S(1)} %copy-done.1, bf16[2048,768]{1,0:T(8,128)(2,1)S(1)} %copy-done.1, bf16[2048,256]{1,0:T(8,128)(2,1)S(1)} %copy-done.3, ...), custom_call_target="tpu_custom_call" | custom-call | flops 5368709120 | bytes 8388608 | tf_op jit(solution)/shard_map/attn_bwd/pallas_call | solution.py:119
  421.7 1.6 copy-done.13
  423.3 112.8 %project_back.1 = (f32[256,2048]{1,0:T(8,128)}, f32[512,768]{1,0:T(8,128)S(1)}, f32[512,256]{1,0:T(8,128)S(1)}, f32[8,2048]{1,0:T(8,128)S(1)}, f32[8,2048]{1,0:T(8,128)S(1)}) custom-call(bf16[8,256,768]{2,1,0:T(8,128)(2,1)} %bitcast.32, bf16[2048,768]{1,0:T(8,128)(2,1)} %get-tuple-element.50.w_attn, bf16[2048,2048]{1,0:T(8,128)(2,1)} %get-tuple-element.51.n1_hbm, ...), custom_call_target="tpu_custom_call" | custom-call | flops 12884901888 | bytes 16777216 | tf_op jit(solution)/shard_map/project_back/pallas_call | solution.py:808
  536.1 0.6 copy.33
  536.7 0.6 copy.30
  537.3 0.6 fusion.2
  538.0 4.1 fusion.1
  542.1 1.0 copy.38
  543.0 1.0 copy-done.18
  544.0 1.3 copy.39
  545.4 1.1 copy.40
  546.5 0.8 copy.41
  (39 shorter events, 0.1 us)
Async XLA Ops:
  7.2 530.8 %reduce-scatter.2.cloned.1.call-start = ((), (), s32[]{:S(2)}) async-start(), calls=%async_computation.1 | async-start | bytes 10485760 | tf_op jit(solution)/shard_map/reduce_scatter | solution.py:1047
  9.3 1.0 copy-start.11
  10.3 0.7 copy-start.12
  11.0 46.4 %copy-start.6 = (s32[6]{0:T(128)S(1)}, s32[6]{0:T(128)}, u32[]{:S(2)}) copy-start(s32[6]{0:T(128)} %grps.3) | copy-start | bytes 76
  11.0 46.4 %copy-start.7 = (s32[6]{0:T(128)S(1)}, s32[6]{0:T(128)}, u32[]{:S(2)}) copy-start(s32[6]{0:T(128)} %lens.3) | copy-start | bytes 76
  57.5 8.9 %copy-start.4 = (bf16[2048,256]{1,0:T(8,128)(2,1)}, bf16[2048,256]{1,0:T(8,128)(2,1)S(1)}, u32[]{:S(2)}) copy-start(bf16[2048,256]{1,0:T(8,128)(2,1)S(1)} %get-tuple-element.40.w_out) | copy-start | bytes 3145732
  57.5 2.3 copy-start
  59.7 5.9 %copy-start.20 = (f32[2048]{0:T(1024)S(1)}, f32[2048]{0:T(1024)}, u32[]{:S(2)}) copy-start(f32[2048]{0:T(1024)} %param.30) | copy-start | bytes 24580
  59.7 5.9 %copy-start.23 = (f32[2048]{0:T(1024)S(1)}, f32[2048]{0:T(1024)}, u32[]{:S(2)}) copy-start(f32[2048]{0:T(1024)} %param.27) | copy-start | bytes 24580
  59.7 6.6 %copy-start.21 = (f32[2048]{0:T(1024)S(1)}, f32[2048]{0:T(1024)}, u32[]{:S(2)}) copy-start(f32[2048]{0:T(1024)} %param.31) | copy-start | bytes 24580
  59.8 6.6 %copy-start.22 = (f32[2048]{0:T(1024)S(1)}, f32[2048]{0:T(1024)}, u32[]{:S(2)}) copy-start(f32[2048]{0:T(1024)} %param.23) | copy-start | bytes 24580
  65.6 91.0 %copy-start.2 = (bf16[2048,256]{1,0:T(8,128)(2,1)}, bf16[2048,256]{1,0:T(8,128)(2,1)S(1)}, u32[]{:S(2)}) copy-start(bf16[2048,256]{1,0:T(8,128)(2,1)S(1)} %get-tuple-element.39.ctx.o_ref) | copy-start | bytes 3145732
  156.6 2.0 copy-start.8
  158.6 1.3 copy-start.9
  159.9 1.0 copy-start.10
  408.8 1.9 copy-start.1
  410.7 1.2 copy-start.3
  411.9 1.2 copy-start.14
  413.1 10.2 %copy-start.5 = (f32[2048]{0:T(1024)S(1)}, f32[2048]{0:T(1024)}, u32[]{:S(2)}) copy-start(f32[2048]{0:T(1024)} %param.28) | copy-start | bytes 24580
  413.1 10.2 %copy-start.15 = (bf16[2048,256]{1,0:T(8,128)(2,1)S(1)}, bf16[2048,256]{1,0:T(8,128)(2,1)}, u32[]{:S(2)}) copy-start(bf16[2048,256]{1,0:T(8,128)(2,1)} %get-tuple-element.52.gw_proj) | copy-start | bytes 3145732
  413.1 10.2 %copy-start.16 = (f32[8,2048]{1,0:T(8,128)S(1)}, f32[8,2048]{1,0:T(8,128)}, u32[]{:S(2)}) copy-start(f32[8,2048]{1,0:T(8,128)} %get-tuple-element.54.stats) | copy-start | bytes 196612
  413.1 10.2 %copy-start.17 = (f32[1,1024]{1,0:T(1,128)S(1)}, f32[1,1024]{1,0:T(1,128)}, u32[]{:S(2)}) copy-start(f32[1,1024]{1,0:T(1,128)} %get-tuple-element.55.up_sum) | copy-start | bytes 12292
  421.6 1.6 copy-start.13
  538.0 4.1 copy-start.19
  542.1 2.0 copy-start.18
Sparse Core Ops, SparseCore 0:
  408.9 124.6 reduce-scatter.1

commit v6 on v5

--- a/solution.py
+++ b/solution.py
@@ -15,6 +15,7 @@
 
 def dg(a,b,ca,cb):
     return lax.dot_general(a,b,(((ca,),(cb,)),((),())),preferred_element_type=F32)
+
 
 def block_info(grps, lens, nb, seqs):
     g = lax.axis_index("grp")
@@ -30,101 +31,110 @@
     return found
 
 
-def attn_fwd_kernel(grps, lens, q_ref, k_ref, v_ref, o_ref, lse_ref, *, nb, seqs):
+def below(shape):
+    return lax.broadcasted_iota(jnp.int32, shape, 0) <= lax.broadcasted_iota(jnp.int32, shape, 1)
+
+
+def attn_fwd_kernel(grps, lens, proj, o_ref, lse_ref, *, nb, seqs, heads):
     info = block_info(grps, lens, nb, seqs)
     c = HD ** -0.5 * LOG2E
+
+    def attend(qi, first):
+        rows = slice(qi * BLK, (qi + 1) * BLK)
+        early = slice(first * BLK, qi * BLK)
+        for h in range(heads):
+            col = 3 * h * HD
+            q = proj[rows, col:col + HD]
+            pieces = [(rows, jnp.where(below((BLK, BLK)), dg(proj[rows, col + HD:col + 2 * HD], q, 1, 1), -1e30))]
+            if first < qi:
+                pieces.append((early, dg(proj[early, col + HD:col + 2 * HD], q, 1, 1)))
+            top = functools.reduce(jnp.maximum, [jnp.max(s, 0, keepdims=True) for _, s in pieces]) * c
+            total, acc = 0.0, 0.0
+            for keys, s in pieces:
+                p = jnp.exp2(s * c - top)
+                total = total + jnp.sum(p, 0, keepdims=True)
+                acc = acc + dg(proj[keys, col + 2 * HD:col + 3 * HD], p.astype(BF), 0, 0)
+            o_ref[rows, h * HD:(h + 1) * HD] = jnp.transpose(acc / total).astype(BF)
+            lse_ref[h, :, rows] = top + jnp.log2(total)
+
     for qi in range(nb):
-        rows = pl.ds(qi*BLK, BLK)
-        @pl.when(info[qi][2] > 0)
-        def _():
-            q = q_ref[rows, :]
-            def step(j, carry, diag=False):
-                m, l, acc = carry
-                kr = pl.ds(pl.multiple_of(j*BLK, BLK), BLK)
-                s = dg(k_ref[kr, :], q, 1, 1)
-                if diag:
-                    ki = lax.broadcasted_iota(jnp.int32, s.shape, 0)
-                    qq = lax.broadcasted_iota(jnp.int32, s.shape, 1)
-                    s = jnp.where(ki <= qq, s, -1e30)
-                mn = jnp.maximum(m, jnp.max(s, 0, keepdims=True))
-                p = jnp.exp2(s*c - mn*c)
-                alpha = jnp.exp2((m - mn)*c)
-                l = l*alpha + jnp.sum(p, 0, keepdims=True)
-                acc = acc*alpha + dg(v_ref[kr, :], p.astype(BF), 0, 0)
-                return mn, l, acc
-            init = (jnp.full((1, BLK), -1e30, F32), jnp.zeros((1, BLK), F32), jnp.zeros((HD, BLK), F32))
-            carry = step(qi, init, True)
-            m, l, acc = lax.fori_loop(info[qi][0], qi, step, carry)
-            o_ref[rows, :] = jnp.transpose(acc / l).astype(BF)
-            lse_ref[0, :, rows] = m*c + jnp.log2(l)
+        for first in range(qi + 1):
+            @pl.when((info[qi][2] > 0) & (info[qi][0] == first))
+            def _():
+                attend(qi, first)
+
         @pl.when(info[qi][2] <= 0)
         def _():
-            o_ref[rows, :] = jnp.zeros((BLK, HD), BF)
-            lse_ref[0, :, rows] = jnp.zeros((1, BLK), F32)
+            o_ref[qi * BLK:(qi + 1) * BLK, :] = jnp.zeros((BLK, heads * HD), BF)
+            lse_ref[:, :, qi * BLK:(qi + 1) * BLK] = jnp.zeros((heads, 1, BLK), F32)
+
 
 def attn_fwd(grps, lens, proj):
     length = proj.shape[0]; heads = proj.shape[1]//(3*HD); nb = length//BLK
-    spec = lambda o: pl.BlockSpec((length, HD), lambda h, grps, lens: (0, 3*h+o))
-    return pl.pallas_call(functools.partial(attn_fwd_kernel, nb=nb, seqs=grps.shape[0]),
-        grid_spec=pltpu.PrefetchScalarGridSpec(num_scalar_prefetch=2, grid=(heads,),
-            in_specs=[spec(0), spec(1), spec(2)],
-            out_specs=[pl.BlockSpec((length, HD), lambda h, grps, lens: (0, h)), pl.BlockSpec((1, 1, length), lambda h, grps, lens: (h, 0, 0))]),
+    vm, sm = pl.BlockSpec(memory_space=pltpu.VMEM), pl.BlockSpec(memory_space=pltpu.SMEM)
+    return pl.pallas_call(functools.partial(attn_fwd_kernel, nb=nb, seqs=grps.shape[0], heads=heads),
+        in_specs=[sm, sm, vm], out_specs=[vm, vm],
         out_shape=[jax.ShapeDtypeStruct((length, heads*HD), BF), jax.ShapeDtypeStruct((heads, 1, length), F32)],
         compiler_params=pltpu.CompilerParams(vmem_limit_bytes=40<<20), name="attn_fwd",
         cost_estimate=pl.CostEstimate(flops=heads*length*length*HD*2, bytes_accessed=length*heads*HD*8, transcendentals=heads*length*length//2),
-    )(grps, lens, proj, proj, proj)
-
-def attn_bwd_kernel(grps, lens, q_ref, k_ref, v_ref, o_ref, do_ref, lse_ref, dp_ref, dq_sc, dl_sc, *, nb, seqs):
+    )(grps, lens, proj)
+
+
+def attn_bwd_kernel(grps, lens, proj, o_ref, do_ref, lse_ref, dp_ref, dq_sc, dl_sc, *, nb, seqs, heads):
     info = block_info(grps, lens, nb, seqs)
-    sc = HD ** -0.5
-    c = sc * LOG2E
-    prod = do_ref[...].astype(F32) * o_ref[...].astype(F32)
-    dl_sc[...] = jnp.sum(jnp.transpose(prod), 0, keepdims=True)
+    scale = HD ** -0.5
+    c = scale * LOG2E
+    for h in range(heads):
+        hc = slice(h * HD, (h + 1) * HD)
+        prod = do_ref[:, hc].astype(F32) * o_ref[:, hc].astype(F32)
+        dl_sc[h] = jnp.sum(jnp.transpose(prod), 0, keepdims=True)
     dq_sc[...] = jnp.zeros_like(dq_sc)
-    for j in range(nb):
-        kr = pl.ds(j*BLK, BLK)
-        @pl.when(info[j][2] > 0)
-        def _():
-            k = k_ref[kr, :]; v = v_ref[kr, :]
-            def step(i, carry, diag=False):
-                dk, dv = carry
-                qr = pl.ds(pl.multiple_of(i*BLK, BLK), BLK)
-                q = q_ref[qr, :]; do = do_ref[qr, :]
-                s = dg(k, q, 1, 1)
-                p = jnp.exp2(s*c - lse_ref[0, :, qr])
+
+    def attend(j, last):
+        keys = slice(j * BLK, (j + 1) * BLK)
+        for h in range(heads):
+            col = 3 * h * HD
+            hc = slice(h * HD, (h + 1) * HD)
+            k, v = proj[keys, col + HD:col + 2 * HD], proj[keys, col + 2 * HD:col + 3 * HD]
+            dk, dv = 0.0, 0.0
+            for diag in (True, False):
+                rows = keys if diag else slice((j + 1) * BLK, (last + 1) * BLK)
+                if rows.start == rows.stop:
+                    continue
+                q, do = proj[rows, col:col + HD], do_ref[rows, hc]
+                p = jnp.exp2(dg(k, q, 1, 1) * c - lse_ref[h, :, rows])
                 if diag:
-                    ki = lax.broadcasted_iota(jnp.int32, s.shape, 0)
-                    qq = lax.broadcasted_iota(jnp.int32, s.shape, 1)
-                    p = jnp.where(ki <= qq, p, 0.0)
-                dp = dg(v, do, 1, 1)
-                ds = (p * (dp - dl_sc[:, qr])).astype(BF)
+                    p = jnp.where(below((BLK, BLK)), p, 0.0)
+                ds = (p * (dg(v, do, 1, 1) - dl_sc[h, :, rows])).astype(BF)
                 dv = dv + dg(p.astype(BF), do, 1, 0)
                 dk = dk + dg(ds, q, 1, 0)
-                dq_sc[qr, :] += dg(ds, k, 0, 0)
-                return dk, dv
-            z = jnp.zeros((BLK, HD), F32)
-            carry = step(j, (z, z), True)
-            dk, dv = lax.fori_loop(j+1, info[j][1]+1, step, carry)
-            dp_ref[kr, HD:2*HD] = (dk*sc).astype(BF)
-            dp_ref[kr, 2*HD:] = dv.astype(BF)
+                dq_sc[h, :, rows] += dg(k, ds, 0, 0)
+            dp_ref[keys, col + HD:col + 2 * HD] = (dk * scale).astype(BF)
+            dp_ref[keys, col + 2 * HD:col + 3 * HD] = dv.astype(BF)
+
+    for j in range(nb):
+        for last in range(j, nb):
+            @pl.when((info[j][2] > 0) & (info[j][1] == last))
+            def _():
+                attend(j, last)
+
         @pl.when(info[j][2] <= 0)
         def _():
-            dp_ref[kr, HD:] = jnp.zeros((BLK, 2*HD), BF)
-    dp_ref[:, :HD] = (dq_sc[...]*sc).astype(BF)
+            dp_ref[j * BLK:(j + 1) * BLK, :] = jnp.zeros((BLK, heads * 3 * HD), BF)
+    for h in range(heads):
+        dp_ref[:, 3 * h * HD:(3 * h + 1) * HD] = jnp.transpose(dq_sc[h] * scale).astype(BF)
+
 
 def attn_bwd(grps, lens, proj, ctx, dctx, lse):
     length = proj.shape[0]; heads = proj.shape[1]//(3*HD); nb = length//BLK
-    spec = lambda o: pl.BlockSpec((length, HD), lambda h, grps, lens: (0, 3*h+o))
-    hs = pl.BlockSpec((length, HD), lambda h, grps, lens: (0, h))
-    return pl.pallas_call(functools.partial(attn_bwd_kernel, nb=nb, seqs=grps.shape[0]),
-        grid_spec=pltpu.PrefetchScalarGridSpec(num_scalar_prefetch=2, grid=(heads,),
-            in_specs=[spec(0), spec(1), spec(2), hs, hs, pl.BlockSpec((1, 1, length), lambda h, grps, lens: (h, 0, 0))],
-            out_specs=pl.BlockSpec((length, 3*HD), lambda h, grps, lens: (0, h)),
-            scratch_shapes=[pltpu.VMEM((length, HD), F32), pltpu.VMEM((1, length), F32)]),
+    vm, sm = pl.BlockSpec(memory_space=pltpu.VMEM), pl.BlockSpec(memory_space=pltpu.SMEM)
+    return pl.pallas_call(functools.partial(attn_bwd_kernel, nb=nb, seqs=grps.shape[0], heads=heads),
+        in_specs=[sm, sm] + [vm]*4, out_specs=vm,
+        scratch_shapes=[pltpu.VMEM((heads, HD, length), F32), pltpu.VMEM((heads, 1, length), F32)],
         out_shape=jax.ShapeDtypeStruct((length, heads*3*HD), BF),
         compiler_params=pltpu.CompilerParams(vmem_limit_bytes=40<<20), name="attn_bwd",
         cost_estimate=pl.CostEstimate(flops=heads*length*length*HD*5, bytes_accessed=length*heads*HD*16, transcendentals=heads*length*length//2),
-    )(grps, lens, proj, proj, proj, ctx, dctx, lse)
+    )(grps, lens, proj, ctx, dctx, lse)
 
 
 MESH = pl.DeviceIdType.MESH
@@ -697,6 +707,10 @@
         rs.start(c)
 
     def weights(i):
+        @pl.when(i == 0)
+        def _():
+            load.wait()
+            load_x.wait()
         k = i // per
         first = pl.multiple_of(owner(k) * block + lax.rem(i, per) * TILE, TILE)
         y = dg(n1[:, pl.ds(first, TILE)], dproj[...].reshape(-1, hw), 0, 0)
@@ -722,9 +736,6 @@
         grad_x[r, :] = dh[r, :] + inverse * (e - inner)
         ln_sum[0:1, :] += jnp.sum(dn * xhat, 0, keepdims=True)
         ln_sum[1:2, :] += jnp.sum(dn, 0, keepdims=True)
-
-    load.wait()
-    load_x.wait()
 
     def tick(i, carry):
         c = i - 1
@@ -821,9 +832,9 @@
     )(dproj.reshape(n, share, hw), w_attn, n1, gw_proj, x.reshape(n, share, width), dh, gain, stats, up_sum)
 
 
-def ffn_kernel(n2_hbm, gradb_hbm, bias_hbm, w_up, w_down, w_out, ctx, hidden, vec, tokens,
+def ffn_kernel(n2_hbm, gradb_hbm, bias_hbm, up_hbm, down_hbm, out_hbm, ctx_hbm, hidden_hbm, vec, tokens,
                gw_hbm, gwo, dctx, dh, res, stats, bsum,
-               gat, acc_up, acc_down, gbuf, actb, dbb, total, gshare, b_up, keep, lsem, gsem, msem, *scratch, n, chunks, rows):
+               w_up, w_down, w_out, ctx, hidden, wsem, acc_out, gat, acc_up, acc_down, gbuf, actb, dbb, total, gshare, b_up, keep, lsem, gsem, msem, *scratch, n, chunks, rows):
     at = Place(n)
     ag1, ag2 = Gather(at, gat, rows, *scratch[:4]), Gather(at, gat, rows, *scratch[4:8])
     rs, mlp = Scatter(at, *scratch[8:15]), Scatter(at, *scratch[15:])
@@ -834,6 +845,10 @@
     load.start()
     load_g = pltpu.make_async_copy(gradb_hbm.at[at.t], gshare, msem.at[0])
     load_g.start()
+    big = [pltpu.make_async_copy(src, dst, wsem.at[j]) for j, (src, dst) in enumerate(
+        ((up_hbm, w_up), (down_hbm, w_down), (hidden_hbm, hidden), (out_hbm, w_out), (ctx_hbm, ctx)))]
+    for copy in big:
+        copy.start()
     load_b = pltpu.make_async_copy(bias_hbm.at[at.t], b_up, msem.at[1])
     load_b.start()
     share = hidden.shape[0]
@@ -849,8 +864,6 @@
         return pltpu.make_async_copy(gradb_hbm.at[:, chunk_rows(c, rows), :], gbuf.at[slot], gsem.at[slot])
 
     fetch(0).start()
-    acc_up[...] = jnp.zeros_like(acc_up)
-    acc_down[...] = jnp.zeros_like(acc_down)
     stats[...] = jnp.zeros_like(stats)
     bsum[...] = jnp.zeros_like(bsum)
     load.wait()
@@ -864,6 +877,10 @@
         return gat[:, chunk_rows(c, rows), :].reshape(m, width)
 
     def forward(c):
+        @pl.when(c == 0)
+        def _():
+            for copy in big:
+                copy.wait()
         fetch(c).wait()
 
         @pl.when(c + 1 < chunks)
@@ -923,6 +940,10 @@
         stats[3:4, :] += jnp.sum(grad, 0, keepdims=True)
 
     def heads(c):
+        def tile(i):
+            x = gat[:, chunk_rows(c, rows), cols(i)].reshape(m, TILE)
+            acc_out[cols(i), :] += dg(x, ctx[:, chunk_rows(c, rows), :].reshape(m, -1), 0, 0)
+        tiles(width // TILE, tile)
         y = dg(wide(c), w_out[...], 1, 0)
         dctx[:, chunk_rows(c, rows), :] = y.astype(BF).reshape(n, rows, y.shape[1])
 
@@ -931,8 +952,40 @@
         def _():
             fn(c)
 
+    def store_copies(j):
+        r = chunk_rows(j, m)
+        return (pltpu.make_async_copy(actb, gw_hbm.at[r, pl.ds(0, hid)], lsem),
+                pltpu.make_async_copy(dbb, gw_hbm.at[r, pl.ds(hid, hid)], msem.at[0]))
+
+    def store_wait(j):
+        for copy in store_copies(j):
+            copy.wait()
+
+    def store(j):
+        @pl.when((j >= 0) & (j < width // m))
+        def _():
+            @pl.when(j > 0)
+            def _():
+                store_wait(j - 1)
+            r = chunk_rows(j, m)
+            actb[...] = acc_up[r, :].astype(BF)
+            dbb[...] = acc_down[r, :].astype(BF)
+            for copy in store_copies(j):
+                copy.start()
+
+    per_slot = -(-(width // m) // (3 * (at.Z - 1)))
+
     def tick(i, carry):
+        def stores(slot):
+            for j in range(per_slot):
+                store(((i - chunks - 2) * (at.Z - 1) + slot) * per_slot + j)
         at_stage(i, ag1.start)
+
+        @pl.when(i == 0)
+        def _():
+            acc_up[...] = jnp.zeros_like(acc_up)
+            acc_down[...] = jnp.zeros_like(acc_down)
+            acc_out[...] = jnp.zeros_like(acc_out)
         at_stage(i - 3, rs.meet)
         for h in range(1, at.Z):
             at_stage(i - 3, lambda c: rs.hop(c, h))
@@ -941,6 +994,7 @@
                 at_stage(i - 4, lambda c: mlp.hop(c, at.Z - 1))
                 at_stage(i - 5, lambda c: ag2.hop(c, at.Z - 1))
                 at_stage(i - 2, forward)
+                stores(0)
             else:
                 if h == 2:
                     def served(c):
@@ -951,6 +1005,7 @@
                     at_stage(i - 3, mlp.meet)
                 at_stage(i - 3, lambda c: mlp.hop(c, h - 1))
                 at_stage(i - 4, lambda c: ag2.hop(c, h - 1))
+                stores(h - 1)
                 if h == 2:
                     at_stage(i - 2, back)
 
@@ -976,28 +1031,12 @@
             mlp.start(c)
         at_stage(i - 2, send_mlp)
 
-        @pl.when(i == chunks + 2)
-        def _():
-            tiles(width // m, store)
         return carry
 
-    def store(i):
-        r = cols(i, m)
-        actb[...] = acc_up[r, :].astype(BF)
-        one = pltpu.make_async_copy(actb, gw_hbm.at[r, pl.ds(0, hid)], lsem)
-        one.start()
-        dbb[...] = acc_down[r, :].astype(BF)
-        two = pltpu.make_async_copy(dbb, gw_hbm.at[r, pl.ds(hid, hid)], msem.at[0])
-        two.start()
-        one.wait()
-        two.wait()
-
     lax.fori_loop(0, chunks + 5, tick, 0)
 
-    def final(i):
-        x = gat[:, :, cols(i)].reshape(-1, TILE)
-        gwo[cols(i), :] = dg(x, ctx[...], 0, 0).astype(BF)
-    tiles(width // TILE, final)
+    store_wait(width // m - 1)
+    gwo[...] = acc_out[...].astype(BF)
 
 
 def feed_forward(n2, gradb, b_up, w_up, w_down, w_out, ctx, hidden, vec, tokens, n, chunks):
@@ -1011,11 +1050,13 @@
     m = n * rows
     return pl.pallas_call(
         functools.partial(ffn_kernel, n=n, chunks=chunks, rows=rows),
-        in_specs=[hbm] * 3 + [vm] * 7,
+        in_specs=[hbm] * 8 + [vm] * 2,
         out_specs=[hbm] + [vm] * 6,
         out_shape=[S((width, 2 * hid), BF), S((width, hw), BF), S((n, share, hw), BF), S((share, width), F32),
                    S((share, width), BF), S((8, width), F32), S((1, hid), F32)],
-        scratch_shapes=[pltpu.VMEM((n, share, width), BF), pltpu.VMEM((width, hid), F32), pltpu.VMEM((width, hid), F32),
+        scratch_shapes=[pltpu.VMEM((width, hid), BF), pltpu.VMEM((width, hid), BF), pltpu.VMEM((width, hw), BF),
+                        pltpu.VMEM((n, share, hw), BF), pltpu.VMEM((share, width), F32), pltpu.SemaphoreType.DMA((5,)),
+                        pltpu.VMEM((width, hw), F32), pltpu.VMEM((n, share, width), BF), pltpu.VMEM((width, hid), F32), pltpu.VMEM((width, hid), F32),
                         pltpu.VMEM((2, n, rows, width), BF),
                         pltpu.VMEM((m, hid), BF), pltpu.VMEM((m, hid), BF), pltpu.VMEM((rows, width), F32),
                         pltpu.VMEM((share, width), BF), pltpu.VMEM((1, hid), F32), pltpu.VMEM((m, 1), F32),
@@ -1024,7 +1065,8 @@
         compiler_params=pltpu.CompilerParams(collective_id=3, has_side_effects=True, vmem_limit_bytes=62 << 20),
         cost_estimate=pl.CostEstimate(flops=12 * length * hid * width, bytes_accessed=1 << 26, transcendentals=0),
         name="feed_forward",
-    )(n2, gradb.reshape(n, share, width), b_up.reshape(n, 1, hid), w_up, w_down, w_out, ctx, hidden, vec, tokens)
+    )(n2, gradb.reshape(n, share, width), b_up.reshape(n, 1, hid), w_up, w_down, w_out, ctx.reshape(n, share, hw),
+      hidden, vec, tokens)
 
 
 def on_device(layer_input, out_cotangent, seq_group, seq_len, w_qkv, b_qv, w_out, b_out, w_up, b_up,

time: 555 us -> 547 us (0.986); the launches traced: 554 us -> 539 us
  Pallas kernels: 512 us -> 492 us
    pallas_call x1, Pallas kernels: 113 us -> 98.7 us  [project_back(): pl.pallas_call(functools.partial(back_kernel, n=n, n_grp=n_grp, chunks=ch...]
    pallas_call x1, Pallas kernels: 90.2 us -> 80.4 us  [attn_out(): pl.pallas_call(functools.partial(out_kernel, n=n, n_grp=n_grp, chunks=chu...]
    pallas_call x1, Pallas kernels: 8.52 us -> 17.1 us  [attn_bwd(): pl.pallas_call(functools.partial(attn_bwd_kernel, nb=nb, seqs=grps.shape[...]
    pallas_call x1, Pallas kernels: 248 us -> 239 us  [feed_forward(): pl.pallas_call(functools.partial(ffn_kernel, n=n, chunks=chunks, rows=row...]
  transfers between devices with their start and end apart: 1 -> 1, of which waited for: 0 -> 1; matrix products, arithmetic and copies ran while one was open for 0% -> 0% of each run, Pallas kernels for 22% -> 21%
where the time goes in v6:
time: 547 us; the launch traced here: 539 us
  Pallas kernels  492 us (90%)
  local copies, waits for them, and re-layouts  24.5 us (4%)
  between operations  14.7 us (3%)
    pallas_call x1, Pallas kernels, feed_forward(): pl.pallas_call(functools.partial(ffn_kernel, n=n, chunks=chunks, rows=row...  239 us
    pallas_call x1, Pallas kernels, project_back(): pl.pallas_call(functools.partial(back_kernel, n=n, n_grp=n_grp, chunks=ch...  98.7 us
    pallas_call x1, Pallas kernels, attn_out(): pl.pallas_call(functools.partial(out_kernel, n=n, n_grp=n_grp, chunks=chu...  80.4 us
    pallas_call x1, Pallas kernels, front(): pl.pallas_call(functools.partial(front_kernel, n=n, n_grp=n_grp, parts=pa...  46.4 us
    unnamed x56, local copies, waits for them, and re-layouts  19.9 us
    pallas_call x1, Pallas kernels, attn_bwd(): pl.pallas_call(functools.partial(attn_bwd_kernel, nb=nb, seqs=grps.shape[...  17.1 us
  transfers between devices with their start and end apart: 1, of which 1 were waited for; matrix products, arithmetic and copies ran while one was open for 0% of the time, Pallas kernels for 21%

profile of v6, /device:TPU:0, one launch (start us, length us, event | category | flops | bytes accessed | tf_op | source)
XLA Modules:
  0.0 539.1 jit_solution(18296364888898688576)
XLA Ops:
  7.2 0.0 reduce-scatter.2.cloned.1.call-start
  7.2 0.7 pad_maximum_fusion.1.vec
  8.0 1.3 fusion
  9.3 1.0 copy-done.9
  10.3 0.7 copy-done.10
  11.0 46.4 %front.1 = (bf16[2048,768]{1,0:T(8,128)(2,1)}, bf16[2048,2048]{1,0:T(8,128)(2,1)}, bf16[2048,768]{1,0:T(8,128)(2,1)}, bf16[2048,256]{1,0:T(8,128)(2,1)S(1)}, bf1...) custom-call(bf16[2048,2048]{1,0:T(8,128)(2,1)} %x_hbm.1, f32[512,768]{1,0:T(8,128)} %w_qkv.1, ...), custom_call_target="tpu_custom_call" | custom-call | flops 6442450944 | bytes 16777216 | tf_op jit(solution)/shard_map/front/pallas_call | solution.py:601
  57.5 0.0 copy-start.2
  57.5 2.2 copy-done.13
  59.8 10.1 %attn_fwd.1 = (bf16[2048,256]{1,0:T(8,128)(2,1)S(1)}, f32[2,1,2048]{2,1,0:T(1,128)S(1)}) custom-call(s32[6]{0:T(128)S(1)} %copy-done.4, s32[6]{0:T(128)S(1)} %copy-done.5, bf16[2048,768]{1,0:T(8,128)(2,1)S(1)} %copy-done.13), custom_call_target="tpu_custom_call" | custom-call | flops 2147483648 | bytes 4194304 | tf_op jit(solution)/shard_map/attn_fwd/pallas_call | solution.py:75
  69.9 0.7 pad_maximum_fusion.2.vec
  70.7 80.4 %attn_out.1 = (f32[256,2048]{1,0:T(8,128)S(1)}, bf16[256,2048]{1,0:T(8,128)(2,1)S(1)}, bf16[2048,1024]{1,0:T(8,128)(2,1)S(1)}, bf16[2048,1024]{1,0:T(8,128)(2,1)}) custom-call(bf16[8,256,256]{2,1,0:T(8,128)(2,1)S(1)} %bitcast.28, bf16[2048,256]{1,0:T(8,128)(2,1)S(1)} %get-tuple-element.40.w_out.out_hbm, f32[3,2048]{1,0:T(4,128)S(1)} %pad_maximum_fusion.vec, ...), custom_call_target="tpu_custom_call" | custom-call | flops 2147483648 | bytes 8388608 | tf_op jit(solution)/shard_map/attn_out/pallas_call | solution.py:503
  151.1 2.0 copy-done.6
  153.1 1.3 copy-done.7
  154.5 1.0 copy-done.8
  155.4 239.4 %feed_forward.1 = (bf16[2048,2048]{1,0:T(8,128)(2,1)}, bf16[2048,256]{1,0:T(8,128)(2,1)}, bf16[8,256,256]{2,1,0:T(8,128)(2,1)}, f32[256,2048]{1,0:T(8,128)}, bf1...) custom-call(bf16[256,2048]{1,0:T(8,128)(2,1)} %copy-done.8, bf16[8,256,2048]{2,1,0:T(8,128)(2,1)} %bitcast.51, ...), custom_call_target="tpu_custom_call" | custom-call | flops 51539607552 | bytes 67108864 | tf_op jit(solution)/shard_map/feed_forward/pallas_call | solution.py:1051
  394.9 0.0 reduce-scatter.2.cloned.1.call-update
  394.9 1.2 copy-done.1
  396.1 0.3 copy-done.12
  396.4 1.9 copy-done.14
  398.3 17.1 %attn_bwd.1 = bf16[2048,768]{1,0:T(8,128)(2,1)S(1)} custom-call(s32[6]{0:T(128)S(1)} %copy-done.4, s32[6]{0:T(128)S(1)} %copy-done.5, bf16[2048,768]{1,0:T(8,128)(2,1)S(1)} %copy-done.14, bf16[2048,256]{1,0:T(8,128)(2,1)S(1)} %copy-done.1, bf16[2048,256]{1,0:T(8,128)(2,1)S(1)} %bitcast.34, f32[2,1,2048]{2,1,0:T(1,128)S(1)} %get-tuple-element.49.lse_ref), custom_call_target="tpu_custom_call" | custom-call | flops 5368709120 | bytes 8388608 | tf_op jit(solution)/shard_map/attn_bwd/pallas_call | solution.py:131
  415.4 1.6 copy-done.11
  417.0 98.7 %project_back.1 = (f32[256,2048]{1,0:T(8,128)}, f32[512,768]{1,0:T(8,128)S(1)}, f32[512,256]{1,0:T(8,128)S(1)}, f32[8,2048]{1,0:T(8,128)S(1)}, f32[8,2048]{1,0:T(8,128)S(1)}) custom-call(bf16[8,256,768]{2,1,0:T(8,128)(2,1)} %bitcast.33, bf16[2048,768]{1,0:T(8,128)(2,1)} %get-tuple-element.50.w_attn, bf16[2048,2048]{1,0:T(8,128)(2,1)} %get-tuple-element.51.n1_hbm, ...), custom_call_target="tpu_custom_call" | custom-call | flops 12884901888 | bytes 16777216 | tf_op jit(solution)/shard_map/project_back/pallas_call | solution.py:819
  515.8 0.6 copy.33
  516.4 0.6 copy.30
  517.0 0.6 fusion.2
  517.6 4.9 reduce-scatter.2.cloned.1.call-done
  522.5 4.0 fusion.1
  526.5 1.0 copy.38
  527.5 1.0 copy-done.18
  528.5 1.3 copy.39
  529.8 1.1 copy.40
  531.0 0.8 copy.41
  (39 shorter events, 0.1 us)
Async XLA Ops:
  7.2 515.3 %reduce-scatter.2.cloned.1.call-start = ((), (), s32[]{:S(2)}) async-start(), calls=%async_computation.1 | async-start | bytes 10485760 | tf_op jit(solution)/shard_map/reduce_scatter | solution.py:1089
  9.3 1.0 copy-start.9
  10.3 0.7 copy-start.10
  11.0 46.4 %copy-start.4 = (s32[6]{0:T(128)S(1)}, s32[6]{0:T(128)}, u32[]{:S(2)}) copy-start(s32[6]{0:T(128)} %grps.3) | copy-start | bytes 76
  11.0 46.4 %copy-start.5 = (s32[6]{0:T(128)S(1)}, s32[6]{0:T(128)}, u32[]{:S(2)}) copy-start(s32[6]{0:T(128)} %lens.3) | copy-start | bytes 76
  57.5 13.2 %copy-start.2 = (bf16[2048,256]{1,0:T(8,128)(2,1)}, bf16[2048,256]{1,0:T(8,128)(2,1)S(1)}, u32[]{:S(2)}) copy-start(bf16[2048,256]{1,0:T(8,128)(2,1)S(1)} %get-tuple-element.40.w_out.out_hbm) | copy-start | bytes 3145732
  57.5 2.3 copy-start.13
  59.7 10.2 %copy-start.20 = (f32[2048]{0:T(1024)S(1)}, f32[2048]{0:T(1024)}, u32[]{:S(2)}) copy-start(f32[2048]{0:T(1024)} %param.30) | copy-start | bytes 24580
  59.7 10.2 %copy-start.23 = (f32[2048]{0:T(1024)S(1)}, f32[2048]{0:T(1024)}, u32[]{:S(2)}) copy-start(f32[2048]{0:T(1024)} %param.27) | copy-start | bytes 24580
  59.7 10.9 %copy-start.21 = (f32[2048]{0:T(1024)S(1)}, f32[2048]{0:T(1024)}, u32[]{:S(2)}) copy-start(f32[2048]{0:T(1024)} %param.31) | copy-start | bytes 24580
  59.8 10.9 %copy-start.22 = (f32[2048]{0:T(1024)S(1)}, f32[2048]{0:T(1024)}, u32[]{:S(2)}) copy-start(f32[2048]{0:T(1024)} %param.23) | copy-start | bytes 24580
  69.9 81.2 %copy-start = (bf16[2048,256]{1,0:T(8,128)(2,1)}, bf16[2048,256]{1,0:T(8,128)(2,1)S(1)}, u32[]{:S(2)}) copy-start(bf16[2048,256]{1,0:T(8,128)(2,1)S(1)} %get-tuple-element.39.o_ref) | copy-start | bytes 3145732
  151.1 2.0 copy-start.6
  153.1 1.3 copy-start.7
  154.5 1.0 copy-start.8
  394.9 1.2 copy-start.1
  394.9 1.5 copy-start.12
  396.4 1.9 copy-start.14
  398.3 18.7 %copy-start.3 = (f32[2048]{0:T(1024)S(1)}, f32[2048]{0:T(1024)}, u32[]{:S(2)}) copy-start(f32[2048]{0:T(1024)} %param.28) | copy-start | bytes 24580
  398.3 18.7 %copy-start.15 = (bf16[2048,256]{1,0:T(8,128)(2,1)S(1)}, bf16[2048,256]{1,0:T(8,128)(2,1)}, u32[]{:S(2)}) copy-start(bf16[2048,256]{1,0:T(8,128)(2,1)} %get-tuple-element.52.gw_proj) | copy-start | bytes 3145732
  398.3 18.7 %copy-start.16 = (f32[8,2048]{1,0:T(8,128)S(1)}, f32[8,2048]{1,0:T(8,128)}, u32[]{:S(2)}) copy-start(f32[8,2048]{1,0:T(8,128)} %get-tuple-element.54.stats) | copy-start | bytes 196612
  398.3 18.7 %copy-start.17 = (f32[1,1024]{1,0:T(1,128)S(1)}, f32[1,1024]{1,0:T(1,128)}, u32[]{:S(2)}) copy-start(f32[1,1024]{1,0:T(1,128)} %get-tuple-element.55.up_sum) | copy-start | bytes 12292
  415.4 1.6 copy-start.11
  517.6 8.9 %copy-start.19 = (bf16[256,2048]{1,0:T(8,128)(2,1)S(1)}, bf16[256,2048]{1,0:T(8,128)(2,1)}, u32[]{:S(2)}) copy-start(bf16[256,2048]{1,0:T(8,128)(2,1)} %get-tuple-element.84) | copy-start | bytes 3145732
  526.5 2.0 copy-start.18
Sparse Core Ops, SparseCore 0:
  395.0 127.4 reduce-scatter.1

commit v7 on v6

--- a/solution.py
+++ b/solution.py
@@ -17,124 +17,142 @@
     return lax.dot_general(a,b,(((ca,),(cb,)),((),())),preferred_element_type=F32)
 
 
-def block_info(grps, lens, nb, seqs):
+def group_tokens(grps, lens, seqs):
     g = lax.axis_index("grp")
-    found = [[jnp.int32(0), jnp.int32(0), jnp.int32(0)] for _ in range(nb)]
-    start = jnp.int32(0)
+    tokens, longest = jnp.int32(0), jnp.int32(0)
     for s in range(seqs):
-        count = jnp.where(grps[s] == g, lens[s] // BLK, 0)
-        for b in range(nb):
-            hit = (start <= b) & (b < start + count)
-            found[b] = [jnp.where(hit, start, found[b][0]), jnp.where(hit, start + count - 1, found[b][1]),
-                        jnp.where(hit, 1, found[b][2])]
-        start = start + count
-    return found
+        count = jnp.where(grps[s] == g, lens[s], 0)
+        tokens, longest = tokens + count, jnp.maximum(longest, count)
+    return tokens, longest > BLK
 
 
 def below(shape):
     return lax.broadcasted_iota(jnp.int32, shape, 0) <= lax.broadcasted_iota(jnp.int32, shape, 1)
 
 
-def attn_fwd_kernel(grps, lens, proj, o_ref, lse_ref, *, nb, seqs, heads):
-    info = block_info(grps, lens, nb, seqs)
+def attn_fwd_kernel(grps, lens, q_ref, k_ref, v_ref, o_ref, lse_ref, *, nb, seqs):
+    tokens, is_long = group_tokens(grps, lens, seqs)
     c = HD ** -0.5 * LOG2E
 
-    def attend(qi, first):
-        rows = slice(qi * BLK, (qi + 1) * BLK)
-        early = slice(first * BLK, qi * BLK)
-        for h in range(heads):
-            col = 3 * h * HD
-            q = proj[rows, col:col + HD]
-            pieces = [(rows, jnp.where(below((BLK, BLK)), dg(proj[rows, col + HD:col + 2 * HD], q, 1, 1), -1e30))]
-            if first < qi:
-                pieces.append((early, dg(proj[early, col + HD:col + 2 * HD], q, 1, 1)))
-            top = functools.reduce(jnp.maximum, [jnp.max(s, 0, keepdims=True) for _, s in pieces]) * c
-            total, acc = 0.0, 0.0
-            for keys, s in pieces:
-                p = jnp.exp2(s * c - top)
-                total = total + jnp.sum(p, 0, keepdims=True)
-                acc = acc + dg(proj[keys, col + 2 * HD:col + 3 * HD], p.astype(BF), 0, 0)
-            o_ref[rows, h * HD:(h + 1) * HD] = jnp.transpose(acc / total).astype(BF)
-            lse_ref[h, :, rows] = top + jnp.log2(total)
-
-    for qi in range(nb):
-        for first in range(qi + 1):
-            @pl.when((info[qi][2] > 0) & (info[qi][0] == first))
+    def attend(rows, early):
+        q = q_ref[rows, :]
+        pieces = [(rows, jnp.where(below((BLK, BLK)), dg(k_ref[rows, :], q, 1, 1), -1e30))]
+        if early is not None:
+            pieces.append((early, dg(k_ref[early, :], q, 1, 1)))
+        top = functools.reduce(jnp.maximum, [jnp.max(s, 0, keepdims=True) for _, s in pieces]) * c
+        total, acc = 0.0, 0.0
+        for keys, s in pieces:
+            p = jnp.exp2(s * c - top)
+            total = total + jnp.sum(p, 0, keepdims=True)
+            acc = acc + dg(v_ref[keys, :], p.astype(BF), 0, 0)
+        o_ref[rows, :] = jnp.transpose(acc / total).astype(BF)
+        lse_ref[0, :, rows] = top + jnp.log2(total)
+
+    @pl.when(is_long)
+    def _():
+        for i in range(nb):
+            attend(slice(i * BLK, (i + 1) * BLK), slice(0, i * BLK) if i else None)
+
+    @pl.when(jnp.logical_not(is_long))
+    def _():
+        def block(i, carry):
+            rows = pl.ds(pl.multiple_of(i * BLK, BLK), BLK)
+
+            @pl.when(i * BLK < tokens)
             def _():
-                attend(qi, first)
-
-        @pl.when(info[qi][2] <= 0)
-        def _():
-            o_ref[qi * BLK:(qi + 1) * BLK, :] = jnp.zeros((BLK, heads * HD), BF)
-            lse_ref[:, :, qi * BLK:(qi + 1) * BLK] = jnp.zeros((heads, 1, BLK), F32)
+                attend(rows, None)
+
+            @pl.when(i * BLK >= tokens)
+            def _():
+                o_ref[rows, :] = jnp.zeros((BLK, HD), BF)
+                lse_ref[0, :, rows] = jnp.zeros((1, BLK), F32)
+            return carry
+        lax.fori_loop(0, nb, block, 0)
 
 
 def attn_fwd(grps, lens, proj):
-    length = proj.shape[0]; heads = proj.shape[1]//(3*HD); nb = length//BLK
-    vm, sm = pl.BlockSpec(memory_space=pltpu.VMEM), pl.BlockSpec(memory_space=pltpu.SMEM)
-    return pl.pallas_call(functools.partial(attn_fwd_kernel, nb=nb, seqs=grps.shape[0], heads=heads),
-        in_specs=[sm, sm, vm], out_specs=[vm, vm],
-        out_shape=[jax.ShapeDtypeStruct((length, heads*HD), BF), jax.ShapeDtypeStruct((heads, 1, length), F32)],
-        compiler_params=pltpu.CompilerParams(vmem_limit_bytes=40<<20), name="attn_fwd",
-        cost_estimate=pl.CostEstimate(flops=heads*length*length*HD*2, bytes_accessed=length*heads*HD*8, transcendentals=heads*length*length//2),
-    )(grps, lens, proj)
-
-
-def attn_bwd_kernel(grps, lens, proj, o_ref, do_ref, lse_ref, dp_ref, dq_sc, dl_sc, *, nb, seqs, heads):
-    info = block_info(grps, lens, nb, seqs)
+    length, heads = proj.shape[0], proj.shape[1] // (3 * HD)
+    spec = lambda o: pl.BlockSpec((length, HD), lambda h, grps, lens: (0, 3 * h + o))
+    return pl.pallas_call(
+        functools.partial(attn_fwd_kernel, nb=length // BLK, seqs=grps.shape[0]),
+        grid_spec=pltpu.PrefetchScalarGridSpec(
+            num_scalar_prefetch=2, grid=(heads,), in_specs=[spec(0), spec(1), spec(2)],
+            out_specs=[pl.BlockSpec((length, HD), lambda h, grps, lens: (0, h)),
+                       pl.BlockSpec((1, 1, length), lambda h, grps, lens: (h, 0, 0))]),
+        out_shape=[jax.ShapeDtypeStruct((length, heads * HD), BF), jax.ShapeDtypeStruct((heads, 1, length), F32)],
+        compiler_params=pltpu.CompilerParams(vmem_limit_bytes=40 << 20),
+        cost_estimate=pl.CostEstimate(flops=heads * length * length * HD * 2, bytes_accessed=length * heads * HD * 8,
+                                      transcendentals=heads * length * length // 2),
+        name="attn_fwd",
+    )(grps, lens, proj, proj, proj)
+
+
+def attn_bwd_kernel(grps, lens, q_ref, k_ref, v_ref, o_ref, do_ref, lse_ref, dp_ref, dq_sc, dl_sc, *, nb, seqs):
+    tokens, is_long = group_tokens(grps, lens, seqs)
     scale = HD ** -0.5
     c = scale * LOG2E
-    for h in range(heads):
-        hc = slice(h * HD, (h + 1) * HD)
-        prod = do_ref[:, hc].astype(F32) * o_ref[:, hc].astype(F32)
-        dl_sc[h] = jnp.sum(jnp.transpose(prod), 0, keepdims=True)
-    dq_sc[...] = jnp.zeros_like(dq_sc)
-
-    def attend(j, last):
-        keys = slice(j * BLK, (j + 1) * BLK)
-        for h in range(heads):
-            col = 3 * h * HD
-            hc = slice(h * HD, (h + 1) * HD)
-            k, v = proj[keys, col + HD:col + 2 * HD], proj[keys, col + 2 * HD:col + 3 * HD]
-            dk, dv = 0.0, 0.0
-            for diag in (True, False):
-                rows = keys if diag else slice((j + 1) * BLK, (last + 1) * BLK)
-                if rows.start == rows.stop:
-                    continue
-                q, do = proj[rows, col:col + HD], do_ref[rows, hc]
-                p = jnp.exp2(dg(k, q, 1, 1) * c - lse_ref[h, :, rows])
-                if diag:
-                    p = jnp.where(below((BLK, BLK)), p, 0.0)
-                ds = (p * (dg(v, do, 1, 1) - dl_sc[h, :, rows])).astype(BF)
-                dv = dv + dg(p.astype(BF), do, 1, 0)
-                dk = dk + dg(ds, q, 1, 0)
-                dq_sc[h, :, rows] += dg(k, ds, 0, 0)
-            dp_ref[keys, col + HD:col + 2 * HD] = (dk * scale).astype(BF)
-            dp_ref[keys, col + 2 * HD:col + 3 * HD] = dv.astype(BF)
-
-    for j in range(nb):
-        for last in range(j, nb):
-            @pl.when((info[j][2] > 0) & (info[j][1] == last))
+    prod = do_ref[...].astype(F32) * o_ref[...].astype(F32)
+    dl_sc[...] = jnp.sum(jnp.transpose(prod), 0, keepdims=True)
+
+    def attend(keys, later, first):
+        k, v = k_ref[keys, :], v_ref[keys, :]
+        dk, dv = 0.0, 0.0
+        for diag, rows in ((True, keys), (False, later)):
+            if rows is None:
+                continue
+            q, do = q_ref[rows, :], do_ref[rows, :]
+            p = jnp.exp2(dg(k, q, 1, 1) * c - lse_ref[0, :, rows])
+            if diag:
+                p = jnp.where(below((BLK, BLK)), p, 0.0)
+            ds = (p * (dg(v, do, 1, 1) - dl_sc[:, rows])).astype(BF)
+            dv = dv + dg(p.astype(BF), do, 1, 0)
+            dk = dk + dg(ds, q, 1, 0)
+            dq = dg(k, ds, 0, 0)
+            dq_sc[:, rows] = dq if first else dq_sc[:, rows] + dq
+        dp_ref[keys, HD:2 * HD] = (dk * scale).astype(BF)
+        dp_ref[keys, 2 * HD:] = dv.astype(BF)
+
+    @pl.when(is_long)
+    def _():
+        for j in range(nb):
+            attend(slice(j * BLK, (j + 1) * BLK), slice((j + 1) * BLK, nb * BLK) if j < nb - 1 else None, j == 0)
+
+    @pl.when(jnp.logical_not(is_long))
+    def _():
+        def block(i, carry):
+            rows = pl.ds(pl.multiple_of(i * BLK, BLK), BLK)
+
+            @pl.when(i * BLK < tokens)
             def _():
-                attend(j, last)
-
-        @pl.when(info[j][2] <= 0)
-        def _():
-            dp_ref[j * BLK:(j + 1) * BLK, :] = jnp.zeros((BLK, heads * 3 * HD), BF)
-    for h in range(heads):
-        dp_ref[:, 3 * h * HD:(3 * h + 1) * HD] = jnp.transpose(dq_sc[h] * scale).astype(BF)
+                attend(rows, None, True)
+
+            @pl.when(i * BLK >= tokens)
+            def _():
+                dp_ref[rows, :] = jnp.zeros((BLK, 3 * HD), BF)
+                dq_sc[:, rows] = jnp.zeros((HD, BLK), F32)
+            return carry
+        lax.fori_loop(0, nb, block, 0)
+    dp_ref[:, :HD] = jnp.transpose(dq_sc[...] * scale).astype(BF)
 
 
 def attn_bwd(grps, lens, proj, ctx, dctx, lse):
-    length = proj.shape[0]; heads = proj.shape[1]//(3*HD); nb = length//BLK
-    vm, sm = pl.BlockSpec(memory_space=pltpu.VMEM), pl.BlockSpec(memory_space=pltpu.SMEM)
-    return pl.pallas_call(functools.partial(attn_bwd_kernel, nb=nb, seqs=grps.shape[0], heads=heads),
-        in_specs=[sm, sm] + [vm]*4, out_specs=vm,
-        scratch_shapes=[pltpu.VMEM((heads, HD, length), F32), pltpu.VMEM((heads, 1, length), F32)],
-        out_shape=jax.ShapeDtypeStruct((length, heads*3*HD), BF),
-        compiler_params=pltpu.CompilerParams(vmem_limit_bytes=40<<20), name="attn_bwd",
-        cost_estimate=pl.CostEstimate(flops=heads*length*length*HD*5, bytes_accessed=length*heads*HD*16, transcendentals=heads*length*length//2),
-    )(grps, lens, proj, ctx, dctx, lse)
+    length, heads = proj.shape[0], proj.shape[1] // (3 * HD)
+    spec = lambda o: pl.BlockSpec((length, HD), lambda h, grps, lens: (0, 3 * h + o))
+    head = pl.BlockSpec((length, HD), lambda h, grps, lens: (0, h))
+    return pl.pallas_call(
+        functools.partial(attn_bwd_kernel, nb=length // BLK, seqs=grps.shape[0]),
+        grid_spec=pltpu.PrefetchScalarGridSpec(
+            num_scalar_prefetch=2, grid=(heads,),
+            in_specs=[spec(0), spec(1), spec(2), head, head,
+                      pl.BlockSpec((1, 1, length), lambda h, grps, lens: (h, 0, 0))],
+            out_specs=pl.BlockSpec((length, 3 * HD), lambda h, grps, lens: (0, h)),
+            scratch_shapes=[pltpu.VMEM((HD, length), F32), pltpu.VMEM((1, length), F32)]),
+        out_shape=jax.ShapeDtypeStruct((length, heads * 3 * HD), BF),
+        compiler_params=pltpu.CompilerParams(vmem_limit_bytes=40 << 20),
+        cost_estimate=pl.CostEstimate(flops=heads * length * length * HD * 5, bytes_accessed=length * heads * HD * 16,
+                                      transcendentals=heads * length * length // 2),
+        name="attn_bwd",
+    )(grps, lens, proj, proj, proj, ctx, dctx, lse)
 
 
 MESH = pl.DeviceIdType.MESH

time: 547 us -> 539 us (0.985)
  transfers between devices with their start and end apart: 1 -> 1, of which waited for: 1 -> 1; matrix products, arithmetic and copies ran while one was open for 0% -> 0% of each run, Pallas kernels for 21% -> 22%
where the time goes in v7:
time: 539 us; the launch traced here: 536 us
  Pallas kernels  492 us (91%)
  local copies, waits for them, and re-layouts  25.4 us (5%)
  between operations  14.2 us (3%)
    pallas_call x1, Pallas kernels, feed_forward(): pl.pallas_call(functools.partial(ffn_kernel, n=n, chunks=chunks, rows=row...  240 us
    pallas_call x1, Pallas kernels, project_back(): pl.pallas_call(functools.partial(back_kernel, n=n, n_grp=n_grp, chunks=ch...  98.9 us
    pallas_call x1, Pallas kernels, attn_out(): pl.pallas_call(functools.partial(out_kernel, n=n, n_grp=n_grp, chunks=chu...  80.4 us
    pallas_call x1, Pallas kernels, front(): pl.pallas_call(functools.partial(front_kernel, n=n, n_grp=n_grp, parts=pa...  46.4 us
    unnamed x56, local copies, waits for them, and re-layouts  20.8 us
    pallas_call x1, Pallas kernels, attn_bwd(): pl.pallas_call(functools.partial(attn_bwd_kernel, nb=length // BLK, seqs=...  16.6 us
  transfers between devices with their start and end apart: 1, of which 1 were waited for; matrix products, arithmetic and copies ran while one was open for 0% of the time, Pallas kernels for 22%

profile of v7, /device:TPU:0, one launch (start us, length us, event | category | flops | bytes accessed | tf_op | source)
XLA Modules:
  0.0 536.3 jit_solution(10619971052082172010)
XLA Ops:
  7.2 0.0 reduce-scatter.2.cloned.1.call-start
  7.2 0.7 pad_maximum_fusion.1.vec
  8.0 1.3 fusion
  9.3 1.0 copy-done.11
  10.3 0.7 copy-done.12
  11.0 46.4 %front.1 = (bf16[2048,768]{1,0:T(8,128)(2,1)}, bf16[2048,2048]{1,0:T(8,128)(2,1)}, bf16[2048,768]{1,0:T(8,128)(2,1)}, bf16[2048,256]{1,0:T(8,128)(2,1)S(1)}, bf1...) custom-call(bf16[2048,2048]{1,0:T(8,128)(2,1)} %x_hbm.1, f32[512,768]{1,0:T(8,128)} %w_qkv.1, ...), custom_call_target="tpu_custom_call" | custom-call | flops 6442450944 | bytes 16777216 | tf_op jit(solution)/shard_map/front/pallas_call | solution.py:619
  57.5 0.0 copy-start.4
  57.5 2.2 copy-done
  59.8 9.4 %attn_fwd.1 = (bf16[2048,256]{1,0:T(8,128)(2,1)S(1)}, f32[2,1,2048]{2,1,0:T(1,128)S(1)}) custom-call(s32[6]{0:T(128)S(1)} %copy-done.6, s32[6]{0:T(128)S(1)} %copy-done.7, bf16[2048,768]{1,0:T(8,128)(2,1)S(1)} %copy-done, bf16[2048,768]{1,0:T(8,128)(2,1)S(1)} %copy-done, bf16[2048,768]{1,0:T(8,128)(2,1)S(1)} %copy-done), custom_call_target="tpu_custom_call" | custom-call | flops 2147483648 | bytes 4194304 | tf_op jit(solution)/shard_map/attn_fwd/pallas_call | solution.py:76
  69.2 0.7 pad_maximum_fusion.2.vec
  69.9 80.4 %attn_out.1 = (f32[256,2048]{1,0:T(8,128)S(1)}, bf16[256,2048]{1,0:T(8,128)(2,1)S(1)}, bf16[2048,1024]{1,0:T(8,128)(2,1)S(1)}, bf16[2048,1024]{1,0:T(8,128)(2,1)}) custom-call(bf16[8,256,256]{2,1,0:T(8,128)(2,1)S(1)} %bitcast.28, bf16[2048,256]{1,0:T(8,128)(2,1)S(1)} %get-tuple-element.40.w_out.out_hbm, f32[3,2048]{1,0:T(4,128)S(1)} %pad_maximum_fusion.vec, ...), custom_call_target="tpu_custom_call" | custom-call | flops 2147483648 | bytes 8388608 | tf_op jit(solution)/shard_map/attn_out/pallas_call | solution.py:521
  150.4 2.0 copy-done.8
  152.4 1.3 copy-done.9
  153.7 1.0 copy-done.10
  154.7 239.9 %feed_forward.1 = (bf16[2048,2048]{1,0:T(8,128)(2,1)}, bf16[2048,256]{1,0:T(8,128)(2,1)}, bf16[8,256,256]{2,1,0:T(8,128)(2,1)}, f32[256,2048]{1,0:T(8,128)}, bf1...) custom-call(bf16[256,2048]{1,0:T(8,128)(2,1)} %copy-done.10, bf16[8,256,2048]{2,1,0:T(8,128)(2,1)} %bitcast.51, ...), custom_call_target="tpu_custom_call" | custom-call | flops 51539607552 | bytes 67108864 | tf_op jit(solution)/shard_map/feed_forward/pallas_call | solution.py:1069
  394.7 0.0 reduce-scatter.2.cloned.1.call-update
  394.7 1.9 copy-done.1
  396.5 1.2 copy-done.3
  397.8 1.2 copy-done.14
  399.0 16.6 %attn_bwd.1 = bf16[2048,768]{1,0:T(8,128)(2,1)S(1)} custom-call(s32[6]{0:T(128)S(1)} %copy-done.6, s32[6]{0:T(128)S(1)} %copy-done.7, bf16[2048,768]{1,0:T(8,128)(2,1)S(1)} %copy-done.1, bf16[2048,768]{1,0:T(8,128)(2,1)S(1)} %copy-done.1, bf16[2048,768]{1,0:T(8,128)(2,1)S(1)} %copy-done.1, bf16[2048,256]{1,0:T(8,128)(2,1)S(1)} %copy-done.3, ...), custom_call_target="tpu_custom_call" | custom-call | flops 5368709120 | bytes 8388608 | tf_op jit(solution)/shard_map/attn_bwd/pallas_call | solution.py:142
  415.7 1.6 copy-done.13
  417.3 98.9 %project_back.1 = (f32[256,2048]{1,0:T(8,128)}, f32[512,768]{1,0:T(8,128)S(1)}, f32[512,256]{1,0:T(8,128)S(1)}, f32[8,2048]{1,0:T(8,128)S(1)}, f32[8,2048]{1,0:T(8,128)S(1)}) custom-call(bf16[8,256,768]{2,1,0:T(8,128)(2,1)} %bitcast.33, bf16[2048,768]{1,0:T(8,128)(2,1)} %get-tuple-element.50.w_attn, bf16[2048,2048]{1,0:T(8,128)(2,1)} %get-tuple-element.51.n1_hbm, ...), custom_call_target="tpu_custom_call" | custom-call | flops 12884901888 | bytes 16777216 | tf_op jit(solution)/shard_map/project_back/pallas_call | solution.py:837
  516.2 0.6 copy.33
  516.8 0.6 copy.30
  517.4 0.6 fusion.2
  518.0 2.2 reduce-scatter.2.cloned.1.call-done
  520.2 4.0 fusion.1
  524.2 1.0 copy.38
  525.2 1.0 copy-done.18
  526.2 1.3 copy.39
  527.5 1.1 copy.40
  528.7 0.8 copy.41
  (39 shorter events, 0.1 us)
Async XLA Ops:
  7.2 513.0 %reduce-scatter.2.cloned.1.call-start = ((), (), s32[]{:S(2)}) async-start(), calls=%async_computation.1 | async-start | bytes 10485760 | tf_op jit(solution)/shard_map/reduce_scatter | solution.py:1107
  9.3 1.0 copy-start.11
  10.3 0.7 copy-start.12
  11.0 46.4 %copy-start.6 = (s32[6]{0:T(128)S(1)}, s32[6]{0:T(128)}, u32[]{:S(2)}) copy-start(s32[6]{0:T(128)} %grps.3) | copy-start | bytes 76
  11.0 46.4 %copy-start.7 = (s32[6]{0:T(128)S(1)}, s32[6]{0:T(128)}, u32[]{:S(2)}) copy-start(s32[6]{0:T(128)} %lens.3) | copy-start | bytes 76
  57.5 12.5 %copy-start.4 = (bf16[2048,256]{1,0:T(8,128)(2,1)}, bf16[2048,256]{1,0:T(8,128)(2,1)S(1)}, u32[]{:S(2)}) copy-start(bf16[2048,256]{1,0:T(8,128)(2,1)S(1)} %get-tuple-element.40.w_out.out_hbm) | copy-start | bytes 3145732
  57.5 2.3 copy-start
  59.7 9.4 %copy-start.20 = (f32[2048]{0:T(1024)S(1)}, f32[2048]{0:T(1024)}, u32[]{:S(2)}) copy-start(f32[2048]{0:T(1024)} %param.30) | copy-start | bytes 24580
  59.7 9.4 %copy-start.23 = (f32[2048]{0:T(1024)S(1)}, f32[2048]{0:T(1024)}, u32[]{:S(2)}) copy-start(f32[2048]{0:T(1024)} %param.27) | copy-start | bytes 24580
  59.7 10.1 %copy-start.21 = (f32[2048]{0:T(1024)S(1)}, f32[2048]{0:T(1024)}, u32[]{:S(2)}) copy-start(f32[2048]{0:T(1024)} %param.31) | copy-start | bytes 24580
  59.8 10.1 %copy-start.22 = (f32[2048]{0:T(1024)S(1)}, f32[2048]{0:T(1024)}, u32[]{:S(2)}) copy-start(f32[2048]{0:T(1024)} %param.23) | copy-start | bytes 24580
  69.2 81.2 %copy-start.2 = (bf16[2048,256]{1,0:T(8,128)(2,1)}, bf16[2048,256]{1,0:T(8,128)(2,1)S(1)}, u32[]{:S(2)}) copy-start(bf16[2048,256]{1,0:T(8,128)(2,1)S(1)} %get-tuple-element.39.o_ref) | copy-start | bytes 3145732
  150.4 2.0 copy-start.8
  152.4 1.3 copy-start.9
  153.7 1.0 copy-start.10
  394.6 1.9 copy-start.1
  396.5 1.2 copy-start.3
  397.8 1.2 copy-start.14
  399.0 18.3 %copy-start.5 = (f32[2048]{0:T(1024)S(1)}, f32[2048]{0:T(1024)}, u32[]{:S(2)}) copy-start(f32[2048]{0:T(1024)} %param.28) | copy-start | bytes 24580
  399.0 18.3 %copy-start.15 = (bf16[2048,256]{1,0:T(8,128)(2,1)S(1)}, bf16[2048,256]{1,0:T(8,128)(2,1)}, u32[]{:S(2)}) copy-start(bf16[2048,256]{1,0:T(8,128)(2,1)} %get-tuple-element.52.gw_proj) | copy-start | bytes 3145732
  399.0 18.3 %copy-start.16 = (f32[8,2048]{1,0:T(8,128)S(1)}, f32[8,2048]{1,0:T(8,128)}, u32[]{:S(2)}) copy-start(f32[8,2048]{1,0:T(8,128)} %get-tuple-element.54.stats) | copy-start | bytes 196612
  399.0 18.3 %copy-start.17 = (f32[1,1024]{1,0:T(1,128)S(1)}, f32[1,1024]{1,0:T(1,128)}, u32[]{:S(2)}) copy-start(f32[1,1024]{1,0:T(1,128)} %get-tuple-element.55.up_sum) | copy-start | bytes 12292
  415.6 1.6 copy-start.13
  518.0 6.2 %copy-start.19 = (bf16[256,2048]{1,0:T(8,128)(2,1)S(1)}, bf16[256,2048]{1,0:T(8,128)(2,1)}, u32[]{:S(2)}) copy-start(bf16[256,2048]{1,0:T(8,128)(2,1)} %get-tuple-element.84) | copy-start | bytes 3145732
  524.2 2.0 copy-start.18
Sparse Core Ops, SparseCore 0:
  394.8 125.3 reduce-scatter.1

commit v8 on v7

--- a/solution.py
+++ b/solution.py
@@ -438,9 +438,9 @@
         lhs = lhs_ref[:, chunk_rows(c, rows), :].reshape(at.n * rows, lhs_ref.shape[2])
 
         def tile(i):
-            y = dg(lhs, w_ref[cols(i), :], 1, 1)
-            rs.parts[:, :, :, cols(i)] = y.astype(BF).reshape(at.Z, 2, rows, TILE)
-        tiles(w_ref.shape[0] // TILE, tile)
+            y = dg(lhs, w_ref[cols(i, 1024), :], 1, 1)
+            rs.parts[:, :, :, cols(i, 1024)] = y.astype(BF).reshape(at.Z, 2, rows, 1024)
+        tiles(w_ref.shape[0] // 1024, tile)
         rs.start(c)
 
     def tick(i, carry):
@@ -575,12 +575,12 @@
         r = chunk_rows(b, block)
 
         def tile(i):
-            m = chunk_rows(i, rows)
+            m = chunk_rows(i, 2 * rows)
             y = dg(n1[m, r], w_attn[r, :], 1, 0)
             if not first:
                 y = y + acc[m, :]
             acc[m, :] = y
-        tiles(parts, tile)
+        tiles(parts // 2, tile)
 
     p, q, P = at.g // 2, lax.rem(at.g, 2), n_grp // 2
     partial(at.g, True)
@@ -719,9 +719,9 @@
         qv[...] += jnp.sum(lhs.astype(F32), 0, keepdims=True)
 
         def tile(i):
-            y = dg(lhs, w_attn[cols(i), :], 1, 1)
-            rs.parts[:, :, :, cols(i)] = y.astype(BF).reshape(at.Z, 2, rows, TILE)
-        tiles(width // TILE, tile)
+            y = dg(lhs, w_attn[cols(i, 1024), :], 1, 1)
+            rs.parts[:, :, :, cols(i, 1024)] = y.astype(BF).reshape(at.Z, 2, rows, 1024)
+        tiles(width // 1024, tile)
         rs.start(c)
 
     def weights(i):
@@ -908,39 +908,39 @@
         keep[...] = alive(n, 0, c)
 
         def tile(i):
-            v = dg(wide(c), w_up[:, cols(i)], 1, 0) + b_up[:, cols(i)]
-            ga = dg(gbuf[slot].reshape(m, width), w_down[:, cols(i)], 1, 0)
+            v = dg(wide(c), w_up[:, cols(i, 512)], 1, 0) + b_up[:, cols(i, 512)]
+            ga = dg(gbuf[slot].reshape(m, width), w_down[:, cols(i, 512)], 1, 0)
             v2 = v * v
             th = jnp.tanh(a0 * (v + a1 * v2 * v))
             half = 0.5 * (1.0 + th)
-            actb[:, cols(i)] = (v * half * keep[...]).astype(BF)
+            actb[:, cols(i, 512)] = (v * half * keep[...]).astype(BF)
             slope = half + 0.5 * v * (1.0 - th * th) * (a0 * (1.0 + 3.0 * a1 * v2))
             db = (ga * slope * keep[...]).astype(BF)
-            dbb[:, cols(i)] = db
-            bsum[:, cols(i)] += jnp.sum(db.astype(F32), 0, keepdims=True)
-        tiles(hid // TILE, tile)
+            dbb[:, cols(i, 512)] = db
+            bsum[:, cols(i, 512)] += jnp.sum(db.astype(F32), 0, keepdims=True)
+        tiles(hid // 512, tile)
 
     def back(c):
         def tile(i):
-            y = dg(dbb[...], w_up[cols(i), :], 1, 1)
-            rs.parts[:, :, :, cols(i)] = y.astype(BF).reshape(at.Z, 2, rows, TILE)
-        tiles(width // TILE, tile)
+            y = dg(dbb[...], w_up[cols(i, 1024), :], 1, 1)
+            rs.parts[:, :, :, cols(i, 1024)] = y.astype(BF).reshape(at.Z, 2, rows, 1024)
+        tiles(width // 1024, tile)
 
     def down(c):
         def tile(i):
-            y = dg(actb[...], w_down[cols(i), :], 1, 1)
-            mlp.parts[:, :, :, cols(i)] = y.astype(BF).reshape(at.Z, 2, rows, TILE)
-        tiles(width // TILE, tile)
+            y = dg(actb[...], w_down[cols(i, 1024), :], 1, 1)
+            mlp.parts[:, :, :, cols(i, 1024)] = y.astype(BF).reshape(at.Z, 2, rows, 1024)
+        tiles(width // 1024, tile)
 
     def weights(c):
         slot = lax.rem(c, 2)
 
         def tile(i):
-            x = gat[:, chunk_rows(c, rows), cols(i)].reshape(m, TILE)
-            acc_up[cols(i), :] += dg(x, dbb[...], 0, 0)
-            y = gbuf[slot, :, :, cols(i)].reshape(m, TILE)
-            acc_down[cols(i), :] += dg(y, actb[...], 0, 0)
-        tiles(width // TILE, tile)
+            x = gat[:, chunk_rows(c, rows), cols(i, 512)].reshape(m, 512)
+            acc_up[cols(i, 512), :] += dg(x, dbb[...], 0, 0)
+            y = gbuf[slot, :, :, cols(i, 512)].reshape(m, 512)
+            acc_down[cols(i, 512), :] += dg(y, actb[...], 0, 0)
+        tiles(width // 512, tile)
 
     def norm_grad(c):
         r = chunk_rows(c, rows)
@@ -959,9 +959,9 @@
 
     def heads(c):
         def tile(i):
-            x = gat[:, chunk_rows(c, rows), cols(i)].reshape(m, TILE)
-            acc_out[cols(i), :] += dg(x, ctx[:, chunk_rows(c, rows), :].reshape(m, -1), 0, 0)
-        tiles(width // TILE, tile)
+            x = gat[:, chunk_rows(c, rows), cols(i, 512)].reshape(m, 512)
+            acc_out[cols(i, 512), :] += dg(x, ctx[:, chunk_rows(c, rows), :].reshape(m, -1), 0, 0)
+        tiles(width // 512, tile)
         y = dg(wide(c), w_out[...], 1, 0)
         dctx[:, chunk_rows(c, rows), :] = y.astype(BF).reshape(n, rows, y.shape[1])
 

time: 539 us -> 525 us (0.974)
  Pallas kernels: 492 us -> 474 us
  waiting for transfers between devices: 2.18 us -> 8.09 us
    pallas_call x1, Pallas kernels: 240 us -> 227 us  [feed_forward(): pl.pallas_call(functools.partial(ffn_kernel, n=n, chunks=chunks, rows=row...]
    pallas_call x1, Pallas kernels: 16.6 us -> 5.15 us  [attn_bwd(): pl.pallas_call(functools.partial(attn_bwd_kernel, nb=length // BLK, seqs=...]
    pallas_call x1, Pallas kernels: 98.9 us -> 108 us  [project_back(): pl.pallas_call(functools.partial(back_kernel, n=n, n_grp=n_grp, chunks=ch...]
    pallas_call x1, Pallas kernels: 9.39 us -> 2.94 us  [attn_fwd(): pl.pallas_call(functools.partial(attn_fwd_kernel, nb=length // BLK, seqs=...]
    reduce_scatter x1, waiting for transfers between devices: 2.16 us -> 8.07 us  [on_device(): lax.psum_scatter(gw_ffn, 'grp', scatter_dimension=0, tiled=True).astype(F32)]
where the time goes in v8:
time: 525 us
  Pallas kernels  474 us (90%)
  local copies, waits for them, and re-layouts  25.4 us (5%)
  between operations  14.2 us (3%)
  waiting for transfers between devices  8.09 us (2%)
    pallas_call x1, Pallas kernels, feed_forward(): pl.pallas_call(functools.partial(ffn_kernel, n=n, chunks=chunks, rows=row...  227 us
    pallas_call x1, Pallas kernels, project_back(): pl.pallas_call(functools.partial(back_kernel, n=n, n_grp=n_grp, chunks=ch...  108 us
    pallas_call x1, Pallas kernels, attn_out(): pl.pallas_call(functools.partial(out_kernel, n=n, n_grp=n_grp, chunks=chu...  84.6 us
    pallas_call x1, Pallas kernels, front(): pl.pallas_call(functools.partial(front_kernel, n=n, n_grp=n_grp, parts=pa...  46.4 us
    unnamed x56, local copies, waits for them, and re-layouts  20.8 us
  transfers between devices with their start and end apart: 1, of which 1 were waited for; matrix products, arithmetic and copies ran while one was open for 0% of the time, Pallas kernels for 22%

profile of v8, /device:TPU:0, one launch (start us, length us, event | category | flops | bytes accessed | tf_op | source)
XLA Modules:
  0.0 524.8 jit_solution(3375813776903899593)
XLA Ops:
  7.2 0.0 reduce-scatter.2.cloned.1.call-start
  7.2 0.7 pad_maximum_fusion.1.vec
  8.0 1.3 fusion
  9.3 1.0 copy-done.11
  10.3 0.7 copy-done.12
  11.0 46.4 %front.1 = (bf16[2048,768]{1,0:T(8,128)(2,1)}, bf16[2048,2048]{1,0:T(8,128)(2,1)}, bf16[2048,768]{1,0:T(8,128)(2,1)}, bf16[2048,256]{1,0:T(8,128)(2,1)S(1)}, bf1...) custom-call(bf16[2048,2048]{1,0:T(8,128)(2,1)} %x_hbm.1, f32[512,768]{1,0:T(8,128)} %w_qkv.1, ...), custom_call_target="tpu_custom_call" | custom-call | flops 6442450944 | bytes 16777216 | tf_op jit(solution)/shard_map/front/pallas_call | solution.py:619
  57.5 2.2 copy-done
  59.8 2.9 attn_fwd.1
  62.7 0.0 copy-start.2
  62.7 0.7 pad_maximum_fusion.2.vec
  63.5 84.6 %attn_out.1 = (f32[256,2048]{1,0:T(8,128)S(1)}, bf16[256,2048]{1,0:T(8,128)(2,1)S(1)}, bf16[2048,1024]{1,0:T(8,128)(2,1)S(1)}, bf16[2048,1024]{1,0:T(8,128)(2,1)}) custom-call(bf16[8,256,256]{2,1,0:T(8,128)(2,1)S(1)} %bitcast.28, bf16[2048,256]{1,0:T(8,128)(2,1)S(1)} %get-tuple-element.40.w_out.out_hbm, f32[3,2048]{1,0:T(4,128)S(1)} %pad_maximum_fusion.vec, ...), custom_call_target="tpu_custom_call" | custom-call | flops 2147483648 | bytes 8388608 | tf_op jit(solution)/shard_map/attn_out/pallas_call | solution.py:521
  148.1 2.0 copy-done.8
  150.1 1.3 copy-done.9
  151.4 1.0 copy-done.10
  152.4 226.7 %feed_forward.1 = (bf16[2048,2048]{1,0:T(8,128)(2,1)}, bf16[2048,256]{1,0:T(8,128)(2,1)}, bf16[8,256,256]{2,1,0:T(8,128)(2,1)}, f32[256,2048]{1,0:T(8,128)}, bf1...) custom-call(bf16[256,2048]{1,0:T(8,128)(2,1)} %copy-done.10, bf16[8,256,2048]{2,1,0:T(8,128)(2,1)} %bitcast.51, ...), custom_call_target="tpu_custom_call" | custom-call | flops 51539607552 | bytes 67108864 | tf_op jit(solution)/shard_map/feed_forward/pallas_call | solution.py:1069
  379.1 0.0 reduce-scatter.2.cloned.1.call-update
  379.2 1.9 copy-done.1
  381.0 1.2 copy-done.3
  382.2 1.2 copy-done.14
  383.5 5.2 attn_bwd.1
  388.6 1.6 copy-done.13
  390.3 108.5 %project_back.1 = (f32[256,2048]{1,0:T(8,128)}, f32[512,768]{1,0:T(8,128)S(1)}, f32[512,256]{1,0:T(8,128)S(1)}, f32[8,2048]{1,0:T(8,128)S(1)}, f32[8,2048]{1,0:T(8,128)S(1)}) custom-call(bf16[8,256,768]{2,1,0:T(8,128)(2,1)} %bitcast.33, bf16[2048,768]{1,0:T(8,128)(2,1)} %get-tuple-element.50.w_attn, bf16[2048,2048]{1,0:T(8,128)(2,1)} %get-tuple-element.51.n1_hbm, ...), custom_call_target="tpu_custom_call" | custom-call | flops 12884901888 | bytes 16777216 | tf_op jit(solution)/shard_map/project_back/pallas_call | solution.py:837
  498.8 0.6 copy.33
  499.4 0.6 copy.30
  500.0 0.6 fusion.2
  500.7 8.1 %reduce-scatter.2.cloned.1.call-done = bf16[512,2048]{1,0:T(8,128)(2,1)} async-done(((bf16[2048,2048]{1,0:T(8,128)(2,1)}), bf16[512,2048]{1,0:T(8,128)(2,1)}) %reduce-scatter.2.cloned.1.call-update) | async-done | bytes 2097168 | tf_op jit(solution)/shard_map/reduce_scatter | solution.py:1107
  508.7 4.0 fusion.1
  512.8 1.0 copy.38
  513.7 1.0 copy-done.18
  514.7 1.3 copy.39
  516.0 1.1 copy.40
  517.2 0.8 copy.41
  (39 shorter events, 0.1 us)
Async XLA Ops:
  7.2 501.6 %reduce-scatter.2.cloned.1.call-start = ((), (), s32[]{:S(2)}) async-start(), calls=%async_computation.1 | async-start | bytes 10485760 | tf_op jit(solution)/shard_map/reduce_scatter | solution.py:1107
  9.3 1.0 copy-start.11
  10.3 0.7 copy-start.12
  11.0 46.4 %copy-start.6 = (s32[6]{0:T(128)S(1)}, s32[6]{0:T(128)}, u32[]{:S(2)}) copy-start(s32[6]{0:T(128)} %grps.3) | copy-start | bytes 76
  11.0 46.4 %copy-start.7 = (s32[6]{0:T(128)S(1)}, s32[6]{0:T(128)}, u32[]{:S(2)}) copy-start(s32[6]{0:T(128)} %lens.3) | copy-start | bytes 76
  57.5 6.0 %copy-start.4 = (bf16[2048,256]{1,0:T(8,128)(2,1)}, bf16[2048,256]{1,0:T(8,128)(2,1)S(1)}, u32[]{:S(2)}) copy-start(bf16[2048,256]{1,0:T(8,128)(2,1)S(1)} %get-tuple-element.40.w_out.out_hbm) | copy-start | bytes 3145732
  57.5 2.3 copy-start
  59.7 3.0 copy-start.20
  59.7 3.0 copy-start.23
  59.7 3.7 copy-start.21
  59.8 3.7 copy-start.22
  62.7 85.4 %copy-start.2 = (bf16[2048,256]{1,0:T(8,128)(2,1)}, bf16[2048,256]{1,0:T(8,128)(2,1)S(1)}, u32[]{:S(2)}) copy-start(bf16[2048,256]{1,0:T(8,128)(2,1)S(1)} %get-tuple-element.39.o_ref) | copy-start | bytes 3145732
  148.1 2.0 copy-start.8
  150.1 1.3 copy-start.9
  151.4 1.0 copy-start.10
  379.1 1.9 copy-start.1
  381.0 1.2 copy-start.3
  382.2 1.2 copy-start.14
  383.5 6.8 %copy-start.5 = (f32[2048]{0:T(1024)S(1)}, f32[2048]{0:T(1024)}, u32[]{:S(2)}) copy-start(f32[2048]{0:T(1024)} %param.28) | copy-start | bytes 24580
  383.5 6.8 %copy-start.15 = (bf16[2048,256]{1,0:T(8,128)(2,1)S(1)}, bf16[2048,256]{1,0:T(8,128)(2,1)}, u32[]{:S(2)}) copy-start(bf16[2048,256]{1,0:T(8,128)(2,1)} %get-tuple-element.52.gw_proj) | copy-start | bytes 3145732
  383.5 6.8 %copy-start.16 = (f32[8,2048]{1,0:T(8,128)S(1)}, f32[8,2048]{1,0:T(8,128)}, u32[]{:S(2)}) copy-start(f32[8,2048]{1,0:T(8,128)} %get-tuple-element.54.stats) | copy-start | bytes 196612
  383.5 6.8 %copy-start.17 = (f32[1,1024]{1,0:T(1,128)S(1)}, f32[1,1024]{1,0:T(1,128)}, u32[]{:S(2)}) copy-start(f32[1,1024]{1,0:T(1,128)} %get-tuple-element.55.up_sum) | copy-start | bytes 12292
  388.6 1.6 copy-start.13
  500.7 12.1 %copy-start.19 = (bf16[256,2048]{1,0:T(8,128)(2,1)S(1)}, bf16[256,2048]{1,0:T(8,128)(2,1)}, u32[]{:S(2)}) copy-start(bf16[256,2048]{1,0:T(8,128)(2,1)} %get-tuple-element.84) | copy-start | bytes 3145732
  512.8 2.0 copy-start.18
Sparse Core Ops, SparseCore 0:
  379.3 129.4 reduce-scatter.1

commit v9 on v8

--- a/solution.py
+++ b/solution.py
@@ -80,7 +80,7 @@
             out_specs=[pl.BlockSpec((length, HD), lambda h, grps, lens: (0, h)),
                        pl.BlockSpec((1, 1, length), lambda h, grps, lens: (h, 0, 0))]),
         out_shape=[jax.ShapeDtypeStruct((length, heads * HD), BF), jax.ShapeDtypeStruct((heads, 1, length), F32)],
-        compiler_params=pltpu.CompilerParams(vmem_limit_bytes=40 << 20),
+        compiler_params=pltpu.CompilerParams(vmem_limit_bytes=62 << 20),
         cost_estimate=pl.CostEstimate(flops=heads * length * length * HD * 2, bytes_accessed=length * heads * HD * 8,
                                       transcendentals=heads * length * length // 2),
         name="attn_fwd",
@@ -148,7 +148,7 @@
             out_specs=pl.BlockSpec((length, 3 * HD), lambda h, grps, lens: (0, h)),
             scratch_shapes=[pltpu.VMEM((HD, length), F32), pltpu.VMEM((1, length), F32)]),
         out_shape=jax.ShapeDtypeStruct((length, heads * 3 * HD), BF),
-        compiler_params=pltpu.CompilerParams(vmem_limit_bytes=40 << 20),
+        compiler_params=pltpu.CompilerParams(vmem_limit_bytes=62 << 20),
         cost_estimate=pl.CostEstimate(flops=heads * length * length * HD * 5, bytes_accessed=length * heads * HD * 16,
                                       transcendentals=heads * length * length // 2),
         name="attn_bwd",
@@ -472,15 +472,20 @@
     lax.fori_loop(0, chunks + 2, tick, 0)
 
 
-def out_kernel(ctx, w_out, vec, x_hbm, up16, down16, hidden, n2, up_hbm, down_hbm,
-               x_share, total, lsem, *sc, n, n_grp, chunks, rows):
+def out_kernel(ctx, w_out, b_out, gain, shift, x_hbm, up16, down16, hidden, n2, up_hbm, down_hbm,
+               x_share, total, up_own, down_own, lsem, *sc, n, n_grp, chunks, rows):
     at = Place(n)
+    fetches = [pltpu.make_async_copy(up16, up_own, lsem.at[3]), pltpu.make_async_copy(down16, down_own, lsem.at[4])]
+    for copy in fetches:
+        copy.start()
     load = pltpu.make_async_copy(x_hbm.at[at.t], x_share, lsem.at[0])
     load.start()
     up, down = GroupGather(at, n_grp, up_hbm, *sc[:2]), GroupGather(at, n_grp, down_hbm, *sc[2:4])
     own = chunk_rows(at.g, up.size)
-    put_up = pltpu.make_async_copy(up16, up_hbm.at[own, :], lsem.at[1])
-    put_down = pltpu.make_async_copy(down16, down_hbm.at[own, :], lsem.at[2])
+    put_up = pltpu.make_async_copy(up_own, up_hbm.at[own, :], lsem.at[1])
+    put_down = pltpu.make_async_copy(down_own, down_hbm.at[own, :], lsem.at[2])
+    for copy in fetches:
+        copy.wait()
     put_up.start()
     put_down.start()
     at.barrier(n_grp)
@@ -492,9 +497,9 @@
 
     def epilogue(c):
         r = chunk_rows(c, rows)
-        h = x_share[r, :].astype(F32) + total[...] + vec[0:1, :]
+        h = x_share[r, :].astype(F32) + total[...] + b_out[...]
         hidden[r, :] = h
-        n2[r, :] = (rows_stats(h)[0] * vec[1:2, :] + vec[2:3, :]).astype(BF)
+        n2[r, :] = (rows_stats(h)[0] * gain[...] + shift[...]).astype(BF)
 
     def extra(i):
         @pl.when(i == chunks // 2)
@@ -510,7 +515,7 @@
     down.finish()
 
 
-def attn_out(ctx, w_out, vec, x, up16, down16, n, n_grp, chunks):
+def attn_out(ctx, w_out, b_out, gain, shift, x, up16, down16, n, n_grp, chunks):
     length, hw = ctx.shape
     width = x.shape[1]
     share = length // n
@@ -520,17 +525,18 @@
     S = jax.ShapeDtypeStruct
     return pl.pallas_call(
         functools.partial(out_kernel, n=n, n_grp=n_grp, chunks=chunks, rows=rows),
-        in_specs=[vm] * 3 + [hbm] * 3, out_specs=[vm] * 2 + [hbm] * 2,
+        in_specs=[vm] * 5 + [hbm] * 3, out_specs=[vm] * 2 + [hbm] * 2,
         out_shape=[S((share, width), F32), S((share, width), BF), S((width, hid), BF), S((width, hid), BF)],
-        scratch_shapes=[pltpu.VMEM((share, width), BF), pltpu.VMEM((rows, width), F32), pltpu.SemaphoreType.DMA((3,))]
+        scratch_shapes=[pltpu.VMEM((share, width), BF), pltpu.VMEM((rows, width), F32), pltpu.VMEM(up16.shape, BF),
+                        pltpu.VMEM(up16.shape, BF), pltpu.SemaphoreType.DMA((5,))]
                        + group_sems(n_grp) * 2 + scatter_scratch(chunks, n // 2, rows, width),
-        compiler_params=pltpu.CompilerParams(collective_id=2, has_side_effects=True, vmem_limit_bytes=40 << 20),
+        compiler_params=pltpu.CompilerParams(collective_id=2, has_side_effects=True, vmem_limit_bytes=62 << 20),
         cost_estimate=pl.CostEstimate(flops=2 * length * hw * width, bytes_accessed=1 << 23, transcendentals=0),
         name="attn_out",
-    )(ctx.reshape(n, share, hw), w_out, vec, x.reshape(n, share, width), up16, down16)
-
-
-def front_kernel(x_hbm, w_qkv, w_out, w_up, w_down, vec, bias_hbm, proj, n1_hbm, w_attn, w_proj, up16, down16,
+    )(ctx.reshape(n, share, hw), w_out, b_out[None], gain[None], shift[None], x.reshape(n, share, width), up16, down16)
+
+
+def front_kernel(x_hbm, w_qkv, w_out, w_up, w_down, gain, shift, bias_hbm, proj, n1_hbm, w_attn, w_proj, up16, down16,
                  xbuf, n1, acc, bias, xsem, osem, bsem, *sc, n, n_grp, parts):
     at = Place(n)
     width, hw = w_attn.shape
@@ -557,6 +563,7 @@
     qkv, out = GroupGather(at, n_grp, w_attn, *sc[:2]), GroupGather(at, n_grp, w_proj, *sc[2:])
     qkv.start()
     w_proj[own, :] = w_out[...].astype(BF)
+    out.start()
     up16[...] = w_up[...].astype(BF)
     down16[...] = w_down[...].astype(BF)
 
@@ -566,7 +573,7 @@
         @pl.when(i + 1 < parts)
         def _():
             fetch(i + 1).start()
-        y = rows_stats(xbuf[lax.rem(i, 2)].astype(F32))[0] * vec[0:1, :] + vec[1:2, :]
+        y = rows_stats(xbuf[lax.rem(i, 2)].astype(F32))[0] * gain[...] + shift[...]
         n1[chunk_rows(i, rows), :] = y.astype(BF)
         put(i).start()
     tiles(parts, norm)
@@ -585,7 +592,6 @@
     p, q, P = at.g // 2, lax.rem(at.g, 2), n_grp // 2
     partial(at.g, True)
     qkv.forward()
-    out.start()
     partial(2 * p + 1 - q)
     for j in range(1, P):
         partial(2 * lax.rem(p + j, P) + q)
@@ -609,7 +615,7 @@
     out.finish()
 
 
-def front(x, w_qkv, w_out, w_up, w_down, vec, b_qv, n, n_grp):
+def front(x, w_qkv, w_out, w_up, w_down, gain, shift, b_qv, n, n_grp):
     length, width = x.shape
     block, hw = w_qkv.shape
     pw, hid = w_out.shape[1], w_up.shape[1]
@@ -618,16 +624,16 @@
     S, dma = jax.ShapeDtypeStruct, pltpu.SemaphoreType.DMA
     return pl.pallas_call(
         functools.partial(front_kernel, n=n, n_grp=n_grp, parts=parts),
-        in_specs=[hbm] + [vm] * 5 + [hbm], out_specs=[vm, hbm] + [vm] * 4,
+        in_specs=[hbm] + [vm] * 6 + [hbm], out_specs=[vm, hbm] + [vm] * 4,
         out_shape=[S((length, hw), BF), S((length, width), BF), S((width, hw), BF), S((width, pw), BF),
                    S((block, hid), BF), S((block, hid), BF)],
         scratch_shapes=[pltpu.VMEM((2, length // parts, width), BF), pltpu.VMEM((length, width), BF),
                         pltpu.VMEM((length, hw), F32), pltpu.VMEM((1, b_qv.shape[0] // n), F32),
                         dma((2,)), dma, dma] + group_sems(n_grp) * 2,
-        compiler_params=pltpu.CompilerParams(collective_id=5, has_side_effects=True, vmem_limit_bytes=50 << 20),
+        compiler_params=pltpu.CompilerParams(collective_id=5, has_side_effects=True, vmem_limit_bytes=62 << 20),
         cost_estimate=pl.CostEstimate(flops=2 * length * hw * width, bytes_accessed=1 << 24, transcendentals=0),
         name="front",
-    )(x, w_qkv, w_out, w_up, w_down, vec, b_qv.reshape(n, 1, -1))
+    )(x, w_qkv, w_out, w_up, w_down, gain[None], shift[None], b_qv.reshape(n, 1, -1))
 
 
 class AllSum:
@@ -677,8 +683,8 @@
             dma((n_grp - 1,)), dma((n_grp - 1,)), dma((n - 1,)), dma((n - 1,))]
 
 
-def back_kernel(dproj, w_attn, n1_hbm, gw_proj, x_hbm, dh, gain, stats, up_sum,
-                grad_x, g_attn, g_proj, sums, owned,
+def back_kernel(dproj, w_attn, n1_hbm, gw_proj, x_hbm, gain, stats, up_sum,
+                grad_x, g_attn, g_proj, a_rest, p_rest, sums, owned,
                 n1, x_share, gw, got, got_proj, total, qv, ln_sum, nsem, ws, wr, ps, pr, *scratch, n, n_grp, chunks, rows):
     at = Place(n)
     width, hw = w_attn.shape
@@ -751,7 +757,7 @@
         dn = total[...]
         e = dn * gain[...]
         inner = jnp.mean(e, -1, keepdims=True) + xhat * jnp.mean(e * xhat, -1, keepdims=True)
-        grad_x[r, :] = dh[r, :] + inverse * (e - inner)
+        grad_x[r, :] = inverse * (e - inner)
         ln_sum[0:1, :] += jnp.sum(dn * xhat, 0, keepdims=True)
         ln_sum[1:2, :] += jnp.sum(dn, 0, keepdims=True)
 
@@ -811,8 +817,8 @@
     for k in range(n_grp - 1):
         send(k).wait()
         send_proj(k).wait()
-        g_attn[...] += got[k].astype(F32)
-        g_proj[...] += got_proj[k].astype(F32)
+    a_rest[...] = sum(got[k].astype(F32) for k in range(n_grp - 1))
+    p_rest[...] = sum(got_proj[k].astype(F32) for k in range(n_grp - 1))
     late.turn()
     early.finish()
     sums[0:4, :] = early.total(0, 4)
@@ -825,7 +831,7 @@
     sums[6:8, :] = jnp.zeros_like(sums[6:8, :])
 
 
-def project_back(dproj, w_attn, n1, gw_proj, x, dh, gain, stats, up_sum, n, n_grp, chunks):
+def project_back(dproj, w_attn, n1, gw_proj, x, gain, stats, up_sum, n, n_grp, chunks):
     length, hw = dproj.shape
     width = w_attn.shape[0]
     share = length // n
@@ -836,8 +842,9 @@
     S, dma = jax.ShapeDtypeStruct, pltpu.SemaphoreType.DMA
     return pl.pallas_call(
         functools.partial(back_kernel, n=n, n_grp=n_grp, chunks=chunks, rows=rows),
-        in_specs=[vm, vm, hbm, vm, hbm] + [vm] * 4, out_specs=[vm] * 5,
-        out_shape=[S((share, width), F32), S((block, hw), F32), S((block, pw), F32), S((8, width), F32),
+        in_specs=[vm, vm, hbm, vm, hbm] + [vm] * 3, out_specs=[vm] * 7,
+        out_shape=[S((share, width), F32), S((block, hw), F32), S((block, pw), F32), S((block, hw), F32),
+                   S((block, pw), F32), S((8, width), F32),
                    S((n, width), F32)],
         scratch_shapes=[pltpu.VMEM((length, width), BF), pltpu.VMEM((share, width), BF), pltpu.VMEM((width, hw), BF),
                         pltpu.VMEM((n_grp - 1, block, hw), BF), pltpu.VMEM((n_grp - 1, block, pw), BF),
@@ -847,10 +854,10 @@
         compiler_params=pltpu.CompilerParams(collective_id=4, has_side_effects=True, vmem_limit_bytes=50 << 20),
         cost_estimate=pl.CostEstimate(flops=4 * length * hw * width, bytes_accessed=1 << 24, transcendentals=0),
         name="project_back",
-    )(dproj.reshape(n, share, hw), w_attn, n1, gw_proj, x.reshape(n, share, width), dh, gain, stats, up_sum)
-
-
-def ffn_kernel(n2_hbm, gradb_hbm, bias_hbm, up_hbm, down_hbm, out_hbm, ctx_hbm, hidden_hbm, vec, tokens,
+    )(dproj.reshape(n, share, hw), w_attn, n1, gw_proj, x.reshape(n, share, width), gain, stats, up_sum)
+
+
+def ffn_kernel(n2_hbm, gradb_hbm, bias_hbm, up_hbm, down_hbm, out_hbm, ctx_hbm, hidden_hbm, gain, b_down, groups, lens,
                gw_hbm, gwo, dctx, dh, res, stats, bsum,
                w_up, w_down, w_out, ctx, hidden, wsem, acc_out, gat, acc_up, acc_down, gbuf, actb, dbb, total, gshare, b_up, keep, lsem, gsem, msem, *scratch, n, chunks, rows):
     at = Place(n)
@@ -870,12 +877,13 @@
     load_b = pltpu.make_async_copy(bias_hbm.at[at.t], b_up, msem.at[1])
     load_b.start()
     share = hidden.shape[0]
+    tokens = jnp.sum(jnp.where(groups[...] == at.g, lens[...], 0), 1, keepdims=True)
 
     def alive(ranks, first, c):
         shape = (ranks, rows, 1)
         place = ((first + lax.broadcasted_iota(jnp.int32, shape, 0)) * share + c * rows
                  + lax.broadcasted_iota(jnp.int32, shape, 1))
-        return jnp.where(place < tokens[...].reshape(1, 1, 1), 1.0, 0.0).reshape(ranks * rows, 1)
+        return jnp.where(place < tokens.reshape(1, 1, 1), 1.0, 0.0).reshape(ranks * rows, 1)
 
     def fetch(c):
         slot = lax.rem(c, 2)
@@ -946,7 +954,7 @@
         r = chunk_rows(c, rows)
         xhat, inverse = rows_stats(hidden[r, :])
         dn2 = total[...]
-        e = dn2 * vec[0:1, :]
+        e = dn2 * gain[...]
         inner = jnp.mean(e, -1, keepdims=True) + xhat * jnp.mean(e * xhat, -1, keepdims=True)
         grad = gshare[r, :].astype(F32) * alive(1, at.t, c)
         d = grad + inverse * (e - inner)
@@ -1018,7 +1026,7 @@
                     def served(c):
                         mlp.finish(c, total)
                         r = chunk_rows(c, rows)
-                        res[r, :] = (alive(1, at.t, c) * (hidden[r, :] + total[...] + vec[1:2, :])).astype(BF)
+                        res[r, :] = (alive(1, at.t, c) * (hidden[r, :] + total[...] + b_down[...])).astype(BF)
                     at_stage(i - 4, served)
                     at_stage(i - 3, mlp.meet)
                 at_stage(i - 3, lambda c: mlp.hop(c, h - 1))
@@ -1057,7 +1065,7 @@
     gwo[...] = acc_out[...].astype(BF)
 
 
-def feed_forward(n2, gradb, b_up, w_up, w_down, w_out, ctx, hidden, vec, tokens, n, chunks):
+def feed_forward(n2, gradb, b_up, w_up, w_down, w_out, ctx, hidden, gain, b_down, groups, lens, n, chunks):
     length, width = gradb.shape
     hid, hw = w_up.shape[1], w_out.shape[1]
     share = length // n
@@ -1068,7 +1076,7 @@
     m = n * rows
     return pl.pallas_call(
         functools.partial(ffn_kernel, n=n, chunks=chunks, rows=rows),
-        in_specs=[hbm] * 8 + [vm] * 2,
+        in_specs=[hbm] * 8 + [vm] * 4,
         out_specs=[hbm] + [vm] * 6,
         out_shape=[S((width, 2 * hid), BF), S((width, hw), BF), S((n, share, hw), BF), S((share, width), F32),
                    S((share, width), BF), S((8, width), F32), S((1, hid), F32)],
@@ -1084,32 +1092,31 @@
         cost_estimate=pl.CostEstimate(flops=12 * length * hid * width, bytes_accessed=1 << 26, transcendentals=0),
         name="feed_forward",
     )(n2, gradb.reshape(n, share, width), b_up.reshape(n, 1, hid), w_up, w_down, w_out, ctx.reshape(n, share, hw),
-      hidden, vec, tokens)
+      hidden, gain[None], b_down[None], groups[None], lens[None])
 
 
 def on_device(layer_input, out_cotangent, seq_group, seq_len, w_qkv, b_qv, w_out, b_out, w_up, b_up,
               w_down, b_down, first_norm_gain, first_norm_bias, second_norm_gain, second_norm_bias):
     n_tp, n_grp = lax.axis_size("tp"), lax.axis_size("grp")
-    grp = lax.axis_index("grp")
-    length, width = layer_input.shape
+    length = layer_input.shape[0]
     hid, qv = w_up.shape[1], b_qv.shape[0] // n_tp
 
     proj, n1, w_attn, w_proj, up16, down16 = front(
-        layer_input, w_qkv, w_out, w_up, w_down, jnp.stack([first_norm_gain, first_norm_bias]), b_qv, n_tp, n_grp)
+        layer_input, w_qkv, w_out, w_up, w_down, first_norm_gain, first_norm_bias, b_qv, n_tp, n_grp)
     context, lse = attn_fwd(seq_group, seq_len, proj)
     hidden, n2, w_expand, w_reduce = attn_out(
-        context, w_proj, jnp.stack([b_out, second_norm_gain, second_norm_bias]), layer_input, up16, down16,
+        context, w_proj, b_out, second_norm_gain, second_norm_bias, layer_input, up16, down16,
         n_tp, n_grp, 8)
-    tokens = jnp.sum(jnp.where(seq_group == grp, seq_len, 0)).reshape(1, 1)
     gw_ffn, gw_proj, dcontext, dh, result, stats, up_sum = feed_forward(
         n2, out_cotangent, b_up, w_expand, w_reduce, w_proj, context, hidden,
-        jnp.stack([second_norm_gain, b_down]), tokens, n_tp, 8)
+        second_norm_gain, b_down, seq_group, seq_len, n_tp, 8)
     grads_ffn = lax.psum_scatter(gw_ffn, "grp", scatter_dimension=0, tiled=True).astype(F32)
     grads_expand, grads_reduce = grads_ffn[:, :hid], grads_ffn[:, hid:]
 
     dproj = attn_bwd(seq_group, seq_len, proj, context, dcontext.reshape(length, -1), lse)
-    grad_x, grads_attn, grads_proj, sums, owned = project_back(
-        dproj, w_attn, n1, gw_proj, layer_input, dh, first_norm_gain[None], stats, up_sum, n_tp, n_grp, 8)
+    grad_x, grads_attn, grads_proj, attn_rest, proj_rest, sums, owned = project_back(
+        dproj, w_attn, n1, gw_proj, layer_input, first_norm_gain[None], stats, up_sum, n_tp, n_grp, 8)
+    grad_x, grads_attn, grads_proj = dh + grad_x, grads_attn + attn_rest, grads_proj + proj_rest
     return (result, grad_x, grads_attn, owned[:, hid:hid + qv].reshape(-1), grads_proj, sums[2],
             grads_expand, owned[:, :hid].reshape(-1), grads_reduce, sums[3], sums[4], sums[5],
             sums[0], sums[1])

time: 525 us -> 518 us (0.987)
  local copies, waits for them, and re-layouts: 25.4 us -> 7.62 us
  Pallas kernels: 474 us -> 486 us
    unnamed x56 -> x19, local copies, waits for them, and re-layouts: 20.8 us -> 2.97 us
    add x0 -> x3, other arithmetic: none -> 5.46 us  [the longest x1 3.25 us: on_device(): dh + grad_x]
  transfers between devices with their start and end apart: 1 -> 1, of which waited for: 1 -> 1; matrix products, arithmetic and copies ran while one was open for 0% -> 1% of each run, Pallas kernels for 22% -> 23%
where the time goes in v9:
time: 518 us; the launch traced here: 517 us
  Pallas kernels  486 us (94%)
  between operations  14.1 us (3%)
  local copies, waits for them, and re-layouts  7.62 us (1%)
  other arithmetic  5.46 us (1%)
    pallas_call x1, Pallas kernels, feed_forward(): pl.pallas_call(functools.partial(ffn_kernel, n=n, chunks=chunks, rows=row...  226 us
    pallas_call x1, Pallas kernels, project_back(): pl.pallas_call(functools.partial(back_kernel, n=n, n_grp=n_grp, chunks=ch...  110 us
    pallas_call x1, Pallas kernels, attn_out(): pl.pallas_call(functools.partial(out_kernel, n=n, n_grp=n_grp, chunks=chu...  87 us
    pallas_call x1, Pallas kernels, front(): pl.pallas_call(functools.partial(front_kernel, n=n, n_grp=n_grp, parts=pa...  46.5 us
  transfers between devices with their start and end apart: 1, of which 1 were waited for; matrix products, arithmetic and copies ran while one was open for 1% of the time, Pallas kernels for 23%

profile of v9, /device:TPU:0, one launch (start us, length us, event | category | flops | bytes accessed | tf_op | source)
XLA Modules:
  0.0 517.1 jit_solution(11309141941072998197)
XLA Ops:
  7.2 0.0 reduce-scatter.2.cloned.1.call-start
  7.2 46.5 %front.1 = (bf16[2048,768]{1,0:T(8,128)(2,1)}, bf16[2048,2048]{1,0:T(8,128)(2,1)}, bf16[2048,768]{1,0:T(8,128)(2,1)}, bf16[2048,256]{1,0:T(8,128)(2,1)}, bf16[51...) custom-call(bf16[2048,2048]{1,0:T(8,128)(2,1)} %x_hbm.1, f32[512,768]{1,0:T(8,128)} %w_qkv.1, f32[512,256]{1,0:T(8,128)} %w_out.1, ...), custom_call_target="tpu_custom_call" | custom-call | flops 6442450944 | bytes 16777216 | tf_op jit(solution)/shard_map/front/pallas_call | solution.py:625
  53.7 7.0 %attn_fwd.1 = (bf16[2048,256]{1,0:T(8,128)(2,1)}, f32[2,1,2048]{2,1,0:T(1,128)}) custom-call(s32[6]{0:T(128)} %grps.3, s32[6]{0:T(128)} %lens.3, bf16[2048,768]{1,0:T(8,128)(2,1)} %get-tuple-element.40.q_ref.k_ref.v_ref, bf16[2048,768]{1,0:T(8,128)(2,1)} %get-tuple-element.40.q_ref.k_ref.v_ref, bf16[2048,768]{1,0:T(8,128)(2,1)} %get-tuple-element.40.q_ref.k_ref.v_ref), custom_call_target="tpu_custom_call" | custom-call | flops 2147483648 | bytes 4194304 | tf_op jit(solution)/shard_map/attn_fwd/pallas_call | solution.py:76
  60.6 87.0 %attn_out.1 = (f32[256,2048]{1,0:T(8,128)}, bf16[256,2048]{1,0:T(8,128)(2,1)}, bf16[2048,1024]{1,0:T(8,128)(2,1)}, bf16[2048,1024]{1,0:T(8,128)(2,1)}) custom-call(bf16[8,256,256]{2,1,0:T(8,128)(2,1)} %bitcast.33, bf16[2048,256]{1,0:T(8,128)(2,1)} %get-tuple-element.42.w_out.out_hbm, f32[1,2048]{1,0:T(1,128)} %bitcast.43, f32[1,2048]{1,0:T(1,128)} %bitcast.45, ...), custom_call_target="tpu_custom_call" | custom-call | flops 2147483648 | bytes 8388608 | tf_op jit(solution)/shard_map/attn_out/pallas_call | solution.py:526
  147.7 225.6 %feed_forward.1 = (bf16[2048,2048]{1,0:T(8,128)(2,1)}, bf16[2048,256]{1,0:T(8,128)(2,1)}, bf16[8,256,256]{2,1,0:T(8,128)(2,1)}, f32[256,2048]{1,0:T(8,128)}, bf1...) custom-call(bf16[256,2048]{1,0:T(8,128)(2,1)} %get-tuple-element.45.n2_hbm, ...), custom_call_target="tpu_custom_call" | custom-call | flops 51539607552 | bytes 67108864 | tf_op jit(solution)/shard_map/feed_forward/pallas_call | solution.py:1077
  373.3 0.0 reduce-scatter.2.cloned.1.call-update
  373.4 0.0 copy-start
  373.4 0.0 copy-start.1
  373.4 0.0 copy-start.2
  373.4 0.0 copy-start.3
  373.4 9.9 %attn_bwd.1 = bf16[2048,768]{1,0:T(8,128)(2,1)} custom-call(s32[6]{0:T(128)} %grps.3, s32[6]{0:T(128)} %lens.3, bf16[2048,768]{1,0:T(8,128)(2,1)} %get-tuple-element.40.q_ref.k_ref.v_ref, bf16[2048,768]{1,0:T(8,128)(2,1)} %get-tuple-element.40.q_ref.k_ref.v_ref, bf16[2048,768]{1,0:T(8,128)(2,1)} %get-tuple-element.40.q_ref.k_ref.v_ref, ...), custom_call_target="tpu_custom_call" | custom-call | flops 5368709120 | bytes 8388608 | tf_op jit(solution)/shard_map/attn_bwd/pallas_call | solution.py:142
  383.3 0.0 copy-done
  383.3 0.0 copy-done.1
  383.3 0.0 copy-done.2
  383.3 0.0 copy-done.3
  383.4 0.0 copy-start.4
  383.4 109.7 %project_back.1 = (f32[256,2048]{1,0:T(8,128)}, f32[512,768]{1,0:T(8,128)S(1)}, f32[512,256]{1,0:T(8,128)S(1)}, f32[512,768]{1,0:T(8,128)}, f32[512,256]{1,0:T(8...) custom-call(bf16[8,256,768]{2,1,0:T(8,128)(2,1)} %bitcast.54, bf16[2048,768]{1,0:T(8,128)(2,1)} %get-tuple-element.53.w_attn, ...), custom_call_target="tpu_custom_call" | custom-call | flops 12884901888 | bytes 16777216 | tf_op jit(solution)/shard_map/project_back/pallas_call | solution.py:843
  493.1 0.6 copy.33
  493.7 0.6 copy.30
  494.4 0.0 copy-done.4
  494.4 3.2 add.11
  497.6 0.0 copy-start.5
  497.6 0.9 add.13
  498.5 0.7 copy-done.5
  499.2 1.3 add.12
  500.6 0.6 fusion.1
  501.2 0.0 copy-start.6
  501.2 4.1 reduce-scatter.2.cloned.1.call-done
  505.3 4.0 fusion
  509.3 0.0 copy-done.6
  509.3 1.0 copy.35
  (2 shorter events, 0.0 us)
Async XLA Ops:
  7.2 498.1 %reduce-scatter.2.cloned.1.call-start = ((), (), s32[]{:S(2)}) async-start(), calls=%async_computation.1 | async-start | bytes 10485760 | tf_op jit(solution)/shard_map/reduce_scatter | solution.py:1113
  373.4 10.0 %copy-start = (f32[2048]{0:T(1024)S(1)}, f32[2048]{0:T(1024)}, u32[]{:S(2)}) copy-start(f32[2048]{0:T(1024)} %param.28) | copy-start | bytes 24580
  373.4 10.0 %copy-start.1 = (bf16[2048,256]{1,0:T(8,128)(2,1)S(1)}, bf16[2048,256]{1,0:T(8,128)(2,1)}, u32[]{:S(2)}) copy-start(bf16[2048,256]{1,0:T(8,128)(2,1)} %get-tuple-element.55.gw_proj) | copy-start | bytes 3145732
  373.4 10.0 %copy-start.2 = (f32[8,2048]{1,0:T(8,128)S(1)}, f32[8,2048]{1,0:T(8,128)}, u32[]{:S(2)}) copy-start(f32[8,2048]{1,0:T(8,128)} %get-tuple-element.56.stats) | copy-start | bytes 196612
  373.4 10.0 %copy-start.3 = (f32[1,1024]{1,0:T(1,128)S(1)}, f32[1,1024]{1,0:T(1,128)}, u32[]{:S(2)}) copy-start(f32[1,1024]{1,0:T(1,128)} %get-tuple-element.57.up_sum) | copy-start | bytes 12292
  383.4 111.0 %copy-start.4 = (f32[256,2048]{1,0:T(8,128)S(1)}, f32[256,2048]{1,0:T(8,128)}, u32[]{:S(2)}) copy-start(f32[256,2048]{1,0:T(8,128)} %get-tuple-element.50) | copy-start | bytes 6291460
  497.6 1.6 copy-start.5
  501.2 8.1 %copy-start.6 = (bf16[256,2048]{1,0:T(8,128)(2,1)S(1)}, bf16[256,2048]{1,0:T(8,128)(2,1)}, u32[]{:S(2)}) copy-start(bf16[256,2048]{1,0:T(8,128)(2,1)} %get-tuple-element.88) | copy-start | bytes 3145732
Sparse Core Ops, SparseCore 0:
  373.5 131.7 reduce-scatter.1

commit v10 on v9

--- a/solution.py
+++ b/solution.py
@@ -777,9 +777,9 @@
         def _():
             rs.hop(c, 2)
 
-        @pl.when(i < width // TILE)
-        def _():
-            weights(i)
+        @pl.when((i >= 2) & (i < width // TILE + 2))
+        def _():
+            weights(i - 2)
 
         @pl.when(inside(c, chunks))
         def _():

time: 518 us -> 517 us (level)
    pallas_call x1, Pallas kernels: 9.93 us -> 18.5 us  [attn_bwd(): pl.pallas_call(functools.partial(attn_bwd_kernel, nb=length // BLK, seqs=...]
    pallas_call x1, Pallas kernels: 110 us -> 104 us  [project_back(): pl.pallas_call(functools.partial(back_kernel, n=n, n_grp=n_grp, chunks=ch...]
  transfers between devices with their start and end apart: 1 -> 1, of which waited for: 1 -> 0; matrix products, arithmetic and copies ran while one was open for 1% -> 1% of each run, Pallas kernels for 23% -> 24%
where the time goes in v10:
time: 517 us; the launch traced here: 516 us
  Pallas kernels  489 us (95%)
  between operations  14.2 us (3%)
  local copies, waits for them, and re-layouts  7.71 us (1%)
  other arithmetic  5.52 us (1%)
    pallas_call x1, Pallas kernels, feed_forward(): pl.pallas_call(functools.partial(ffn_kernel, n=n, chunks=chunks, rows=row...  225 us
    pallas_call x1, Pallas kernels, project_back(): pl.pallas_call(functools.partial(back_kernel, n=n, n_grp=n_grp, chunks=ch...  104 us
    pallas_call x1, Pallas kernels, attn_out(): pl.pallas_call(functools.partial(out_kernel, n=n, n_grp=n_grp, chunks=chu...  83.8 us
    pallas_call x1, Pallas kernels, front(): pl.pallas_call(functools.partial(front_kernel, n=n, n_grp=n_grp, parts=pa...  46.5 us
    pallas_call x1, Pallas kernels, attn_bwd(): pl.pallas_call(functools.partial(attn_bwd_kernel, nb=length // BLK, seqs=...  18.5 us
    pallas_call x1, Pallas kernels, attn_fwd(): pl.pallas_call(functools.partial(attn_fwd_kernel, nb=length // BLK, seqs=...  10.9 us
  transfers between devices with their start and end apart: 1, of which 0 were waited for; matrix products, arithmetic and copies ran while one was open for 1% of the time, Pallas kernels for 24%

profile of v10, /device:TPU:0, one launch (start us, length us, event | category | flops | bytes accessed | tf_op | source)
XLA Modules:
  0.0 516.4 jit_solution(4439108668437948175)
XLA Ops:
  7.2 0.0 reduce-scatter.2.cloned.1.call-start
  7.2 46.5 %front.1 = (bf16[2048,768]{1,0:T(8,128)(2,1)}, bf16[2048,2048]{1,0:T(8,128)(2,1)}, bf16[2048,768]{1,0:T(8,128)(2,1)}, bf16[2048,256]{1,0:T(8,128)(2,1)}, bf16[51...) custom-call(bf16[2048,2048]{1,0:T(8,128)(2,1)} %x_hbm.1, f32[512,768]{1,0:T(8,128)} %w_qkv.1, f32[512,256]{1,0:T(8,128)} %w_out.1, ...), custom_call_target="tpu_custom_call" | custom-call | flops 6442450944 | bytes 16777216 | tf_op jit(solution)/shard_map/front/pallas_call | solution.py:625
  53.7 10.9 %attn_fwd.1 = (bf16[2048,256]{1,0:T(8,128)(2,1)}, f32[2,1,2048]{2,1,0:T(1,128)}) custom-call(s32[6]{0:T(128)} %grps.3, s32[6]{0:T(128)} %lens.3, bf16[2048,768]{1,0:T(8,128)(2,1)} %get-tuple-element.40.q_ref.k_ref.v_ref, bf16[2048,768]{1,0:T(8,128)(2,1)} %get-tuple-element.40.q_ref.k_ref.v_ref, bf16[2048,768]{1,0:T(8,128)(2,1)} %get-tuple-element.40.q_ref.k_ref.v_ref), custom_call_target="tpu_custom_call" | custom-call | flops 2147483648 | bytes 4194304 | tf_op jit(solution)/shard_map/attn_fwd/pallas_call | solution.py:76
  64.6 83.8 %attn_out.1 = (f32[256,2048]{1,0:T(8,128)}, bf16[256,2048]{1,0:T(8,128)(2,1)}, bf16[2048,1024]{1,0:T(8,128)(2,1)}, bf16[2048,1024]{1,0:T(8,128)(2,1)}) custom-call(bf16[8,256,256]{2,1,0:T(8,128)(2,1)} %bitcast.33, bf16[2048,256]{1,0:T(8,128)(2,1)} %get-tuple-element.42.w_out.out_hbm, f32[1,2048]{1,0:T(1,128)} %bitcast.43, f32[1,2048]{1,0:T(1,128)} %bitcast.45, ...), custom_call_target="tpu_custom_call" | custom-call | flops 2147483648 | bytes 8388608 | tf_op jit(solution)/shard_map/attn_out/pallas_call | solution.py:526
  148.4 225.1 %feed_forward.1 = (bf16[2048,2048]{1,0:T(8,128)(2,1)}, bf16[2048,256]{1,0:T(8,128)(2,1)}, bf16[8,256,256]{2,1,0:T(8,128)(2,1)}, f32[256,2048]{1,0:T(8,128)}, bf1...) custom-call(bf16[256,2048]{1,0:T(8,128)(2,1)} %get-tuple-element.45.n2_hbm, ...), custom_call_target="tpu_custom_call" | custom-call | flops 51539607552 | bytes 67108864 | tf_op jit(solution)/shard_map/feed_forward/pallas_call | solution.py:1077
  373.5 0.0 reduce-scatter.2.cloned.1.call-update
  373.5 0.0 copy-start
  373.5 0.0 copy-start.1
  373.6 0.0 copy-start.2
  373.6 0.0 copy-start.3
  373.6 18.5 %attn_bwd.1 = bf16[2048,768]{1,0:T(8,128)(2,1)} custom-call(s32[6]{0:T(128)} %grps.3, s32[6]{0:T(128)} %lens.3, bf16[2048,768]{1,0:T(8,128)(2,1)} %get-tuple-element.40.q_ref.k_ref.v_ref, bf16[2048,768]{1,0:T(8,128)(2,1)} %get-tuple-element.40.q_ref.k_ref.v_ref, bf16[2048,768]{1,0:T(8,128)(2,1)} %get-tuple-element.40.q_ref.k_ref.v_ref, ...), custom_call_target="tpu_custom_call" | custom-call | flops 5368709120 | bytes 8388608 | tf_op jit(solution)/shard_map/attn_bwd/pallas_call | solution.py:142
  392.1 0.0 copy-done
  392.1 0.0 copy-done.1
  392.1 0.0 copy-done.2
  392.1 0.0 copy-done.3
  392.1 0.0 copy-start.4
  392.1 104.2 %project_back.1 = (f32[256,2048]{1,0:T(8,128)}, f32[512,768]{1,0:T(8,128)S(1)}, f32[512,256]{1,0:T(8,128)S(1)}, f32[512,768]{1,0:T(8,128)}, f32[512,256]{1,0:T(8...) custom-call(bf16[8,256,768]{2,1,0:T(8,128)(2,1)} %bitcast.54, bf16[2048,768]{1,0:T(8,128)(2,1)} %get-tuple-element.53.w_attn, ...), custom_call_target="tpu_custom_call" | custom-call | flops 12884901888 | bytes 16777216 | tf_op jit(solution)/shard_map/project_back/pallas_call | solution.py:843
  496.4 0.6 copy.33
  497.0 0.6 copy.30
  497.6 0.0 copy-done.4
  497.6 3.3 add.11
  500.9 0.0 copy-start.5
  500.9 0.9 add.13
  501.8 0.7 copy-done.5
  502.5 1.3 add.12
  503.9 0.6 fusion.1
  504.5 0.0 copy-start.6
  504.5 0.0 reduce-scatter.2.cloned.1.call-done
  504.5 4.1 fusion
  508.6 0.0 copy-done.6
  508.6 1.0 copy.35
  (2 shorter events, 0.0 us)
Async XLA Ops:
  7.2 497.3 %reduce-scatter.2.cloned.1.call-start = ((), (), s32[]{:S(2)}) async-start(), calls=%async_computation.1 | async-start | bytes 10485760 | tf_op jit(solution)/shard_map/reduce_scatter | solution.py:1113
  373.5 18.6 %copy-start = (f32[2048]{0:T(1024)S(1)}, f32[2048]{0:T(1024)}, u32[]{:S(2)}) copy-start(f32[2048]{0:T(1024)} %param.28) | copy-start | bytes 24580
  373.5 18.6 %copy-start.1 = (bf16[2048,256]{1,0:T(8,128)(2,1)S(1)}, bf16[2048,256]{1,0:T(8,128)(2,1)}, u32[]{:S(2)}) copy-start(bf16[2048,256]{1,0:T(8,128)(2,1)} %get-tuple-element.55.gw_proj) | copy-start | bytes 3145732
  373.6 18.6 %copy-start.2 = (f32[8,2048]{1,0:T(8,128)S(1)}, f32[8,2048]{1,0:T(8,128)}, u32[]{:S(2)}) copy-start(f32[8,2048]{1,0:T(8,128)} %get-tuple-element.56.stats) | copy-start | bytes 196612
  373.6 18.6 %copy-start.3 = (f32[1,1024]{1,0:T(1,128)S(1)}, f32[1,1024]{1,0:T(1,128)}, u32[]{:S(2)}) copy-start(f32[1,1024]{1,0:T(1,128)} %get-tuple-element.57.up_sum) | copy-start | bytes 12292
  392.1 105.5 %copy-start.4 = (f32[256,2048]{1,0:T(8,128)S(1)}, f32[256,2048]{1,0:T(8,128)}, u32[]{:S(2)}) copy-start(f32[256,2048]{1,0:T(8,128)} %get-tuple-element.50) | copy-start | bytes 6291460
  500.9 1.6 copy-start.5
  504.5 4.1 copy-start.6
Sparse Core Ops, SparseCore 0:
  373.7 124.6 reduce-scatter.1
